TPU v7x, 256 devices: a whole 4x4x8 slice. The times are simulated.
256 devices in a mesh: dp: 8 (over y, core), tensor: 32 (over x, z).
Axes of the slice: x: 4, y: 4, z: 8, core: 2. Of those that a mesh axis runs over, the one named last changes fastest.
Arguments:
- hidden_sel: bfloat16 [8, 512, 2048], P('dp', 'tensor'), may hold values from -8 to 8
- picked: int32 [8, 512], P('dp'), may hold values from 0 to 12287, as said below
- order: int32 [8, 12], P('dp'), may hold values from 0 to 11, each once within a row
- lengths: int32 [8, 3], P('dp'), may hold values from 1 to 6, 12 in all within a row
- offsets: int32 [8, 3], P('dp'), may hold values from 0 to 4095
- cache_keys: bfloat16 [8, 12288, 2048], P('dp', 'tensor'), may hold values from -64 to 64
- cache_values: bfloat16 [8, 12288, 2048], P('dp', 'tensor'), may hold values from -6 to 6
- w_qkv: bfloat16 [3, 2048, 2048], P(None, 'dp', 'tensor'), may hold values from -0.088388348 to 0.088388348
- w_out: bfloat16 [2048, 2048], P('tensor', 'dp'), may hold values from -0.125 to 0.125
- w_gate_up: bfloat16 [2, 2048, 8192], P(None, 'dp', 'tensor'), may hold values from -0.125 to 0.125
- w_down: bfloat16 [8192, 2048], P('tensor', 'dp'), may hold values from -0.0625 to 0.0625
- gains: float32 [4, 2048], replicated, may hold values from 0.5 to 1.5
Outputs:
- layer_out: bfloat16 [8, 512, 2048], P('dp', 'tensor')
- fresh_keys: bfloat16 [8, 512, 2048], P('dp', 'tensor')
Inputs may be any that keep to these rules, and one draw needn't show every extreme that they name: `picked`: distinct context rows in increasing order; the first and last rows of the context are always among them. `lengths`: they sum to 12.
All inputs are finite; a program needn't handle non-finite values.
Results may differ from a plain program's by a relative error of at most 0.04.
Values may be sent and summed in bfloat16 or wider, within the bound.
A program may use at most 64 MiB of HBM per device.

v0:
```python
import math

import jax
import jax.numpy as jnp
from jax import lax
from jax.sharding import PartitionSpec as P

HEAD_DIM = 128
CH = 1024
NCH = 12
REQS = 3


THETA = 500000.0
EPSILON = 1e-06
NEGATIVE = -1e30


def token_meta(rows, order_row, length_row, offset_row):
    slot_index = rows // CH
    in_span = rows % CH
    ordinal = jnp.sum(
        jnp.where(
            slot_index[:, None] == jnp.arange(NCH, dtype=jnp.int32)[None, :], order_row[None, :], 0
        ),
        axis=1,
    )
    request_end = jnp.cumsum(length_row)
    request = jnp.sum((ordinal[:, None] >= request_end[None, :]).astype(jnp.int32), axis=1)
    request_pick = request[:, None] == jnp.arange(REQS, dtype=jnp.int32)[None, :]
    request_start = jnp.sum(jnp.where(request_pick, (request_end - length_row)[None, :], 0), axis=1)
    request_shift = jnp.sum(jnp.where(request_pick, offset_row[None, :], 0), axis=1)
    position = request_shift + (ordinal - request_start) * CH + in_span
    return (request, position, in_span)


def frequencies(index_float):
    return jnp.exp(index_float * (-2.0 * math.log(THETA) / HEAD_DIM))


def rope_full(values_in, position):
    row_count = values_in.shape[0]
    half_dim = HEAD_DIM // 2
    split = values_in.reshape(row_count, -1, HEAD_DIM)
    angles = (
        position.astype(jnp.float32)[:, None]
        * frequencies(jnp.arange(half_dim, dtype=jnp.int32).astype(jnp.float32))[None, :]
    )
    cosine = jnp.cos(angles)[:, None, :]
    sine = jnp.sin(angles)[:, None, :]
    first = split[..., :half_dim]
    second = split[..., half_dim:]
    turned = jnp.concatenate(
        [first * cosine - second * sine, second * cosine + first * sine], axis=-1
    )
    return turned.reshape(row_count, -1)


def rms_scale(values_in, gain):
    return (
        values_in
        * lax.rsqrt(jnp.mean(values_in * values_in, axis=-1, keepdims=True) + EPSILON)
        * gain
    )


def shards(
    hidden_sel,
    picked,
    order,
    lengths,
    offsets,
    cache_keys,
    cache_values,
    w_qkv,
    w_out,
    w_gate_up,
    w_down,
    gains,
):
    hidden = hidden_sel[0]
    picked_row = picked[0]
    order_row = order[0]
    length_row = lengths[0]
    offset_row = offsets[0]
    keys_local = cache_keys[0]
    values_local = cache_values[0]
    lane_count = lax.axis_size("tensor")
    lane_index = lax.axis_index("tensor")
    sel_dev = hidden.shape[0]
    sel_all = sel_dev * lane_count
    ctx_dev = keys_local.shape[0]
    model_width = hidden.shape[1]
    head_count = model_width // HEAD_DIM
    qkv_full, out_full = (
        lax.all_gather(w_qkv, "dp", axis=1, tiled=True),
        lax.all_gather(w_out, "dp", axis=1, tiled=True),
    )
    query_request, query_position, _ = token_meta(picked_row, order_row, length_row, offset_row)
    cache_rows = lane_index * ctx_dev + jnp.arange(ctx_dev, dtype=jnp.int32)
    cache_request, cache_position, cache_local = token_meta(
        cache_rows, order_row, length_row, offset_row
    )
    chosen = jnp.any(picked_row[:, None] == cache_rows[None, :], axis=0)
    fresh_request = lax.dynamic_slice_in_dim(query_request, lane_index * sel_dev, sel_dev)
    fresh_position = lax.dynamic_slice_in_dim(query_position, lane_index * sel_dev, sel_dev)
    projected = jnp.einsum(
        "nd,kdc->knc",
        lax.all_gather(hidden, "tensor", axis=0, tiled=True),
        qkv_full,
        preferred_element_type=jnp.float32,
    )
    own_rows = lax.all_to_all(
        projected.astype(jnp.bfloat16), "tensor", split_axis=1, concat_axis=2, tiled=True
    ).astype(projected.dtype)
    query_tok = rope_full(rms_scale(own_rows[0], gains[0]), fresh_position).astype(jnp.bfloat16)
    key_fresh = rope_full(rms_scale(own_rows[1], gains[1]), fresh_position).astype(jnp.bfloat16)
    value_fresh = own_rows[2].astype(jnp.bfloat16)
    queries = lax.all_gather(query_tok, "tensor", axis=0, tiled=True)
    turned_keys = rope_full(keys_local.astype(jnp.float32), cache_position - cache_local).astype(
        jnp.bfloat16
    )
    all_keys = jnp.concatenate([turned_keys, key_fresh], axis=0).reshape(-1, head_count, HEAD_DIM)
    all_values = jnp.concatenate([values_local, value_fresh], axis=0).reshape(
        -1, head_count, HEAD_DIM
    )
    key_request = jnp.concatenate([cache_request, fresh_request])
    key_position = jnp.concatenate([cache_position, fresh_position])
    key_live = jnp.concatenate([jnp.logical_not(chosen), jnp.ones((sel_dev,), bool)])
    block_rows = min(512, sel_all)
    block_count = sel_all // block_rows

    def attend(operands):
        query_block, block_request, block_position = operands
        scores = jnp.einsum(
            "qhd,khd->hqk",
            query_block.reshape(block_rows, head_count, HEAD_DIM),
            all_keys,
            preferred_element_type=jnp.float32,
        ) * HEAD_DIM ** (-0.5)
        usable = (
            (block_request[:, None] == key_request[None, :])
            & (key_position[None, :] <= block_position[:, None])
            & key_live[None, :]
        )
        masked = jnp.where(usable[None], scores, NEGATIVE)
        local_max = jnp.max(masked, axis=2)
        weights = jnp.where(usable[None], jnp.exp(masked - local_max[:, :, None]), 0.0)
        totals = jnp.sum(weights, axis=2)
        mixed = jnp.einsum(
            "hqk,khd->qhd",
            weights.astype(jnp.bfloat16),
            all_values,
            preferred_element_type=jnp.float32,
        )
        return (mixed.reshape(block_rows, model_width), local_max.T, totals.T)

    partial_out, local_max, totals = lax.map(
        attend,
        (
            queries.reshape(block_count, block_rows, model_width),
            query_request.reshape(block_count, block_rows),
            query_position.reshape(block_count, block_rows),
        ),
    )
    partial_out = partial_out.reshape(sel_all, model_width)
    local_max = local_max.reshape(sel_all, head_count)
    totals = totals.reshape(sel_all, head_count)
    row_max = lax.pmax(local_max.astype(jnp.bfloat16), "tensor").astype(local_max.dtype)
    factor = jnp.exp(local_max - row_max)
    scaled_out = (partial_out.reshape(sel_all, head_count, HEAD_DIM) * factor[:, :, None]).reshape(
        sel_all, model_width
    )
    scaled_total = totals * factor
    summed = lax.psum_scatter(
        scaled_out.astype(jnp.bfloat16), "tensor", scatter_dimension=0, tiled=True
    ).astype(jnp.float32)
    weight_sum = lax.psum_scatter(
        scaled_total.astype(jnp.bfloat16), "tensor", scatter_dimension=0, tiled=True
    ).astype(jnp.float32)
    attn_rows = (
        (summed.reshape(sel_dev, head_count, HEAD_DIM) / weight_sum[:, :, None])
        .reshape(sel_dev, model_width)
        .astype(jnp.bfloat16)
    )
    attn_cols = lax.all_to_all(attn_rows, "tensor", split_axis=1, concat_axis=0, tiled=True)
    attn_proj = lax.psum_scatter(
        jnp.dot(attn_cols, out_full, preferred_element_type=jnp.float32).astype(jnp.bfloat16),
        "tensor",
        scatter_dimension=0,
        tiled=True,
    ).astype(jnp.float32)
    hidden_next = (hidden.astype(jnp.float32) + rms_scale(attn_proj, gains[2])).astype(jnp.bfloat16)
    gate_full, down_full = (
        lax.all_gather(w_gate_up, "dp", axis=1, tiled=True),
        lax.all_gather(w_down, "dp", axis=1, tiled=True),
    )
    rows_piece = lax.all_gather(hidden_next, "tensor", axis=0, tiled=True)
    gate_part = jnp.dot(rows_piece, gate_full[0], preferred_element_type=jnp.float32)
    up_part = jnp.dot(rows_piece, gate_full[1], preferred_element_type=jnp.float32)
    activated = (jax.nn.silu(gate_part) * up_part).astype(jnp.bfloat16)
    mlp_out = lax.psum_scatter(
        jnp.dot(activated, down_full, preferred_element_type=jnp.float32).astype(jnp.bfloat16),
        "tensor",
        scatter_dimension=0,
        tiled=True,
    ).astype(jnp.float32)
    result = (hidden_next.astype(jnp.float32) + rms_scale(mlp_out, gains[3])).astype(jnp.bfloat16)
    return (result[None], key_fresh[None])


def solution(mesh):
    placed = (
        P("dp", "tensor", None),
        P("dp", None),
        P("dp", None),
        P("dp", None),
        P("dp", None),
        P("dp", "tensor", None),
        P("dp", "tensor", None),
        P(None, "dp", "tensor"),
        P("tensor", "dp"),
        P(None, "dp", "tensor"),
        P("tensor", "dp"),
        P(),
    )
    return jax.shard_map(
        shards,
        mesh=mesh,
        in_specs=placed,
        out_specs=(P("dp", "tensor", None), P("dp", "tensor", None)),
        check_vma=False,
    )
```

profile of v0, /device:TPU:6, one launch (start us, length us, event | category | flops | bytes accessed | tf_op | source)
XLA Modules:
  0.0 1328.8 jit_solution(13304637815611621171)
XLA Ops:
  14.0 14.1 %all_gather.21 = bf16[3,2048,64]{1,2,0:T(8,128)(2,1)S(1)} all-gather(bf16[3,256,64]{1,2,0:T(8,128)(2,1)} %param.19), channel_id=1, replica_groups=mesh['dp'=8,'tensor'=32] {'dp'}, dimensions={1}, use_global_device_ids=true | all-gather | bytes 884736 | tf_op jit(solution)/shard_map/all_gather | solution.py:96
  28.1 62.7 %all-gather.15.cloned.1.call-done = bf16[1,512,2048]{2,1,0:T(8,128)(2,1)} async-done(((bf16[1,16,2048]{2,1,0:T(8,128)(2,1)}), bf16[1,512,2048]{2,1,0:T(8,128)(2,1)}) %all-gather.15.cloned.1.call-update) | async-done | bytes 2097168 | tf_op jit(solution)/shard_map/all_gather | solution.py:109
  90.8 2.4 fusion.24
  94.6 7.5 all-to-all-start
  102.8 8.0 all-to-all-done
  116.9 2.1 fusion.64
  119.0 2.1 copy.92
  121.1 3.3 copy.93
  124.4 2.6 copy.69
  127.0 2.6 copy.73
  133.8 1.6 and_and_fusion
  136.9 4.4 subtract_convert_fusion
  142.7 45.0 %all-gather.7.cloned.1.call-done = bf16[512,2048]{1,0:T(8,128)(2,1)} async-done(((bf16[16,2048]{1,0:T(8,128)(2,1)}), bf16[512,2048]{1,0:T(8,128)(2,1)}) %all-gather.7.cloned.1.call-update) | async-done | bytes 2097168 | tf_op jit(solution)/shard_map/all_gather | solution.py:119
  187.8 2.9 copy.78
  190.7 5.5 fusion
  196.2 4.6 copy-done
  200.8 3.2 fusion.1
  204.0 128.2 %pmax.7 = bf16[512,16]{0,1:T(8,128)(2,1)S(1)} all-reduce(bf16[512,16]{0,1:T(8,128)(2,1)S(1)} %bitcast_convert_fusion), channel_id=1, replica_groups=mesh['dp'=8,'tensor'=32] {'tensor'}, use_global_device_ids=true, to_apply=%region_13.14 | all-reduce | flops 8192 | bytes 32768 | tf_op jit(solution)/shard_map/pmax | solution.py:169
  333.3 9.1 fusion.6
  342.4 2.5 copy.85
  344.9 187.0 %reduce-scatter.13.cloned.1.call-done = bf16[16,16]{1,0:T(8,128)(2,1)} async-done(((bf16[512,16]{1,0:T(8,128)(2,1)}), bf16[16,16]{1,0:T(8,128)(2,1)}) %reduce-scatter.13.cloned.1.call-update) | async-done | bytes 528
  532.7 217.9 %reduce-scatter.7.cloned.1.call-done = bf16[16,2048]{1,0:T(8,128)(2,1)} async-done(((bf16[512,2048]{1,0:T(8,128)(2,1)}), bf16[16,2048]{1,0:T(8,128)(2,1)}) %reduce-scatter.7.cloned.1.call-update) | async-done | bytes 65552 | tf_op jit(solution)/shard_map/reduce_scatter | solution.py:175
  752.6 8.0 all-to-all-start.1
  760.6 13.2 all_gather.24
  774.0 2.0 convolution_convert_fusion.1
  776.7 215.2 %reduce-scatter.9.cloned.1.call-done = bf16[16,2048]{1,0:T(8,128)(2,1)} async-done(((bf16[512,2048]{1,0:T(8,128)(2,1)}), bf16[16,2048]{1,0:T(8,128)(2,1)}) %reduce-scatter.9.cloned.1.call-update) | async-done | bytes 65552 | tf_op jit(solution)/shard_map/reduce_scatter | solution.py:187
  992.8 1.6 fusion.37
  995.1 75.2 %all-gather.9.cloned.1.call-done = bf16[512,2048]{1,0:T(8,128)(2,1)} async-done(((bf16[16,2048]{1,0:T(8,128)(2,1)}), bf16[512,2048]{1,0:T(8,128)(2,1)}) %all-gather.9.cloned.1.call-update) | async-done | bytes 2097168 | tf_op jit(solution)/shard_map/all_gather | solution.py:198
  1070.3 2.6 fusion.27
  1072.8 23.8 %all-gather.13.cloned.1.call-done = bf16[256,2048]{1,0:T(8,128)(2,1)} async-done(((bf16[256,256]{1,0:T(8,128)(2,1)}), bf16[256,2048]{1,0:T(8,128)(2,1)}) %all-gather.13.cloned.1.call-update) | async-done | bytes 1048592 | tf_op jit(solution)/shard_map/all_gather | solution.py:196
  1096.7 5.5 convolution_convert_fusion
  1102.9 216.1 %reduce-scatter.11.cloned.1.call-done = bf16[16,2048]{1,0:T(8,128)(2,1)} async-done(((bf16[512,2048]{1,0:T(8,128)(2,1)}), bf16[16,2048]{1,0:T(8,128)(2,1)}) %reduce-scatter.11.cloned.1.call-update) | async-done | bytes 65552 | tf_op jit(solution)/shard_map/reduce_scatter | solution.py:202
  (117 shorter events, 30.5 us)
Async XLA Ops:
  8.0 82.8 %all-gather.15.cloned.1.call-start = ((), (), s32[]{:S(2)}) async-start(), calls=%async_computation.13 | async-start | bytes 2162688 | tf_op jit(solution)/shard_map/all_gather | solution.py:109
  9.6 4.3 copy-start.15
  9.6 84.0 %copy-start.13 = (f32[64]{0:T(128)}, f32[64]{0:T(128)S(1)}, u32[]{:S(2)}) copy-start(f32[64]{0:T(128)S(1)} %multiply_exponential_fusion) | copy-start | bytes 772
  11.1 103.1 %copy-start.11 = (s32[512]{0:T(512)}, s32[512]{0:T(512)S(1)}, u32[]{:S(2)}) copy-start(s32[512]{0:T(512)S(1)} %convert_reduce_fusion) | copy-start | bytes 6148
  11.8 0.7 copy-start.14
  13.2 0.8 copy-start.12
  28.1 74.1 %copy-start.7 = (f32[4,2048]{1,0:T(4,128)S(1)}, f32[4,2048]{1,0:T(4,128)}, u32[]{:S(2)}) copy-start(f32[4,2048]{1,0:T(4,128)} %param.23) | copy-start | bytes 98308
  94.6 16.2 %all-to-all-start = ((bf16[32,2,1536]{2,1,0:T(2,128)(2,1)}), bf16[32,2,1536]{2,1,0:T(2,128)(2,1)S(1)}, u32[]{:S(2)}, u32[]{:S(2)}) async-start(bf16[32,2,1536]{2,1,0:T(2,128)(2,1)} %reshape.396), calls=%async_computation | async-start | bytes 393216 | tf_op jit(solution)/shard_map/all_to_all | solution.py:113
  102.2 85.6 %all-gather.7.cloned.1.call-start = ((), (), s32[]{:S(2)}) async-start(), calls=%async_computation.6 | async-start | bytes 2162688 | tf_op jit(solution)/shard_map/all_gather | solution.py:119
  111.2 4.2 copy-start.10
  111.2 4.8 copy-start.1
  113.9 417.9 %reduce-scatter.13.cloned.1.call-start = ((), (), s32[]{:S(2)}) async-start(), calls=%async_computation.14 | async-start | bytes 135168
  136.9 4.5 copy-start.2
  142.7 47.9 %copy-start.3 = (pred[512,400]{0,1:T(8,128)(4,1)S(1)}, pred[512,400]{0,1:T(8,128)(4,1)}, u32[]{:S(2)}) copy-start(pred[512,400]{0,1:T(8,128)(4,1)} %and_and_fusion) | copy-start | bytes 614404
  196.1 4.7 copy-start
  333.0 417.5 %reduce-scatter.7.cloned.1.call-start = ((), (), s32[]{:S(2)}) async-start(), calls=%async_computation.7 | async-start | bytes 2162688 | tf_op jit(solution)/shard_map/reduce_scatter | solution.py:175
  344.8 415.8 %copy-start.6 = (bf16[64,256]{1,0:T(8,128)(2,1)S(1)}, bf16[64,256]{1,0:T(8,128)(2,1)}, u32[]{:S(2)}) copy-start(bf16[64,256]{1,0:T(8,128)(2,1)} %param.20) | copy-start | bytes 98308
  752.6 21.3 %all-to-all-start.1 = ((bf16[32,2,512]{2,1,0:T(2,128)(2,1)}), bf16[32,2,512]{2,1,0:T(2,128)(2,1)S(1)}, u32[]{:S(2)}, u32[]{:S(2)}) async-start(bf16[32,2,512]{2,1,0:T(2,128)(2,1)} %reshape.398), calls=%async_computation.2 | async-start | bytes 131072 | tf_op jit(solution)/shard_map/all_to_all | solution.py:186
  760.6 231.2 %reduce-scatter.9.cloned.1.call-start = ((), (), s32[]{:S(2)}) async-start(), calls=%async_computation.8 | async-start | bytes 2162688 | tf_op jit(solution)/shard_map/reduce_scatter | solution.py:187
  774.0 218.8 %copy-start.5 = (bf16[1,16,2048]{2,1,0:T(8,128)(2,1)S(1)}, bf16[1,16,2048]{2,1,0:T(8,128)(2,1)}, u32[]{:S(2)}) copy-start(bf16[1,16,2048]{2,1,0:T(8,128)(2,1)} %param.12) | copy-start | bytes 196612
  774.0 218.8 %copy-start.9 = (f32[1,2048]{1,0:T(1,128)S(1)}, f32[1,2048]{1,0:T(1,128)}, u32[]{:S(2)}) copy-start(f32[1,2048]{1,0:T(1,128)} %get-tuple-element.61) | copy-start | bytes 24580
  776.0 219.0 %all-gather.11.cloned.1.call-start = ((), (), s32[]{:S(2)}) async-start(), calls=%async_computation.10 | async-start | bytes 2359296 | tf_op jit(solution)/shard_map/all_gather | solution.py:195
  776.6 293.6 %all-gather.9.cloned.1.call-start = ((), (), s32[]{:S(2)}) async-start(), calls=%async_computation.9 | async-start | bytes 2162688 | tf_op jit(solution)/shard_map/all_gather | solution.py:198
  994.4 102.2 %all-gather.13.cloned.1.call-start = ((), (), s32[]{:S(2)}) async-start(), calls=%async_computation.11 | async-start | bytes 1179648 | tf_op jit(solution)/shard_map/all_gather | solution.py:196
  995.0 323.9 %reduce-scatter.11.cloned.1.call-start = ((), (), s32[]{:S(2)}) async-start(), calls=%async_computation.12 | async-start | bytes 2162688 | tf_op jit(solution)/shard_map/reduce_scatter | solution.py:202
  995.1 101.6 %copy-start.16 = (bf16[2,2048,256]{2,1,0:T(8,128)(2,1)S(1)}, bf16[2,2048,256]{2,1,0:T(8,128)(2,1)}, u32[]{:S(2)}) copy-start(bf16[2,2048,256]{2,1,0:T(8,128)(2,1)} %all-gather.11.cloned.1.call-done) | copy-start | bytes 6291460
  1102.2 217.8 %copy-start.4 = (bf16[16,2048]{1,0:T(8,128)(2,1)S(1)}, bf16[16,2048]{1,0:T(8,128)(2,1)}, u32[]{:S(2)}) copy-start(bf16[16,2048]{1,0:T(8,128)(2,1)} %fusion.37) | copy-start | bytes 196612
  1102.2 217.8 %copy-start.8 = (f32[1,2048]{1,0:T(1,128)S(1)}, f32[1,2048]{1,0:T(1,128)}, u32[]{:S(2)}) copy-start(f32[1,2048]{1,0:T(1,128)} %get-tuple-element.58) | copy-start | bytes 24580
Sparse Core Ops, SparseCore 0:
  11.4 79.3 all-gather.14
  114.0 73.6 all-gather.6
  333.1 198.6 reduce-scatter.12
  536.0 214.4 reduce-scatter.6
  776.2 215.6 reduce-scatter.8
Sparse Core Ops, SparseCore 1:
  778.3 28.2 all-gather.10
  994.5 75.7 all-gather.8
  1072.1 24.5 all-gather.12
  1102.3 216.6 reduce-scatter.10
where the time goes:
time: 1330 us
  waiting for transfers between devices  1050 us (79%)
  blocking collectives  156 us (12%)
  local copies, waits for them, and re-layouts  31.9 us (2%)
  other arithmetic  29.5 us (2%)
  matrix products  27.1 us (2%)
  starting transfers between devices  16.3 us (1%)
  between operations  15.9 us (1%)
    reduce_scatter x1, waiting for transfers between devices, shards(): lax.psum_scatter(scaled_out.astype(jnp.bfloat16), 'tensor', scatter_dimen...  218 us
    reduce_scatter x1, waiting for transfers between devices, shards(): lax.psum_scatter(jnp.dot(activated, down_full, preferred_element_type=jnp...  216 us
    reduce_scatter x1, waiting for transfers between devices, shards(): lax.psum_scatter(jnp.dot(attn_cols, out_full, preferred_element_type=jnp....  215 us
    unnamed x10, waiting for transfers between devices  189 us
    pmax x1, blocking collectives, shards(): lax.pmax(local_max.astype(jnp.bfloat16), 'tensor').astype(local_max.dtype)  128 us
    all_gather x1, waiting for transfers between devices, shards(): rows_piece = lax.all_gather(hidden_next, 'tensor', axis=0, tiled=True)  75.2 us
    all_gather x1, waiting for transfers between devices, shards(): lax.all_gather(hidden, 'tensor', axis=0, tiled=True)  62.7 us
    all_gather x1, waiting for transfers between devices, shards(): queries = lax.all_gather(query_tok, 'tensor', axis=0, tiled=True)  45 us
  transfers between devices with their start and end apart: 11, of which 9 were waited for; matrix products, arithmetic and copies ran while one was open for 4% of the time, Pallas kernels for 0%

commit v1 on v0

v1 whole, which is shorter than its diff:
```python
import math

import jax
import jax.numpy as jnp
from jax import lax
from jax.sharding import PartitionSpec as P

HEAD_DIM = 128
CH = 1024
NCH = 12
REQS = 3
NX = 4
NZ = 8

THETA = 500000.0
EPSILON = 1e-06
NEGATIVE = -1e30

ZG = [[x * NZ + z for z in range(NZ)] for x in range(NX)]
XG = [[x * NZ + z for x in range(NX)] for z in range(NZ)]


def token_meta(rows, order_row, length_row, offset_row):
    slot_index = rows // CH
    in_span = rows % CH
    ordinal = jnp.sum(
        jnp.where(
            slot_index[:, None] == jnp.arange(NCH, dtype=jnp.int32)[None, :], order_row[None, :], 0
        ),
        axis=1,
    )
    request_end = jnp.cumsum(length_row)
    request = jnp.sum((ordinal[:, None] >= request_end[None, :]).astype(jnp.int32), axis=1)
    request_pick = request[:, None] == jnp.arange(REQS, dtype=jnp.int32)[None, :]
    request_start = jnp.sum(jnp.where(request_pick, (request_end - length_row)[None, :], 0), axis=1)
    request_shift = jnp.sum(jnp.where(request_pick, offset_row[None, :], 0), axis=1)
    position = request_shift + (ordinal - request_start) * CH + in_span
    return (request, position, in_span)


def frequencies(index_float):
    return jnp.exp(index_float * (-2.0 * math.log(THETA) / HEAD_DIM))


def rope_full(values_in, position):
    row_count = values_in.shape[0]
    half_dim = HEAD_DIM // 2
    split = values_in.reshape(row_count, -1, HEAD_DIM)
    angles = (
        position.astype(jnp.float32)[:, None]
        * frequencies(jnp.arange(half_dim, dtype=jnp.int32).astype(jnp.float32))[None, :]
    )
    cosine = jnp.cos(angles)[:, None, :]
    sine = jnp.sin(angles)[:, None, :]
    first = split[..., :half_dim]
    second = split[..., half_dim:]
    turned = jnp.concatenate(
        [first * cosine - second * sine, second * cosine + first * sine], axis=-1
    )
    return turned.reshape(row_count, -1)


def rms_scale(values_in, gain):
    return (
        values_in
        * lax.rsqrt(jnp.mean(values_in * values_in, axis=-1, keepdims=True) + EPSILON)
        * gain
    )


def swap(blocks, groups):
    return lax.all_to_all(
        blocks, "tensor", split_axis=0, concat_axis=0, axis_index_groups=groups, tiled=True
    )


def share(block, groups):
    count = len(groups[0])
    return swap(jnp.broadcast_to(block[None], (count,) + block.shape), groups)


def shards(
    hidden_sel,
    picked,
    order,
    lengths,
    offsets,
    cache_keys,
    cache_values,
    w_qkv,
    w_out,
    w_gate_up,
    w_down,
    gains,
):
    f32, bf16 = jnp.float32, jnp.bfloat16
    hidden = hidden_sel[0]
    meta = (order[0], lengths[0], offsets[0])
    picked_row = picked[0]
    lane = lax.axis_index("tensor")
    at_x, at_z = lane // NZ, lane % NZ
    own, width = hidden.shape
    sel = own * NX * NZ
    ctx = cache_keys.shape[1]
    part = width // NX
    heads = part // HEAD_DIM
    qkv_full = lax.all_gather(w_qkv, "dp", axis=1, tiled=True)
    out_full = lax.all_gather(w_out, "dp", axis=1, tiled=True)
    gate_full = lax.all_gather(w_gate_up, "dp", axis=1, tiled=True)
    down_full = lax.all_gather(w_down, "dp", axis=1, tiled=True)
    out_rows = share(out_full, ZG).reshape(part, width)
    cache = jnp.concatenate([cache_keys[0], cache_values[0]], axis=0)
    cache = swap(cache.reshape(2 * ctx, NX, part).transpose(1, 0, 2), XG)
    raw_keys = cache[:, :ctx].reshape(NX * ctx, part)
    values_c = cache[:, ctx:].reshape(NX * ctx, part)
    rows = (
        (jnp.arange(NX, dtype=jnp.int32)[:, None] * NZ + at_z) * ctx
        + jnp.arange(ctx, dtype=jnp.int32)[None, :]
    ).reshape(-1)
    c_req, c_pos, c_local = token_meta(rows, *meta)
    chosen = jnp.any(picked_row[:, None] == rows[None, :], axis=0)
    keys_c = rope_full(raw_keys.astype(f32), c_pos - c_local).astype(bf16)
    x_rows = share(hidden, ZG).reshape(NZ * own, width)
    all_rows = share(x_rows, XG).reshape(sel, width)
    proj = jnp.einsum("nd,kdc->knc", all_rows, qkv_full, preferred_element_type=f32).astype(bf16)
    cols = proj.shape[2]
    q_req, q_pos, _ = token_meta(picked_row, *meta)

    def by_z(rows_in):
        return rows_in.reshape(NX, NZ, own, -1).transpose(1, 0, 2, 3).reshape(NZ, NX * own, -1)

    def of_z(vector):
        return lax.dynamic_index_in_dim(
            vector.reshape(NX, NZ, own).transpose(1, 0, 2).reshape(NZ, NX * own),
            at_z, 0, keepdims=False,
        )

    f_req, f_pos = of_z(q_req), of_z(q_pos)
    payload = jnp.concatenate(
        [jnp.broadcast_to(proj[0][None], (NZ, sel, cols)), by_z(proj[1]), by_z(proj[2])], axis=1
    )
    got = swap(payload, ZG).transpose(1, 0, 2).reshape(-1, part).astype(f32)
    squares = jnp.sum(got[: sel + NX * own] ** 2, axis=1)
    squares = jnp.sum(share(squares, XG), axis=0)
    scale = lax.rsqrt(squares / width + EPSILON)[:, None]
    gain_x = lax.dynamic_slice_in_dim(gains, at_x * part, part, axis=1)
    query = rope_full(got[:sel] * scale[:sel] * gain_x[0], q_pos).astype(bf16)
    key_f = rope_full(got[sel : sel + NX * own] * scale[sel:] * gain_x[1], f_pos).astype(bf16)
    value_f = got[sel + NX * own :].astype(bf16)
    fresh_out = swap(key_f.reshape(NX, own, part), XG).transpose(1, 0, 2).reshape(own, width)
    all_keys = jnp.concatenate([keys_c, key_f], axis=0).reshape(-1, heads, HEAD_DIM)
    all_values = jnp.concatenate([values_c, value_f], axis=0).reshape(-1, heads, HEAD_DIM)
    k_req = jnp.concatenate([c_req, f_req])
    k_pos = jnp.concatenate([c_pos, f_pos])
    live = jnp.concatenate([jnp.logical_not(chosen), jnp.ones((NX * own,), bool)])
    scores = jnp.einsum(
        "qhd,khd->hqk", query.reshape(sel, heads, HEAD_DIM), all_keys, preferred_element_type=f32
    ) * HEAD_DIM ** (-0.5)
    usable = (
        (q_req[:, None] == k_req[None, :]) & (k_pos[None, :] <= q_pos[:, None]) & live[None, :]
    )
    masked = jnp.where(usable[None], scores, NEGATIVE)
    top = jnp.max(masked, axis=2)
    weights = jnp.where(usable[None], jnp.exp(masked - top[:, :, None]), 0.0)
    total = jnp.sum(weights, axis=2)
    mixed = jnp.einsum(
        "hqk,khd->qhd", weights.astype(bf16), all_values, preferred_element_type=f32
    ).reshape(sel, part)
    mixed = swap(by_z(mixed.astype(bf16)), ZG).astype(f32).reshape(NZ, NX * own, heads, HEAD_DIM)
    stats = swap(by_z(jnp.concatenate([top, total], axis=0).T), ZG)
    top, total = stats[..., :heads], stats[..., heads:]
    factor = jnp.exp(top - jnp.max(top, axis=0))
    attn = jnp.sum(mixed * factor[..., None], axis=0) / jnp.sum(total * factor, axis=0)[..., None]
    attn = attn.reshape(NX * own, part).astype(bf16)
    y_part = jnp.dot(attn, out_rows, preferred_element_type=f32).astype(bf16)
    y = jnp.sum(swap(y_part.reshape(NX, own, width), XG).astype(f32), axis=0)
    hidden_next = (hidden.astype(f32) + rms_scale(y, gains[2])).astype(bf16)
    x_rows = share(hidden_next, ZG).reshape(NZ * own, width)
    all_next = share(x_rows, XG).reshape(sel, width)
    gate_part = jnp.dot(all_next, gate_full[0], preferred_element_type=f32)
    up_part = jnp.dot(all_next, gate_full[1], preferred_element_type=f32)
    activated = (jax.nn.silu(gate_part) * up_part).astype(bf16)
    down = jnp.dot(activated, down_full, preferred_element_type=f32).astype(bf16)
    down = jnp.sum(swap(down.reshape(NX, NZ * own, width), XG).astype(f32), axis=0).astype(bf16)
    down = jnp.sum(swap(down.reshape(NZ, own, width), ZG).astype(f32), axis=0)
    result = (hidden_next.astype(f32) + rms_scale(down, gains[3])).astype(bf16)
    return (result[None], fresh_out[None])


def solution(mesh):
    placed = (
        P("dp", "tensor", None),
        P("dp", None),
        P("dp", None),
        P("dp", None),
        P("dp", None),
        P("dp", "tensor", None),
        P("dp", "tensor", None),
        P(None, "dp", "tensor"),
        P("tensor", "dp"),
        P(None, "dp", "tensor"),
        P("tensor", "dp"),
        P(),
    )
    return jax.shard_map(
        shards,
        mesh=mesh,
        in_specs=placed,
        out_specs=(P("dp", "tensor", None), P("dp", "tensor", None)),
        check_vma=False,
    )
```

time: 1330 us -> 394 us (0.30)
  waiting for transfers between devices: 1050 us -> 156 us
  blocking collectives: 156 us -> 45 us
  starting transfers between devices: 16.3 us -> 72.8 us
  local copies, waits for them, and re-layouts: 31.9 us -> 45.3 us
    reduce_scatter x3 -> x0, waiting for transfers between devices: 649 us -> none  [the longest x1 218 us: shards(): lax.psum_scatter(scaled_out.astype(jnp.bfloat16), 'tensor', scatter_dimen...]
    all_gather x5 -> x2, waiting for transfers between devices: 207 us -> 2.03 us  [the longest x1 2.02 us: shards(): down_full = lax.all_gather(w_down, 'dp', axis=1, tiled=True)]
    unnamed x10 -> x2, waiting for transfers between devices: 189 us -> 1.19 us
    all_to_all x2 -> x13, waiting for transfers between devices: 7.99 us -> 153 us  [swap(): lax.all_to_all(blocks, 'tensor', split_axis=0, concat_axis=0, axis_index_...]
    pmax x1 -> x0, blocking collectives: 128 us -> none  [shards(): lax.pmax(local_max.astype(jnp.bfloat16), 'tensor').astype(local_max.dtype)]
    all_to_all x2 -> x13, starting transfers between devices: 15.6 us -> 72.6 us  [swap(): lax.all_to_all(blocks, 'tensor', split_axis=0, concat_axis=0, axis_index_...]
    all_to_all x0 -> x1, blocking collectives: none -> 17.7 us  [swap(): lax.all_to_all(blocks, 'tensor', split_axis=0, concat_axis=0, axis_index_...]
  transfers between devices with their start and end apart: 11 -> 15, of which waited for: 9 -> 12; matrix products, arithmetic and copies ran while one was open for 4% -> 19% of each run, Pallas kernels for 0% -> 0%
where the time goes in v1:
time: 394 us; the launch traced here: 391 us
  waiting for transfers between devices  156 us (40%)
  starting transfers between devices  72.8 us (18%)
  local copies, waits for them, and re-layouts  45.3 us (11%)
  blocking collectives  45 us (11%)
  other arithmetic  36.6 us (9%)
  matrix products  20.3 us (5%)
  between operations  14.7 us (4%)
    all_to_all x13, waiting for transfers between devices, swap(): lax.all_to_all(blocks, 'tensor', split_axis=0, concat_axis=0, axis_index_...  153 us
    all_to_all x13, starting transfers between devices, swap(): lax.all_to_all(blocks, 'tensor', split_axis=0, concat_axis=0, axis_index_...  72.6 us
    all_to_all x1, blocking collectives, swap(): lax.all_to_all(blocks, 'tensor', split_axis=0, concat_axis=0, axis_index_...  17.7 us
    all_gather x1, blocking collectives, shards(): qkv_full = lax.all_gather(w_qkv, 'dp', axis=1, tiled=True)  13.9 us
    all_gather x1, blocking collectives, shards(): out_full = lax.all_gather(w_out, 'dp', axis=1, tiled=True)  13.4 us
    concatenate x4, local copies, waits for them, and re-layouts, shards(): cache = jnp.concatenate([cache_keys[0], cache_values[0]], axis=0)  8.78 us
  transfers between devices with their start and end apart: 15, of which 12 were waited for; matrix products, arithmetic and copies ran while one was open for 19% of the time, Pallas kernels for 0%

profile of v1, /device:TPU:6, one launch (start us, length us, event | category | flops | bytes accessed | tf_op | source)
XLA Modules:
  0.0 390.7 jit_solution(4341000119119259487)
XLA Ops:
  8.8 8.5 %all-to-all-start.1 = ((bf16[8,16,2048]{2,1,0:T(8,128)(2,1)}), bf16[8,16,2048]{2,1,0:T(8,128)(2,1)S(1)}, u32[]{:S(2)}, u32[]{:S(2)}) async-start(bf16[8,16,2048]{2,1,0:T(8,128)(2,1)} %broadcast_in_dim.177), calls=%async_computation.1 | async-start | bytes 1048576 | tf_op jit(solution)/shard_map/all_to_all | solution.py:72
  28.8 6.0 %all-to-all-done.1 = bf16[8,16,2048]{2,1,0:T(8,128)(2,1)S(1)} async-done(((bf16[8,16,2048]{2,1,0:T(8,128)(2,1)}), bf16[8,16,2048]{2,1,0:T(8,128)(2,1)S(1)}, u32[]{:S(2)}, u32[]{:S(2)}) %all-to-all-start.1) | async-done | bytes 524320 | tf_op jit(solution)/shard_map/all_to_all | solution.py:72
  36.4 4.8 %all-to-all-start.2 = ((bf16[4,128,2048]{2,1,0:T(8,128)(2,1)}), bf16[4,128,2048]{2,1,0:T(8,128)(2,1)S(1)}, u32[]{:S(2)}, u32[]{:S(2)}) async-start(bf16[4,128,2048]{2,1,0:T(8,128)(2,1)} %broadcast_in_dim.179), calls=%async_computation.2 | async-start | bytes 4194304 | tf_op jit(solution)/shard_map/all_to_all | solution.py:72
  42.2 3.7 maximum_bitcast_fusion
  46.0 19.7 %all-to-all-done.2 = bf16[4,128,2048]{2,1,0:T(8,128)(2,1)S(1)} async-done(((bf16[4,128,2048]{2,1,0:T(8,128)(2,1)}), bf16[4,128,2048]{2,1,0:T(8,128)(2,1)S(1)}, u32[]{:S(2)}, u32[]{:S(2)}) %all-to-all-start.2) | async-done | bytes 2097184 | tf_op jit(solution)/shard_map/all_to_all | solution.py:72
  67.0 5.7 %all-to-all-start = ((bf16[4,768,512]{2,1,0:T(8,128)(2,1)}), bf16[4,768,512]{2,1,0:T(8,128)(2,1)S(1)}, u32[]{:S(2)}, u32[]{:S(2)}) async-start(bf16[4,768,512]{2,1,0:T(8,128)(2,1)} %maximum_bitcast_fusion), calls=%async_computation | async-start | bytes 6291456 | tf_op jit(solution)/shard_map/all_to_all | solution.py:72
  73.6 13.9 %all_gather.12 = bf16[3,2048,64]{1,2,0:T(8,128)(2,1)S(1)} all-gather(bf16[3,256,64]{1,2,0:T(8,128)(2,1)S(1)} %copy-done.13), channel_id=1, replica_groups=mesh['dp'=8,'tensor'=32] {'dp'}, dimensions={1}, use_global_device_ids=true | all-gather | bytes 884736 | tf_op jit(solution)/shard_map/all_gather | solution.py:107
  90.0 4.3 %multiply_cosine_fusion = (f32[1536,64]{1,0:T(8,128)}, f32[1536,64]{1,0:T(8,128)}) fusion(f32[64]{0:T(128)S(1)} %multiply_exponential_fusion, f32[1536]{0:T(1024)S(1)} %get-tuple-element.35), kind=kLoop, calls=%fused_computation.33 | loop fusion | flops 98304 | bytes 792832 | tf_op jit(solution)/shard_map/cos | solution.py:53
  99.1 8.4 %all-to-all-done = bf16[4,768,512]{2,1,0:T(8,128)(2,1)S(1)} async-done(((bf16[4,768,512]{2,1,0:T(8,128)(2,1)}), bf16[4,768,512]{2,1,0:T(8,128)(2,1)S(1)}, u32[]{:S(2)}, u32[]{:S(2)}) %all-to-all-start) | async-done | bytes 3145760 | tf_op jit(solution)/shard_map/all_to_all | solution.py:72
  107.5 4.2 %all-to-all-start.3 = ((bf16[8,640,64]{1,2,0:T(8,128)(2,1)}), bf16[8,640,64]{1,2,0:T(8,128)(2,1)}, u32[]{:S(2)}, u32[]{:S(2)}) async-start(bf16[8,640,64]{1,2,0:T(8,128)(2,1)} %pad_maximum_fusion), calls=%async_computation.3 | async-start | bytes 1310720 | tf_op jit(solution)/shard_map/all_to_all | solution.py:72
  120.2 3.5 fusion.71
  123.7 6.7 %all-to-all-done.3 = bf16[8,640,64]{1,2,0:T(8,128)(2,1)} async-done(((bf16[8,640,64]{1,2,0:T(8,128)(2,1)}), bf16[8,640,64]{1,2,0:T(8,128)(2,1)}, u32[]{:S(2)}, u32[]{:S(2)}) %all-to-all-start.3) | async-done | bytes 655392 | tf_op jit(solution)/shard_map/all_to_all | solution.py:72
  133.5 5.3 %all-to-all-start.4 = ((f32[4,1,576]{2,1,0:T(1,128)}), f32[4,1,576]{2,1,0:T(1,128)S(1)}, u32[]{:S(2)}, u32[]{:S(2)}) async-start(f32[4,1,576]{2,1,0:T(1,128)} %broadcast_in_dim.196), calls=%async_computation.4 | async-start | bytes 20480 | tf_op jit(solution)/shard_map/all_to_all | solution.py:72
  138.8 4.8 %subtract_convert_fusion = (bf16[1536,4,64]{2,0,1:T(8,128)(2,1)}, bf16[1536,4,64]{2,0,1:T(8,128)(2,1)}) fusion(f32[1536,4,64]{2,1,0:T(4,128)} %get-tuple-element.18, f32[1536,4,64]{2,1,0:T(4,128)S(1)} %copy-done.1, f32[1536,64]{1,0:T(8,128)} %get-tuple-element.37, f32[1536,64]{1,0:T(8,128)} %get-tuple-element.36), kind=kLoop, calls=%fused_computation.10 | loop fusion | flops 3145728 | bytes 5505024 | tf_op jit(solution)/shard_map/convert.3
  154.0 3.6 fusion
  157.6 3.3 fusion.1
  166.8 7.6 %fusion.21 = bf16[512,4,128]{0,2,1:T(8,128)(2,1)S(1)} fusion(f32[4,512,1600]{1,2,0:T(8,128)} %copy-done, f32[4,512]{1,0:T(4,128)S(1)} %get-tuple-element.42, pred[512,1600]{0,1:T(8,128)(4,1)S(1)} %copy-done.5, bf16[64,4,128]{2,0,1:T(8,128)(2,1)S(1)} %copy-done.14, bf16[1536,4,128]{2,0,1:T(8,128)(2,1)S(1)} %copy-done.7), kind=kOutput, calls=%fused_computation.27 | convolution fusion | flops 858783744 | bytes 16097280 | tf_op jit(solution)/shard_map/hqk,khd->qhd/dot_general | solution.py:166
  175.8 7.1 %all-to-all-start.5 = ((bf16[8,64,512]{2,1,0:T(8,128)(2,1)}), bf16[8,64,512]{2,1,0:T(8,128)(2,1)S(1)}, u32[]{:S(2)}, u32[]{:S(2)}) async-start(bf16[8,64,512]{2,1,0:T(8,128)(2,1)} %bitcast.33), calls=%async_computation.5 | async-start | bytes 1048576 | tf_op jit(solution)/shard_map/all_to_all | solution.py:72
  182.9 13.4 %all_gather.13 = bf16[64,2048]{1,0:T(8,128)(2,1)S(1)} all-gather(bf16[64,256]{1,0:T(8,128)(2,1)S(1)} %copy-done.15), channel_id=1, replica_groups=mesh['dp'=8,'tensor'=32] {'dp'}, dimensions={1}, use_global_device_ids=true | all-gather | bytes 294912 | tf_op jit(solution)/shard_map/all_gather | solution.py:108
  199.0 6.1 %all-to-all-start.7 = ((bf16[8,64,2048]{2,1,0:T(8,128)(2,1)}), bf16[8,64,2048]{2,1,0:T(8,128)(2,1)S(1)}, u32[]{:S(2)}, u32[]{:S(2)}) async-start(bf16[8,64,2048]{2,1,0:T(8,128)(2,1)} %broadcast_in_dim.199), calls=%async_computation.7 | async-start | bytes 4194304 | tf_op jit(solution)/shard_map/all_to_all | solution.py:72
  211.1 45.6 %all-to-all-done.7 = bf16[8,64,2048]{2,1,0:T(8,128)(2,1)S(1)} async-done(((bf16[8,64,2048]{2,1,0:T(8,128)(2,1)}), bf16[8,64,2048]{2,1,0:T(8,128)(2,1)S(1)}, u32[]{:S(2)}, u32[]{:S(2)}) %all-to-all-start.7) | async-done | bytes 2097184 | tf_op jit(solution)/shard_map/all_to_all | solution.py:72
  257.9 4.8 %all-to-all-start.8 = ((bf16[4,16,2048]{2,1,0:T(8,128)(2,1)}), bf16[4,16,2048]{2,1,0:T(8,128)(2,1)S(1)}, u32[]{:S(2)}, u32[]{:S(2)}) async-start(bf16[4,16,2048]{2,1,0:T(8,128)(2,1)} %bitcast.37), calls=%async_computation.8 | async-start | bytes 524288 | tf_op jit(solution)/shard_map/all_to_all | solution.py:72
  262.8 4.6 %all-to-all-done.8 = bf16[4,16,2048]{2,1,0:T(8,128)(2,1)S(1)} async-done(((bf16[4,16,2048]{2,1,0:T(8,128)(2,1)}), bf16[4,16,2048]{2,1,0:T(8,128)(2,1)S(1)}, u32[]{:S(2)}, u32[]{:S(2)}) %all-to-all-start.8) | async-done | bytes 262176 | tf_op jit(solution)/shard_map/all_to_all | solution.py:72
  267.7 17.7 %all_to_all.71 = bf16[8,16,2048]{2,1,0:T(8,128)(2,1)S(1)} all-to-all(bf16[8,16,2048]{2,1,0:T(8,128)(2,1)S(1)} %broadcast_in_dim.201), channel_id=1, replica_groups={{0,1,2,3,4,5,6,7},{8,9,10,11,12,13,14,15},{16,17,18,19,20,21,22,23},{24..., dimensions={0} | all-to-all | bytes 1048576 | tf_op jit(solution)/shard_map/all_to_all | solution.py:72
  287.0 5.7 %all-to-all-start.10 = ((bf16[4,128,2048]{2,1,0:T(8,128)(2,1)}), bf16[4,128,2048]{2,1,0:T(8,128)(2,1)S(1)}, u32[]{:S(2)}, u32[]{:S(2)}) async-start(bf16[4,128,2048]{2,1,0:T(8,128)(2,1)} %broadcast_in_dim.203), calls=%async_computation.10 | async-start | bytes 4194304 | tf_op jit(solution)/shard_map/all_to_all | solution.py:72
  293.4 19.5 %all-to-all-done.10 = bf16[4,128,2048]{2,1,0:T(8,128)(2,1)S(1)} async-done(((bf16[4,128,2048]{2,1,0:T(8,128)(2,1)}), bf16[4,128,2048]{2,1,0:T(8,128)(2,1)S(1)}, u32[]{:S(2)}, u32[]{:S(2)}) %all-to-all-start.10) | async-done | bytes 2097184 | tf_op jit(solution)/shard_map/all_to_all | solution.py:72
  316.8 5.1 %convolution_convert_fusion = bf16[512,2048]{1,0:T(8,128)(2,1)} fusion(bf16[256,2048]{1,0:T(8,128)(2,1)} %all-gather.5.cloned.1.call-done, bf16[512,2048]{1,0:T(8,128)(2,1)S(1)} %bitcast.112, bf16[2,2048,256]{2,1,0:T(8,128)(2,1)} %all-gather.3.cloned.1.call-done, f32[512,256]{1,0:T(8,128)S(1)} %fusion.28), kind=kOutput, calls=%fused_computation.12 | convolution fusion | flops 1075576832 | bytes 6815744 | tf_op jit(solution)/shard_map/dot_general | solution.py:183
  322.0 4.8 %all-to-all-start.11 = ((bf16[4,128,2048]{2,1,0:T(8,128)(2,1)}), bf16[4,128,2048]{2,1,0:T(8,128)(2,1)S(1)}, u32[]{:S(2)}, u32[]{:S(2)}) async-start(bf16[4,128,2048]{2,1,0:T(8,128)(2,1)} %bitcast.113), calls=%async_computation.11 | async-start | bytes 4194304 | tf_op jit(solution)/shard_map/all_to_all | solution.py:72
  327.5 23.9 %all-to-all-done.11 = bf16[4,128,2048]{2,1,0:T(8,128)(2,1)S(1)} async-done(((bf16[4,128,2048]{2,1,0:T(8,128)(2,1)}), bf16[4,128,2048]{2,1,0:T(8,128)(2,1)S(1)}, u32[]{:S(2)}, u32[]{:S(2)}) %all-to-all-start.11) | async-done | bytes 2097184 | tf_op jit(solution)/shard_map/all_to_all | solution.py:72
  351.5 5.3 %all-to-all-start.13 = ((bf16[4,16,512]{2,1,0:T(8,128)(2,1)}), bf16[4,16,512]{2,1,0:T(8,128)(2,1)S(1)}, u32[]{:S(2)}, u32[]{:S(2)}) async-start(bf16[4,16,512]{2,1,0:T(8,128)(2,1)} %convert_element_type.166), calls=%async_computation.13 | async-start | bytes 131072 | tf_op jit(solution)/shard_map/all_to_all | solution.py:72
  360.3 7.0 %all-to-all-start.12 = ((bf16[8,16,2048]{2,1,0:T(8,128)(2,1)}), bf16[8,16,2048]{2,1,0:T(8,128)(2,1)S(1)}, u32[]{:S(2)}, u32[]{:S(2)}) async-start(bf16[8,16,2048]{2,1,0:T(8,128)(2,1)} %bitcast.46), calls=%async_computation.12 | async-start | bytes 1048576 | tf_op jit(solution)/shard_map/all_to_all | solution.py:72
  368.1 14.9 %all-to-all-done.12 = bf16[8,16,2048]{2,1,0:T(8,128)(2,1)S(1)} async-done(((bf16[8,16,2048]{2,1,0:T(8,128)(2,1)}), bf16[8,16,2048]{2,1,0:T(8,128)(2,1)S(1)}, u32[]{:S(2)}, u32[]{:S(2)}) %all-to-all-start.12) | async-done | bytes 524320 | tf_op jit(solution)/shard_map/all_to_all | solution.py:72
  (172 shorter events, 76.4 us)
Async XLA Ops:
  8.8 26.0 %all-to-all-start.1 = ((bf16[8,16,2048]{2,1,0:T(8,128)(2,1)}), bf16[8,16,2048]{2,1,0:T(8,128)(2,1)S(1)}, u32[]{:S(2)}, u32[]{:S(2)}) async-start(bf16[8,16,2048]{2,1,0:T(8,128)(2,1)} %broadcast_in_dim.177), calls=%async_computation.1 | async-start | bytes 1048576 | tf_op jit(solution)/shard_map/all_to_all | solution.py:72
  22.6 4.5 %copy-start.16 = (s32[1,512]{1,0:T(1,128)S(1)}, s32[1,512]{1,0:T(1,128)}, u32[]{:S(2)}) copy-start(s32[1,512]{1,0:T(1,128)} %param.13) | copy-start | bytes 6148
  22.6 4.5 %copy-start.19 = (s32[1,12]{1,0:T(1,128)S(1)}, s32[1,12]{1,0:T(1,128)}, u32[]{:S(2)}) copy-start(s32[1,12]{1,0:T(1,128)} %param.14) | copy-start | bytes 148
  22.6 4.7 %copy-start.20 = (s32[1,3]{1,0:T(1,128)S(1)}, s32[1,3]{1,0:T(1,128)}, u32[]{:S(2)}) copy-start(s32[1,3]{1,0:T(1,128)} %param.15) | copy-start | bytes 40
  22.6 4.7 %copy-start.18 = (s32[1,3]{1,0:T(1,128)S(1)}, s32[1,3]{1,0:T(1,128)}, u32[]{:S(2)}) copy-start(s32[1,3]{1,0:T(1,128)} %param.16) | copy-start | bytes 40
  36.4 29.2 %all-to-all-start.2 = ((bf16[4,128,2048]{2,1,0:T(8,128)(2,1)}), bf16[4,128,2048]{2,1,0:T(8,128)(2,1)S(1)}, u32[]{:S(2)}, u32[]{:S(2)}) async-start(bf16[4,128,2048]{2,1,0:T(8,128)(2,1)} %broadcast_in_dim.179), calls=%async_computation.2 | async-start | bytes 4194304 | tf_op jit(solution)/shard_map/all_to_all | solution.py:72
  46.0 27.6 %copy-start.13 = (bf16[3,256,64]{1,2,0:T(8,128)(2,1)S(1)}, bf16[3,256,64]{1,2,0:T(8,128)(2,1)}, u32[]{:S(2)}) copy-start(bf16[3,256,64]{1,2,0:T(8,128)(2,1)} %param.19) | copy-start | bytes 294916
  67.0 40.5 %all-to-all-start = ((bf16[4,768,512]{2,1,0:T(8,128)(2,1)}), bf16[4,768,512]{2,1,0:T(8,128)(2,1)S(1)}, u32[]{:S(2)}, u32[]{:S(2)}) async-start(bf16[4,768,512]{2,1,0:T(8,128)(2,1)} %maximum_bitcast_fusion), calls=%async_computation | async-start | bytes 6291456 | tf_op jit(solution)/shard_map/all_to_all | solution.py:72
  72.7 21.5 %copy-start.4 = (bf16[4,128,2048]{2,1,0:T(8,128)(2,1)S(1)}, bf16[4,128,2048]{2,1,0:T(8,128)(2,1)}, u32[]{:S(2)}) copy-start(bf16[4,128,2048]{2,1,0:T(8,128)(2,1)} %copy-done.3) | copy-start | bytes 6291460
  107.5 22.9 %all-to-all-start.3 = ((bf16[8,640,64]{1,2,0:T(8,128)(2,1)}), bf16[8,640,64]{1,2,0:T(8,128)(2,1)}, u32[]{:S(2)}, u32[]{:S(2)}) async-start(bf16[8,640,64]{1,2,0:T(8,128)(2,1)} %pad_maximum_fusion), calls=%async_computation.3 | async-start | bytes 1310720 | tf_op jit(solution)/shard_map/all_to_all | solution.py:72
  123.7 15.1 %copy-start.1 = (f32[1536,4,64]{2,1,0:T(4,128)S(1)}, f32[1536,4,64]{2,1,0:T(4,128)}, u32[]{:S(2)}) copy-start(f32[1536,4,64]{2,1,0:T(4,128)} %get-tuple-element.17) | copy-start | bytes 4718596
  133.5 16.3 %all-to-all-start.4 = ((f32[4,1,576]{2,1,0:T(1,128)}), f32[4,1,576]{2,1,0:T(1,128)S(1)}, u32[]{:S(2)}, u32[]{:S(2)}) async-start(f32[4,1,576]{2,1,0:T(1,128)} %broadcast_in_dim.196), calls=%async_computation.4 | async-start | bytes 20480 | tf_op jit(solution)/shard_map/all_to_all | solution.py:72
  146.0 3.9 %slice-start = ((f32[640,8,64]{0,2,1:T(8,128)}), f32[512,8,64]{0,2,1:T(8,128)S(1)}, s32[]{:S(2)}) async-start(f32[640,8,64]{0,2,1:T(8,128)} %copy-done.2), calls=%async_computation.16 | async-start | bytes 2097152 | tf_op jit(solution)/shard_map/slice | solution.py:147
  150.1 2.0 copy-start.11
  150.5 3.2 copy-start.5
  151.9 2.0 copy-start.9
  157.6 4.9 %copy-start = (f32[4,512,1600]{1,2,0:T(8,128)}, f32[4,512,1600]{1,2,0:T(8,128)S(1)}, u32[]{:S(2)}) copy-start(f32[4,512,1600]{1,2,0:T(8,128)S(1)} %get-tuple-element.43) | copy-start | bytes 39321604
  157.6 9.2 %copy-start.7 = (bf16[1536,4,128]{2,0,1:T(8,128)(2,1)S(1)}, bf16[1536,4,128]{2,0,1:T(8,128)(2,1)}, u32[]{:S(2)}) copy-start(bf16[1536,4,128]{2,0,1:T(8,128)(2,1)} %copy.128) | copy-start | bytes 4718596
  157.6 9.2 %copy-start.14 = (bf16[64,4,128]{2,0,1:T(8,128)(2,1)S(1)}, bf16[64,4,128]{2,0,1:T(8,128)(2,1)}, u32[]{:S(2)}) copy-start(bf16[64,4,128]{2,0,1:T(8,128)(2,1)} %copy.129) | copy-start | bytes 196612
  163.4 12.4 %all-to-all-start.6 = ((f32[8,1,512]{2,1,0:T(1,128)}), f32[8,1,512]{2,1,0:T(1,128)S(1)}, u32[]{:S(2)}, u32[]{:S(2)}) async-start(f32[8,1,512]{2,1,0:T(1,128)} %reshape.668), calls=%async_computation.6 | async-start | bytes 32768 | tf_op jit(solution)/shard_map/all_to_all | solution.py:72
  174.4 8.5 %copy-start.15 = (bf16[64,256]{1,0:T(8,128)(2,1)S(1)}, bf16[64,256]{1,0:T(8,128)(2,1)}, u32[]{:S(2)}) copy-start(bf16[64,256]{1,0:T(8,128)(2,1)} %param.20) | copy-start | bytes 98308
  175.8 21.6 %all-to-all-start.5 = ((bf16[8,64,512]{2,1,0:T(8,128)(2,1)}), bf16[8,64,512]{2,1,0:T(8,128)(2,1)S(1)}, u32[]{:S(2)}, u32[]{:S(2)}) async-start(bf16[8,64,512]{2,1,0:T(8,128)(2,1)} %bitcast.33), calls=%async_computation.5 | async-start | bytes 1048576 | tf_op jit(solution)/shard_map/all_to_all | solution.py:72
  199.0 57.8 %all-to-all-start.7 = ((bf16[8,64,2048]{2,1,0:T(8,128)(2,1)}), bf16[8,64,2048]{2,1,0:T(8,128)(2,1)S(1)}, u32[]{:S(2)}, u32[]{:S(2)}) async-start(bf16[8,64,2048]{2,1,0:T(8,128)(2,1)} %broadcast_in_dim.199), calls=%async_computation.7 | async-start | bytes 4194304 | tf_op jit(solution)/shard_map/all_to_all | solution.py:72
  205.0 88.3 %all-gather.3.cloned.1.call-start = ((), (), s32[]{:S(2)}) async-start(), calls=%async_computation.14 | async-start | bytes 2359296 | tf_op jit(solution)/shard_map/all_gather | solution.py:109
  207.9 54.9 %copy-start.17 = (f32[4,2048]{1,0:T(4,128)S(1)}, f32[4,2048]{1,0:T(4,128)}, u32[]{:S(2)}) copy-start(f32[4,2048]{1,0:T(4,128)} %param.23) | copy-start | bytes 98308
  209.3 58.2 %copy-start.10 = (bf16[1,16,2048]{2,1,0:T(8,128)(2,1)S(1)}, bf16[1,16,2048]{2,1,0:T(8,128)(2,1)}, u32[]{:S(2)}) copy-start(bf16[1,16,2048]{2,1,0:T(8,128)(2,1)} %param.12) | copy-start | bytes 196612
  257.9 9.4 %all-to-all-start.8 = ((bf16[4,16,2048]{2,1,0:T(8,128)(2,1)}), bf16[4,16,2048]{2,1,0:T(8,128)(2,1)S(1)}, u32[]{:S(2)}, u32[]{:S(2)}) async-start(bf16[4,16,2048]{2,1,0:T(8,128)(2,1)} %bitcast.37), calls=%async_computation.8 | async-start | bytes 524288 | tf_op jit(solution)/shard_map/all_to_all | solution.py:72
  287.0 25.9 %all-to-all-start.10 = ((bf16[4,128,2048]{2,1,0:T(8,128)(2,1)}), bf16[4,128,2048]{2,1,0:T(8,128)(2,1)S(1)}, u32[]{:S(2)}, u32[]{:S(2)}) async-start(bf16[4,128,2048]{2,1,0:T(8,128)(2,1)} %broadcast_in_dim.203), calls=%async_computation.10 | async-start | bytes 4194304 | tf_op jit(solution)/shard_map/all_to_all | solution.py:72
  292.6 24.2 %all-gather.5.cloned.1.call-start = ((), (), s32[]{:S(2)}) async-start(), calls=%async_computation.15 | async-start | bytes 1179648 | tf_op jit(solution)/shard_map/all_gather | solution.py:110
  322.0 29.5 %all-to-all-start.11 = ((bf16[4,128,2048]{2,1,0:T(8,128)(2,1)}), bf16[4,128,2048]{2,1,0:T(8,128)(2,1)S(1)}, u32[]{:S(2)}, u32[]{:S(2)}) async-start(bf16[4,128,2048]{2,1,0:T(8,128)(2,1)} %bitcast.113), calls=%async_computation.11 | async-start | bytes 4194304 | tf_op jit(solution)/shard_map/all_to_all | solution.py:72
  351.5 8.9 %all-to-all-start.13 = ((bf16[4,16,512]{2,1,0:T(8,128)(2,1)}), bf16[4,16,512]{2,1,0:T(8,128)(2,1)S(1)}, u32[]{:S(2)}, u32[]{:S(2)}) async-start(bf16[4,16,512]{2,1,0:T(8,128)(2,1)} %convert_element_type.166), calls=%async_computation.13 | async-start | bytes 131072 | tf_op jit(solution)/shard_map/all_to_all | solution.py:72
  360.3 22.6 %all-to-all-start.12 = ((bf16[8,16,2048]{2,1,0:T(8,128)(2,1)}), bf16[8,16,2048]{2,1,0:T(8,128)(2,1)S(1)}, u32[]{:S(2)}, u32[]{:S(2)}) async-start(bf16[8,16,2048]{2,1,0:T(8,128)(2,1)} %bitcast.46), calls=%async_computation.12 | async-start | bytes 1048576 | tf_op jit(solution)/shard_map/all_to_all | solution.py:72
  (6 other events, 9.2 us)
Sparse Core Ops, SparseCore 0:
  207.7 28.6 all-gather.2
  295.3 21.5 all-gather.4

commit v2 on v1

v2 whole, which is shorter than its diff:
```python
import math

import jax
import jax.numpy as jnp
from jax import lax
from jax.experimental import pallas as pl
from jax.experimental.pallas import tpu as pltpu
from jax.sharding import PartitionSpec as P

HEAD_DIM = 128
CH = 1024
NCH = 12
REQS = 3
NX = 4
NZ = 8
NDP = 8
NY = 4
D = 2048
PART = D // NX
HEADS = PART // HEAD_DIM
OWN = 16
GRP = NX * OWN
SEL = NZ * GRP
CTX = 384
CACHED = NX * CTX
KEYS = CACHED + 128
SPAN = 1 << 14
DEAD = 1 << 30

THETA = 500000.0
EPSILON = 1e-06
NEGATIVE = -1e30
FLOOR = -1e20
SCORE = HEAD_DIM ** (-0.5) * math.log2(math.e)
MESH = pl.DeviceIdType.MESH
F32, BF16 = jnp.float32, jnp.bfloat16
HIGH = lax.Precision.HIGHEST


def lanes(rows):
    return lax.broadcasted_iota(jnp.int32, (rows, HEAD_DIM), 1)


def kernel(
    hidden,
    keys,
    values,
    w4,
    wo,
    wm,
    gains,
    qmeta,
    fcode,
    qcos,
    qsin,
    scos,
    ssin,
    sbase,
    out,
    fresh,
    hid,
    w4buf,
    wobuf,
    wbuf,
    kraw,
    kall,
    vall,
    kcode,
    qpk,
    kvs,
    qrecv,
    kvrecv,
    sq,
    stat,
    qh,
    kf,
    frecv,
    obuf,
    obst,
    orecv,
    strecv,
    ysend,
    yrecv,
    hn,
    hbuf,
    act,
    dsend,
    drecv,
    hz_s,
    hz_r,
    hx_s,
    hx_r,
    w4_s,
    w4_r,
    oz_s,
    oz_r,
    oy_s,
    oy_r,
    os_s,
    os_r,
    wx_s,
    wx_r,
    wy_s,
    wy_r,
    ws_s,
    ws_r,
    k_s,
    k_r,
    v_s,
    v_r,
    q_s,
    q_r,
    c_s,
    c_r,
    st_s,
    st_r,
    f_s,
    f_r,
    o_s,
    o_r,
    t_s,
    t_r,
    y_s,
    y_r,
    n_s,
    n_r,
    d_s,
    d_r,
    loc,
):
    tens = lax.axis_index("tensor")
    dp = lax.axis_index("dp")
    x = lax.div(tens, NZ)
    z = lax.rem(tens, NZ)
    core = lax.rem(dp, 2)
    sib = dp + 1 - 2 * core

    def xa(k):
        return lax.rem(x + k, NX)

    def za(k):
        return lax.rem(z + k, NZ)

    def ya(k):
        return lax.rem(dp + 2 * k, NDP)

    def da(k):
        return lax.rem(dp + k, NDP)

    def zdev(k):
        return {"tensor": x * NZ + za(k)}

    def xdev(k):
        return {"tensor": xa(k) * NZ + z}

    def send(src, dst, ssem, rsem, dev):
        return pltpu.make_async_remote_copy(
            src_ref=src, dst_ref=dst, send_sem=ssem, recv_sem=rsem, device_id=dev,
            device_id_type=MESH,
        )

    def each(first, last, body):
        def step(k, carry):
            body(k)
            return carry

        lax.fori_loop(first, last, step, 0)

    def hz(k):
        return send(hidden, hid.at[z * NX + x], hz_s.at[k], hz_r.at[k], zdev(k))

    def hz_in(k):
        at = hid.at[za(NZ - k) * NX + x]
        return send(at, at, hz_s.at[k], hz_r.at[k], zdev(k))

    def hx(k, j):
        at = hid.at[za(NZ - k) * NX + x]
        return send(at, at, hx_s.at[k, j], hx_r.at[k, j], xdev(j))

    def hx_in(k, j):
        at = hid.at[za(NZ - k) * NX + xa(NX - j)]
        return send(at, at, hx_s.at[k, j], hx_r.at[k, j], xdev(j))

    def w4c(k):
        return send(w4, w4buf.at[dp], w4_s.at[k], w4_r.at[k], {"dp": da(k)})

    def w4_in(k):
        at = w4buf.at[da(NDP - k)]
        return send(at, at, w4_s.at[k], w4_r.at[k], {"dp": da(k)})

    def oz(k):
        return send(wo, wobuf.at[dp, z], oz_s.at[k], oz_r.at[k], zdev(k))

    def oz_in(k):
        at = wobuf.at[dp, za(NZ - k)]
        return send(at, at, oz_s.at[k], oz_r.at[k], zdev(k))

    def oy(k):
        at = wobuf.at[dp]
        return send(at, at, oy_s.at[k], oy_r.at[k], {"dp": ya(k)})

    def oy_in(k):
        at = wobuf.at[ya(NY - k)]
        return send(at, at, oy_s.at[k], oy_r.at[k], {"dp": ya(k)})

    def osib(k):
        at = wobuf.at[ya(NY - k)]
        return send(at, at, os_s.at[k], os_r.at[k], {"dp": sib})

    def osib_in(k):
        at = wobuf.at[lax.rem(sib + 2 * (NY - k), NDP)]
        return send(at, at, os_s.at[k], os_r.at[k], {"dp": sib})

    def wx(k):
        return send(wm, wbuf.at[dp, x], wx_s.at[k], wx_r.at[k], xdev(k))

    def wx_in(k):
        at = wbuf.at[dp, xa(NX - k)]
        return send(at, at, wx_s.at[k], wx_r.at[k], xdev(k))

    def wy(k, j):
        at = wbuf.at[dp, xa(NX - k)]
        return send(at, at, wy_s.at[k, j], wy_r.at[k, j], {"dp": ya(j)})

    def wy_in(k, j):
        at = wbuf.at[ya(NY - j), xa(NX - k)]
        return send(at, at, wy_s.at[k, j], wy_r.at[k, j], {"dp": ya(j)})

    def ws(k, j):
        at = wbuf.at[ya(NY - j), xa(NX - k)]
        return send(at, at, ws_s.at[k, j], ws_r.at[k, j], {"dp": sib})

    def ws_in(k, j):
        at = wbuf.at[lax.rem(sib + 2 * (NY - j), NDP), xa(NX - k)]
        return send(at, at, ws_s.at[k, j], ws_r.at[k, j], {"dp": sib})

    def columns(at):
        return pl.ds(pl.multiple_of(at * PART, PART), PART)

    def key_rows(at):
        return pl.ds(pl.multiple_of(at * CTX, 128), CTX)

    def kx(k):
        return send(keys.at[:, columns(xa(k))], kraw.at[x], k_s.at[k], k_r.at[k], xdev(k))

    def kx_in(k):
        at = kraw.at[xa(NX - k)]
        return send(at, at, k_s.at[k], k_r.at[k], xdev(k))

    def vx(k):
        return send(
            values.at[:, columns(xa(k))], vall.at[key_rows(x)], v_s.at[k], v_r.at[k], xdev(k)
        )

    def vx_in(k):
        at = vall.at[key_rows(xa(NX - k))]
        return send(at, at, v_s.at[k], v_r.at[k], xdev(k))

    def qz(k):
        return send(qpk, qrecv.at[z], q_s.at[k], q_r.at[k], zdev(k))

    def qz_in(k):
        at = qrecv.at[za(NZ - k)]
        return send(at, at, q_s.at[k], q_r.at[k], zdev(k))

    def cz(k):
        return send(kvs.at[za(k)], kvrecv.at[z], c_s.at[k], c_r.at[k], zdev(k))

    def cz_in(k):
        at = kvrecv.at[za(NZ - k)]
        return send(at, at, c_s.at[k], c_r.at[k], zdev(k))

    def stx(k):
        return send(stat.at[x], stat.at[x], st_s.at[k], st_r.at[k], xdev(k))

    def stx_in(k):
        at = stat.at[xa(NX - k)]
        return send(at, at, st_s.at[k], st_r.at[k], xdev(k))

    def fx(k):
        return send(kf.at[xa(k)], frecv.at[x], f_s.at[k], f_r.at[k], xdev(k))

    def fx_in(k):
        at = frecv.at[xa(NX - k)]
        return send(at, at, f_s.at[k], f_r.at[k], xdev(k))

    def oex(k):
        return send(obuf.at[za(k)], orecv.at[z], o_s.at[k], o_r.at[k], zdev(k))

    def oex_in(k):
        at = orecv.at[za(NZ - k)]
        return send(at, at, o_s.at[k], o_r.at[k], zdev(k))

    def tex(k):
        return send(obst.at[za(k)], strecv.at[z], t_s.at[k], t_r.at[k], zdev(k))

    def tex_in(k):
        at = strecv.at[za(NZ - k)]
        return send(at, at, t_s.at[k], t_r.at[k], zdev(k))

    def yx(k):
        return send(ysend.at[xa(k)], yrecv.at[x], y_s.at[k], y_r.at[k], xdev(k))

    def yx_in(k):
        at = yrecv.at[xa(NX - k)]
        return send(at, at, y_s.at[k], y_r.at[k], xdev(k))

    def nz(k):
        return send(hn, hbuf.at[z], n_s.at[k], n_r.at[k], zdev(k))

    def nz_in(k):
        at = hbuf.at[za(NZ - k)]
        return send(at, at, n_s.at[k], n_r.at[k], zdev(k))

    def dz(k):
        return send(dsend.at[za(k)], drecv.at[z], d_s.at[k], d_r.at[k], zdev(k))

    def dz_in(k):
        at = drecv.at[za(NZ - k)]
        return send(at, at, d_s.at[k], d_r.at[k], zdev(k))

    own_copies = [
        pltpu.make_async_copy(hidden, hid.at[z * NX + x], loc.at[0]),
        pltpu.make_async_copy(w4, w4buf.at[dp], loc.at[1]),
        pltpu.make_async_copy(wo, wobuf.at[dp, z], loc.at[2]),
        pltpu.make_async_copy(wm, wbuf.at[dp, x], loc.at[3]),
        pltpu.make_async_copy(keys.at[:, columns(x)], kraw.at[x], loc.at[4]),
        pltpu.make_async_copy(values.at[:, columns(x)], vall.at[key_rows(x)], loc.at[5]),
    ]
    for copy in own_copies:
        copy.start()

    barrier = pltpu.get_barrier_semaphore()

    def greet(dev):
        pl.semaphore_signal(barrier, inc=1, device_id=dev, device_id_type=MESH)

    each(1, NZ, lambda k: greet(zdev(k)))
    each(1, NX, lambda k: greet(xdev(k)))
    each(1, NDP, lambda k: greet({"dp": da(k)}))
    pl.semaphore_wait(barrier, NZ + NX + NDP - 3)

    own_copies[0].wait()
    each(1, NZ, lambda k: hz(k).start())
    each(1, NX, lambda j: hx(0, j).start())
    each(1, NDP, lambda k: w4c(k).start())
    each(1, NX, lambda k: wx(k).start())
    each(1, NZ, lambda k: oz(k).start())

    def forward(k):
        hz_in(k).wait_recv()
        each(1, NX, lambda j: hx(k, j).start())

    each(1, NZ, forward)
    own_copies[3].wait()
    each(1, NY, lambda j: wy(0, j).start())
    ws(0, 0).start()
    each(1, NX, lambda k: kx(k).start())
    each(1, NX, lambda k: vx(k).start())

    for block in range(NX):
        first = (block * NZ + z) * CTX
        slot = lax.div(first, CH)
        later = lax.min(slot + 1, NCH - 1)
        row = first + lax.broadcasted_iota(jnp.int32, (1, CTX), 1)
        code = jnp.where(
            row < (slot + 1) * CH, sbase[slot] - slot * CH, sbase[later] - (slot + 1) * CH
        ) + row
        hit = jnp.max(
            jnp.where(qmeta[:, 2:3] == row, 1, 0), axis=0, keepdims=True
        )
        kcode[:, block * CTX : (block + 1) * CTX] = jnp.where(hit > 0, DEAD, code)
    kcode[:, CACHED:KEYS] = fcode[pl.ds(z, 1), :]
    kall[CACHED:KEYS, :] = jnp.zeros((KEYS - CACHED, PART), BF16)
    vall[CACHED:KEYS, :] = jnp.zeros((KEYS - CACHED, PART), BF16)

    def arrived(k):
        each(1, NX, lambda j: hx_in(k, j).wait_recv())

    each(0, NZ, arrived)
    own_copies[1].wait()
    each(1, NDP, lambda k: w4_in(k).wait_recv())
    low = lanes(SEL // 2) < HEAD_DIM // 2

    def project(part):
        rows = hid[pl.ds(part * 8, 8)].reshape(128, D)
        got = jnp.dot(rows, w4buf[...].reshape(D, 256), preferred_element_type=F32)
        got = got.astype(BF16)
        kvs[pl.ds(part * 2, 2)] = got[:, :HEAD_DIM].reshape(2, GRP, HEAD_DIM)
        return got[:, HEAD_DIM:]

    for half in range(2):
        first = project(half)
        second = project(half + 2)
        qpk[half * 128 : (half + 1) * 128, :] = jnp.where(
            low[:128], first.astype(F32), second.astype(F32)
        ).astype(BF16)
    each(1, NZ, lambda k: qz(k).start())
    each(1, NZ, lambda k: cz(k).start())
    qrecv[pl.ds(z, 1)] = qpk[...][None]
    kvrecv[pl.ds(z, 1)] = kvs[pl.ds(z, 1)]

    own_copies[2].wait()
    each(1, NZ, lambda k: oz_in(k).wait_recv())
    each(1, NY, lambda k: oy(k).start())
    osib(0).start()

    def weights_on(k):
        wx_in(k).wait_recv()
        each(1, NY, lambda j: wy(k, j).start())
        ws(k, 0).start()

    each(1, NX, weights_on)

    def weights_side(k):
        def one(j):
            wy_in(k, j).wait_recv()
            ws(k, j).start()

        each(1, NY, one)

    each(1, NZ, lambda k: qz_in(k).wait_recv())
    each(1, NZ, lambda k: cz_in(k).wait_recv())
    low_f = lanes(GRP) < HEAD_DIM // 2

    def q_head(h):
        a = qrecv[2 * h].astype(F32)
        b = qrecv[2 * h + 1].astype(F32)
        top = jnp.where(low, a, pltpu.roll(b, 64, 1))
        bottom = jnp.where(low, pltpu.roll(a, 64, 1), b)
        return top, bottom

    def f_head(h):
        a = kvrecv[2 * h].astype(F32)
        b = kvrecv[2 * h + 1].astype(F32)
        return jnp.where(low_f, a, pltpu.roll(b, 64, 1)), jnp.where(low_f, pltpu.roll(a, 64, 1), b)

    sq[...] = jnp.zeros_like(sq)
    for h in range(HEADS):
        top, bottom = q_head(h)
        sq[: SEL // 2] += top * top
        sq[SEL // 2 : SEL] += bottom * bottom
        key, value = f_head(h)
        sq[SEL : SEL + GRP] += key * key
        vall[CACHED : CACHED + GRP, h * HEAD_DIM : (h + 1) * HEAD_DIM] = value.astype(BF16)
    stat[pl.ds(x, 1)] = lax.dot_general(
        jnp.ones((8, HEAD_DIM), F32), sq[...], (((1,), (1,)), ((), ())),
        precision=HIGH, preferred_element_type=F32,
    )[None]
    each(1, NX, lambda k: stx(k).start())
    each(1, NX, lambda k: stx_in(k).wait_recv())
    total = stat[0] + stat[1] + stat[2] + stat[3]
    factor = lax.rsqrt(total * (1.0 / D) + EPSILON)
    sq[...] = lax.dot_general(
        factor, jnp.full((8, HEAD_DIM), 0.125, F32), (((0,), (0,)), ((), ())),
        precision=HIGH, preferred_element_type=F32,
    )
    grp_rows = pl.ds(pl.multiple_of(z * GRP, GRP), GRP)
    for h in range(HEADS):
        cols = pl.ds(pl.multiple_of(x * PART + h * HEAD_DIM, HEAD_DIM), HEAD_DIM)
        top, bottom = q_head(h)
        gain = gains[0:1, cols]
        for part, rows in ((top, slice(0, SEL // 2)), (bottom, slice(SEL // 2, SEL))):
            v = part * sq[rows] * gain
            qh[h, rows] = (v * qcos[rows] + pltpu.roll(v, 64, 1) * qsin[rows]).astype(BF16)
        key, _ = f_head(h)
        v = key * sq[SEL : SEL + GRP] * gains[1:2, cols]
        v = (v * qcos[grp_rows] + pltpu.roll(v, 64, 1) * qsin[grp_rows]).astype(BF16)
        kall[CACHED : CACHED + GRP, h * HEAD_DIM : (h + 1) * HEAD_DIM] = v
        kf[:, :, h * HEAD_DIM : (h + 1) * HEAD_DIM] = v.reshape(NX, OWN, HEAD_DIM)
    each(1, NX, lambda k: fx(k).start())
    frecv[pl.ds(x, 1)] = kf[pl.ds(x, 1)]
    weights_side(0)

    own_copies[4].wait()
    each(1, NX, lambda k: kx_in(k).wait_recv())

    def turn(block):
        first = (block * NZ + z) * CTX
        slot = lax.div(first, CH)
        later = lax.min(slot + 1, NCH - 1)
        row = first + lax.broadcasted_iota(jnp.int32, (CTX, HEAD_DIM), 0)
        here = row < (slot + 1) * CH
        cosine = jnp.where(here, scos[pl.ds(slot, 1), :], scos[pl.ds(later, 1), :])
        sine = jnp.where(here, ssin[pl.ds(slot, 1), :], ssin[pl.ds(later, 1), :])
        for h in range(HEADS):
            cols = slice(h * HEAD_DIM, (h + 1) * HEAD_DIM)
            v = kraw[block, :, cols].astype(F32)
            kall[key_rows(block), cols] = (v * cosine + pltpu.roll(v, 64, 1) * sine).astype(BF16)

    each(0, NX, turn)
    own_copies[5].wait()
    each(1, NX, lambda k: vx_in(k).wait_recv())

    obst[...] = jnp.zeros_like(obst)
    lane = lanes(128)

    def attend(step):
        h = lax.div(step, SEL // 128)
        part = lax.rem(step, SEL // 128)
        rows = pl.ds(pl.multiple_of(part * 128, 128), 128)
        cols = pl.ds(pl.multiple_of(h * HEAD_DIM, HEAD_DIM), HEAD_DIM)
        scores = lax.dot_general(
            qh[h, rows], kall[:, cols], (((1,), (1,)), ((), ())), preferred_element_type=F32
        )
        code = kcode[...]
        usable = (code <= qmeta[rows, 0:1]) & (code >= qmeta[rows, 1:2])
        scores = jnp.where(usable, scores * SCORE, NEGATIVE)
        most = jnp.maximum(jnp.max(scores, axis=1, keepdims=True), FLOOR)
        weight = jnp.exp2(scores - most)
        mass = jnp.sum(weight, axis=1, keepdims=True)
        mixed = jnp.dot(weight.astype(BF16), vall[:, cols], preferred_element_type=F32)
        two = pl.ds(part * 2, 2)
        obuf[two, :, cols] = mixed.astype(BF16).reshape(2, GRP, HEAD_DIM)
        old = obst[two].reshape(128, HEAD_DIM)
        new = jnp.where(lane == h, most, jnp.where(lane == h + HEADS, mass, old))
        obst[two] = new.reshape(2, GRP, HEAD_DIM)

    each(0, HEADS * (SEL // 128), attend)
    each(1, NZ, lambda k: tex(k).start())
    each(1, NZ, lambda k: oex(k).start())
    orecv[pl.ds(z, 1)] = obuf[pl.ds(z, 1)]
    strecv[pl.ds(z, 1)] = obst[pl.ds(z, 1)]
    each(1, NY, lambda k: oy_in(k).wait_recv())
    each(1, NY, lambda k: osib(k).start())
    weights_side(1)
    each(1, NZ, lambda k: tex_in(k).wait_recv())
    each(1, NZ, lambda k: oex_in(k).wait_recv())
    peak = strecv[0]
    for p in range(1, NZ):
        peak = jnp.maximum(peak, strecv[p])
    mass = jnp.zeros((GRP, HEAD_DIM), F32)
    for p in range(NZ):
        mass += jnp.exp2(strecv[p] - peak) * pltpu.roll(strecv[p], HEAD_DIM - HEADS, 1)
    valid = lanes(GRP) < HEADS
    inverse = 1.0 / jnp.where(valid, mass, 1.0)
    heads = [jnp.zeros((GRP, HEAD_DIM), F32) for _ in range(HEADS)]
    for p in range(NZ):
        share = jnp.exp2(strecv[p] - peak) * inverse
        for h in range(HEADS):
            part = orecv[p, :, h * HEAD_DIM : (h + 1) * HEAD_DIM].astype(F32)
            heads[h] += part * share[:, h : h + 1]
    attn = jnp.concatenate(heads, axis=1).astype(BF16)
    each(0, NY, lambda k: osib_in(k).wait_recv())

    def out_block(c):
        got = jnp.dot(attn, wobuf[c].reshape(PART, 256), preferred_element_type=F32)
        cols = pl.ds(pl.multiple_of(c * 256, 256), 256)
        ysend[:, :, cols] = got.astype(BF16).reshape(NX, OWN, 256)

    each(0, NDP, out_block)
    each(1, NX, lambda k: yx(k).start())
    yrecv[pl.ds(x, 1)] = ysend[pl.ds(x, 1)]
    weights_side(2)
    each(1, NX, lambda k: yx_in(k).wait_recv())
    y = yrecv[0].astype(F32)
    for p in range(1, NX):
        y += yrecv[p].astype(F32)
    y = y * lax.rsqrt(jnp.mean(y * y, axis=1, keepdims=True) + EPSILON) * gains[2:3, :]
    following = (hid[z * NX + x].astype(F32) + y).astype(BF16)
    hn[...] = following
    each(1, NZ, lambda k: nz(k).start())
    hbuf[pl.ds(z, 1)] = following[None]
    weights_side(3)

    each(1, NZ, lambda k: nz_in(k).wait_recv())

    def sides(k):
        each(0, NY, lambda j: ws_in(k, j).wait_recv())

    each(0, NX, sides)

    def gate(c):
        rows = hbuf[...].reshape(NZ * OWN, D)
        g = jnp.dot(rows, wbuf[:, c, 0].reshape(D, 256), preferred_element_type=F32)
        u = jnp.dot(rows, wbuf[:, c, 1].reshape(D, 256), preferred_element_type=F32)
        cols = pl.ds(pl.multiple_of(c * 256, 256), 256)
        act[:, cols] = (jax.nn.silu(g) * u).astype(BF16)

    each(0, NX, gate)

    def down(c):
        got = jnp.dot(act[...], wbuf[c, :, 2].reshape(NX * 256, 256), preferred_element_type=F32)
        cols = pl.ds(pl.multiple_of(c * 256, 256), 256)
        dsend[:, :, cols] = got.astype(BF16).reshape(NZ, OWN, 256)

    each(0, NDP, down)
    each(1, NZ, lambda k: dz(k).start())
    drecv[pl.ds(z, 1)] = dsend[pl.ds(z, 1)]

    each(1, NX, lambda k: fx_in(k).wait_recv())
    for p in range(NX):
        fresh[:, p * PART : (p + 1) * PART] = frecv[p]

    each(1, NZ, lambda k: dz_in(k).wait_recv())
    t = drecv[0].astype(F32)
    for p in range(1, NZ):
        t += drecv[p].astype(F32)
    t = t * lax.rsqrt(jnp.mean(t * t, axis=1, keepdims=True) + EPSILON) * gains[3:4, :]
    out[...] = (hn[...].astype(F32) + t).astype(BF16)

    for copy in (hz, oz, qz, cz, oex, tex, nz, dz):
        each(1, NZ, lambda k, copy=copy: copy(k).wait_send())
    for copy in (wx, kx, vx, stx, fx, yx):
        each(1, NX, lambda k, copy=copy: copy(k).wait_send())
    each(1, NDP, lambda k: w4c(k).wait_send())
    each(1, NY, lambda k: oy(k).wait_send())
    each(0, NY, lambda k: osib(k).wait_send())
    each(0, NZ, lambda k: each(1, NX, lambda j: hx(k, j).wait_send()))
    each(0, NX, lambda k: each(1, NY, lambda j: wy(k, j).wait_send()))
    each(0, NX, lambda k: each(0, NY, lambda j: ws(k, j).wait_send()))


def frequencies(index_float):
    return jnp.exp(index_float * (-2.0 * math.log(THETA) / HEAD_DIM))


def tables(position):
    half = jnp.arange(HEAD_DIM // 2, dtype=jnp.int32).astype(F32)
    angles = position.astype(F32)[:, None] * frequencies(half)[None, :]
    cosine, sine = jnp.cos(angles), jnp.sin(angles)
    return jnp.concatenate([cosine, cosine], axis=1), jnp.concatenate([-sine, sine], axis=1)


def layer(
    hidden_sel, picked, order, lengths, offsets, cache_keys, cache_values, w_qkv, w_out,
    w_gate_up, w_down, gains,
):
    order_row, length_row, offset_row = order[0], lengths[0], offsets[0]
    ends = jnp.cumsum(length_row)
    request = jnp.sum((order_row[:, None] >= ends[None, :]).astype(jnp.int32), axis=1)
    mine = request[:, None] == jnp.arange(REQS, dtype=jnp.int32)[None, :]
    start = jnp.sum(jnp.where(mine, (ends - length_row)[None, :], 0), axis=1)
    shift = jnp.sum(jnp.where(mine, offset_row[None, :], 0), axis=1)
    base = shift + (order_row - start) * CH
    code = request * SPAN + base
    scos, ssin = tables(jnp.pad(base, (0, 16 - NCH)))
    rows = picked[0].reshape(NX, NZ, OWN).transpose(1, 0, 2).reshape(SEL)
    chosen = (rows // CH)[:, None] == jnp.arange(NCH, dtype=jnp.int32)[None, :]
    in_span = rows % CH
    q_code = jnp.sum(jnp.where(chosen, code[None, :], 0), axis=1) + in_span
    q_low = (q_code // SPAN) * SPAN
    qcos, qsin = tables(q_code - q_low)
    qmeta = jnp.stack([q_code, q_low, rows, rows], axis=1)
    fcode = jnp.pad(q_code.reshape(NZ, GRP), ((0, 0), (0, HEAD_DIM - GRP)), constant_values=DEAD)
    w4 = jnp.concatenate([w_qkv[1], w_qkv[2], w_qkv[0], w_qkv[0]], axis=1)
    wm = jnp.concatenate([w_gate_up, w_down[None]], axis=0)

    vmem = pl.BlockSpec(memory_space=pltpu.VMEM)
    far = pl.BlockSpec(memory_space=pl.ANY)
    smem = pl.BlockSpec(memory_space=pltpu.SMEM)
    dma = pltpu.SemaphoreType.DMA
    out, fresh = pl.pallas_call(
        kernel,
        out_shape=(
            jax.ShapeDtypeStruct((OWN, D), BF16),
            jax.ShapeDtypeStruct((OWN, D), BF16),
        ),
        in_specs=[vmem, far, far, far, far, far, vmem, vmem, vmem, vmem, vmem, vmem, vmem, smem],
        out_specs=(vmem, vmem),
        scratch_shapes=[
            pltpu.VMEM((NZ * NX, OWN, D), BF16),
            pltpu.VMEM((NDP, 256, 256), BF16),
            pltpu.VMEM((NDP, NZ, 64, 256), BF16),
            pltpu.VMEM((NDP, NX, 3, 256, 256), BF16),
            pltpu.VMEM((NX, CTX, PART), BF16),
            pltpu.VMEM((KEYS, PART), BF16),
            pltpu.VMEM((KEYS, PART), BF16),
            pltpu.VMEM((1, KEYS), jnp.int32),
            pltpu.VMEM((SEL // 2, HEAD_DIM), BF16),
            pltpu.VMEM((NZ, GRP, HEAD_DIM), BF16),
            pltpu.VMEM((NZ, SEL // 2, HEAD_DIM), BF16),
            pltpu.VMEM((NZ, GRP, HEAD_DIM), BF16),
            pltpu.VMEM((SEL + 128, HEAD_DIM), F32),
            pltpu.VMEM((NX, 8, SEL + 128), F32),
            pltpu.VMEM((HEADS, SEL, HEAD_DIM), BF16),
            pltpu.VMEM((NX, OWN, PART), BF16),
            pltpu.VMEM((NX, OWN, PART), BF16),
            pltpu.VMEM((NZ, GRP, PART), BF16),
            pltpu.VMEM((NZ, GRP, HEAD_DIM), F32),
            pltpu.VMEM((NZ, GRP, PART), BF16),
            pltpu.VMEM((NZ, GRP, HEAD_DIM), F32),
            pltpu.VMEM((NX, OWN, D), BF16),
            pltpu.VMEM((NX, OWN, D), BF16),
            pltpu.VMEM((OWN, D), BF16),
            pltpu.VMEM((NZ, OWN, D), BF16),
            pltpu.VMEM((NZ * OWN, NX * 256), BF16),
            pltpu.VMEM((NZ, OWN, D), BF16),
            pltpu.VMEM((NZ, OWN, D), BF16),
            dma((NZ,)), dma((NZ,)),
            dma((NZ, NX)), dma((NZ, NX)),
            dma((NDP,)), dma((NDP,)),
            dma((NZ,)), dma((NZ,)),
            dma((NY,)), dma((NY,)),
            dma((NY,)), dma((NY,)),
            dma((NX,)), dma((NX,)),
            dma((NX, NY)), dma((NX, NY)),
            dma((NX, NY)), dma((NX, NY)),
            dma((NX,)), dma((NX,)),
            dma((NX,)), dma((NX,)),
            dma((NZ,)), dma((NZ,)),
            dma((NZ,)), dma((NZ,)),
            dma((NX,)), dma((NX,)),
            dma((NX,)), dma((NX,)),
            dma((NZ,)), dma((NZ,)),
            dma((NZ,)), dma((NZ,)),
            dma((NX,)), dma((NX,)),
            dma((NZ,)), dma((NZ,)),
            dma((NZ,)), dma((NZ,)),
            dma((6,)),
        ],
        compiler_params=pltpu.CompilerParams(
            collective_id=0, has_side_effects=True, vmem_limit_bytes=56 << 20
        ),
    )(
        hidden_sel[0], cache_keys[0], cache_values[0], w4, w_out, wm, gains, qmeta, fcode,
        qcos, qsin, scos, ssin, code,
    )
    return (out[None], fresh[None])


def solution(mesh):
    placed = (
        P("dp", "tensor", None),
        P("dp", None),
        P("dp", None),
        P("dp", None),
        P("dp", None),
        P("dp", "tensor", None),
        P("dp", "tensor", None),
        P(None, "dp", "tensor"),
        P("tensor", "dp"),
        P(None, "dp", "tensor"),
        P("tensor", "dp"),
        P(),
    )
    return jax.shard_map(
        layer,
        mesh=mesh,
        in_specs=placed,
        out_specs=(P("dp", "tensor", None), P("dp", "tensor", None)),
        check_vma=False,
    )
```

time: 394 us -> 178 us (0.45)
  Pallas kernels: 0 us -> 161 us
  waiting for transfers between devices: 156 us -> 0 us
  starting transfers between devices: 72.8 us -> 0 us
  blocking collectives: 45 us -> 0 us
  local copies, waits for them, and re-layouts: 45.3 us -> 5.7 us
  other arithmetic: 36.6 us -> 10.1 us
  matrix products: 20.3 us -> 0 us
  between operations: 14.7 us -> 0.74 us
    pallas_call x0 -> x1, Pallas kernels: none -> 161 us  [layer(): pl.pallas_call(kernel, out_shape=(jax.ShapeDtypeStruct((OWN, D), BF16), j...]
    all_to_all x13 -> x0, waiting for transfers between devices: 153 us -> none  [swap(): lax.all_to_all(blocks, 'tensor', split_axis=0, concat_axis=0, axis_index_...]
    all_to_all x13 -> x0, starting transfers between devices: 72.6 us -> none  [swap(): lax.all_to_all(blocks, 'tensor', split_axis=0, concat_axis=0, axis_index_...]
    all_gather x2 -> x0, blocking collectives: 27.3 us -> none  [the longest x1 13.9 us: shards(): qkv_full = lax.all_gather(w_qkv, 'dp', axis=1, tiled=True)]
    dot_general x6 -> x0, matrix products: 20.3 us -> none  [the longest x1 7.61 us: shards(): jnp.einsum('hqk,khd->qhd', weights.astype(bf16), all_values, preferred_el...]
    all_to_all x1 -> x0, blocking collectives: 17.7 us -> none  [swap(): lax.all_to_all(blocks, 'tensor', split_axis=0, concat_axis=0, axis_index_...]
    concatenate x8 -> x0, local copies, waits for them, and re-layouts: 13.2 us -> none  [the longest x4 8.78 us: shards(): cache = jnp.concatenate([cache_keys[0], cache_values[0]], axis=0)]
    broadcast_in_dim x8 -> x0, local copies, waits for them, and re-layouts: 8.61 us -> none  [the longest x6 7.07 us: share(): return swap(jnp.broadcast_to(block[None], (count,) + block.shape), groups)]
  transfers between devices with their start and end apart: 15 -> 0, of which waited for: 12 -> 0; matrix products, arithmetic and copies ran while one was open for 19% -> 0% of each run, Pallas kernels for 0% -> 0%
where the time goes in v2:
time: 178 us
  Pallas kernels  161 us (90%)
  other arithmetic  10.1 us (6%)
  local copies, waits for them, and re-layouts  5.7 us (3%)
    pallas_call x1, Pallas kernels, layer(): pl.pallas_call(kernel, out_shape=(jax.ShapeDtypeStruct((OWN, D), BF16), j...  161 us
    unnamed x14, local copies, waits for them, and re-layouts  3.83 us

profile of v2, /device:TPU:6, one launch (start us, length us, event | category | flops | bytes accessed | tf_op | source)
XLA Modules:
  0.0 177.9 jit_solution(13782878564035059459)
XLA Ops:
  0.6 0.0 copy-start.3
  0.7 0.9 reduce-window.4
  1.5 0.7 convert_reduce_fusion
  2.3 0.7 fusion.17
  2.9 0.7 select_reduce_fusion.2
  3.7 0.7 fusion.18
  4.3 0.5 broadcast.251
  4.8 1.3 reduce.3
  6.2 0.1 reshape_squeeze.3
  6.3 0.1 reshape.204
  6.4 0.1 select_reduce_fusion
  6.5 0.0 copy-start
  6.5 0.0 copy-start.1
  6.5 1.0 fusion
  7.5 1.0 pad_maximum_fusion.1
  8.5 0.6 multiply_add_fusion.1
  9.1 0.1 fusion.3
  9.2 0.7 pad_maximum_fusion.4
  9.9 0.1 reshape.207
  10.0 0.9 copy.37.qmeta
  10.9 0.1 reduce_sum.51
  11.0 0.1 reshape.208
  11.1 0.6 pad.8.fcode
  11.7 0.1 copy.38
  11.8 0.1 copy.39
  11.9 0.1 copy.40
  12.0 0.8 pad_maximum_fusion.3.w4
  12.8 0.0 copy-done
  12.8 0.8 pad_maximum_fusion.wm
  13.6 161.3 %shard_map.131 = (bf16[16,2048]{1,0:T(8,128)(2,1)}, bf16[16,2048]{1,0:T(8,128)(2,1)}) custom-call(bf16[16,2048]{1,0:T(8,128)(2,1)} %bitcast.54, bf16[384,2048]{1,0:T(8,128)(2,1)} %bitcast.45, bf16[384,2048]{1,0:T(8,128)(2,1)} %bitcast.46, bf16[256,256]{1,0:T(8,128)(2,1)} %pad_maximum_fusion.3.w4, bf16[64,256]{1,0:T(8,128)(2,1)} %wo.1, ...), custom_call_target="tpu_custom_call" | custom-call | tf_op jit(solution)/shard_map/pallas_call | solution.py:653
  174.9 1.5 copy.45
  176.4 1.5 copy.46
  (13 shorter events, 0.1 us)
Async XLA Ops:
  0.6 7.9 %copy-start.3 = (s32[1,12]{1,0:T(1,128)S(1)}, s32[1,12]{1,0:T(1,128)}, u32[]{:S(2)}) copy-start(s32[1,12]{1,0:T(1,128)} %param.14) | copy-start | bytes 148
  0.6 11.0 %copy-start.2 = (bf16[3,256,64]{1,2,0:T(8,128)(2,1)S(1)}, bf16[3,256,64]{1,2,0:T(8,128)(2,1)}, u32[]{:S(2)}) copy-start(bf16[3,256,64]{1,2,0:T(8,128)(2,1)} %param.19) | copy-start | bytes 294916
  6.5 6.3 %copy-start = (bf16[2,256,256]{2,1,0:T(8,128)(2,1)S(1)}, bf16[2,256,256]{2,1,0:T(8,128)(2,1)}, u32[]{:S(2)}) copy-start(bf16[2,256,256]{2,1,0:T(8,128)(2,1)} %param.21) | copy-start | bytes 786436
  6.5 6.3 %copy-start.1 = (bf16[256,256]{1,0:T(8,128)(2,1)S(1)}, bf16[256,256]{1,0:T(8,128)(2,1)}, u32[]{:S(2)}) copy-start(bf16[256,256]{1,0:T(8,128)(2,1)} %param.22) | copy-start | bytes 393220

commit v3 on v2

--- a/solution.py
+++ b/solution.py
@@ -66,6 +66,8 @@
     kall,
     vall,
     kcode,
+    psend,
+    precv,
     qpk,
     kvs,
     qrecv,
@@ -76,9 +78,7 @@
     kf,
     frecv,
     obuf,
-    obst,
     orecv,
-    strecv,
     ysend,
     yrecv,
     hn,
@@ -88,26 +88,15 @@
     drecv,
     hz_s,
     hz_r,
-    hx_s,
-    hx_r,
-    w4_s,
-    w4_r,
-    oz_s,
-    oz_r,
-    oy_s,
-    oy_r,
-    os_s,
-    os_r,
-    wx_s,
-    wx_r,
-    wy_s,
-    wy_r,
-    ws_s,
-    ws_r,
+    w4_sems,
+    wo_sems,
+    wm_sems,
     k_s,
     k_r,
     v_s,
     v_r,
+    p_s,
+    p_r,
     q_s,
     q_r,
     c_s,
@@ -118,8 +107,6 @@
     f_r,
     o_s,
     o_r,
-    t_s,
-    t_r,
     y_s,
     y_r,
     n_s,
@@ -141,9 +128,6 @@
     def za(k):
         return lax.rem(z + k, NZ)
 
-    def ya(k):
-        return lax.rem(dp + 2 * k, NDP)
-
     def da(k):
         return lax.rem(dp + k, NDP)
 
@@ -166,73 +150,102 @@
 
         lax.fori_loop(first, last, step, 0)
 
+    class Spread:
+        def __init__(self, sems, slots, source, first, peers, entry, entry_in, at):
+            (self.e_s, self.e_r, self.n_s, self.y_r, self.r_s, self.s_s, self.s_r) = sems
+            self.slots, self.source, self.first, self.peers = slots, source, first, peers
+            self.entry, self.entry_in, self.at = entry, entry_in, at
+
+        def enter(self, k):
+            return send(self.source, self.entry, self.e_s.at[k], self.e_r.at[k], self.first(k))
+
+        def enter_in(self, k):
+            at = self.entry_in(k)
+            return send(at, at, self.e_s.at[k], self.e_r.at[k], self.first(k))
+
+        def near(self, k, j):
+            at = self.at(dp, k)
+            return send(at, at, self.n_s.at[k, j], self.y_r.at[k, j], {"dp": da(2 * j)})
+
+        def near_in(self, k, j):
+            at = self.at(da(NDP - 2 * j), k)
+            return send(at, at, self.n_s.at[k, j], self.y_r.at[k, j], {"dp": da(2 * j)})
+
+        def way(self, k):
+            return 1 + 2 * lax.div(k, self.slots // 2)
+
+        def relay(self, k):
+            j = self.way(k)
+            at = self.at(da(NDP - 2 * j), k)
+            return send(at, at, self.r_s.at[k], self.y_r.at[k, 2], {"dp": da(2 * j)})
+
+        def relay_in(self, k):
+            at = self.at(da(4), k)
+            return send(at, at, self.r_s.at[k], self.y_r.at[k, 2], {"dp": da(2)})
+
+        def side(self, k, j):
+            at = self.at(da(NDP - 2 * j), k)
+            return send(at, at, self.s_s.at[k, j], self.s_r.at[k, j], {"dp": sib})
+
+        def side_in(self, k, j):
+            at = self.at(lax.rem(sib + NDP - 2 * j, NDP), k)
+            return send(at, at, self.s_s.at[k, j], self.s_r.at[k, j], {"dp": sib})
+
+        def start(self):
+            each(1, self.peers, lambda k: self.enter(k).start())
+
+        def go_near(self, k):
+            self.near(k, 1).start()
+            self.near(k, 3).start()
+            self.side(k, 0).start()
+
+        def step_near(self, k):
+            self.near_in(k, 1).wait_recv()
+            self.near_in(k, 3).wait_recv()
+            self.relay(k).start()
+            self.side(k, 1).start()
+            self.side(k, 3).start()
+
+        def step_far(self, k):
+            self.relay_in(k).wait_recv()
+            self.side(k, 2).start()
+
+        def arrive(self):
+            each(0, self.slots, lambda k: each(0, NY, lambda j: self.side_in(k, j).wait_recv()))
+
+        def finish(self):
+            each(1, self.peers, lambda k: self.enter(k).wait_send())
+
+            def one(k):
+                self.near(k, 1).wait_send()
+                self.near(k, 3).wait_send()
+                self.relay(k).wait_send()
+                each(0, NY, lambda j: self.side(k, j).wait_send())
+
+            each(0, self.slots, one)
+
+    def x_slot(buf):
+        return lambda d, k: buf.at[d, xa(NX - k)]
+
+    qkv_w = Spread(
+        w4_sems, NX, w4, xdev, NX, w4buf.at[dp, x], lambda k: w4buf.at[dp, xa(NX - k)],
+        x_slot(w4buf),
+    )
+    ffn_w = Spread(
+        wm_sems, NX, wm, xdev, NX, wbuf.at[dp, x], lambda k: wbuf.at[dp, xa(NX - k)],
+        x_slot(wbuf),
+    )
+    out_w = Spread(
+        wo_sems, 2, wo, zdev, NZ, wobuf.at[dp, z], lambda k: wobuf.at[dp, za(NZ - k)],
+        lambda d, k: wobuf.at[d, pl.ds(4 * k, 4)],
+    )
+
     def hz(k):
-        return send(hidden, hid.at[z * NX + x], hz_s.at[k], hz_r.at[k], zdev(k))
+        return send(hidden, hid.at[z], hz_s.at[k], hz_r.at[k], zdev(k))
 
     def hz_in(k):
-        at = hid.at[za(NZ - k) * NX + x]
+        at = hid.at[za(NZ - k)]
         return send(at, at, hz_s.at[k], hz_r.at[k], zdev(k))
-
-    def hx(k, j):
-        at = hid.at[za(NZ - k) * NX + x]
-        return send(at, at, hx_s.at[k, j], hx_r.at[k, j], xdev(j))
-
-    def hx_in(k, j):
-        at = hid.at[za(NZ - k) * NX + xa(NX - j)]
-        return send(at, at, hx_s.at[k, j], hx_r.at[k, j], xdev(j))
-
-    def w4c(k):
-        return send(w4, w4buf.at[dp], w4_s.at[k], w4_r.at[k], {"dp": da(k)})
-
-    def w4_in(k):
-        at = w4buf.at[da(NDP - k)]
-        return send(at, at, w4_s.at[k], w4_r.at[k], {"dp": da(k)})
-
-    def oz(k):
-        return send(wo, wobuf.at[dp, z], oz_s.at[k], oz_r.at[k], zdev(k))
-
-    def oz_in(k):
-        at = wobuf.at[dp, za(NZ - k)]
-        return send(at, at, oz_s.at[k], oz_r.at[k], zdev(k))
-
-    def oy(k):
-        at = wobuf.at[dp]
-        return send(at, at, oy_s.at[k], oy_r.at[k], {"dp": ya(k)})
-
-    def oy_in(k):
-        at = wobuf.at[ya(NY - k)]
-        return send(at, at, oy_s.at[k], oy_r.at[k], {"dp": ya(k)})
-
-    def osib(k):
-        at = wobuf.at[ya(NY - k)]
-        return send(at, at, os_s.at[k], os_r.at[k], {"dp": sib})
-
-    def osib_in(k):
-        at = wobuf.at[lax.rem(sib + 2 * (NY - k), NDP)]
-        return send(at, at, os_s.at[k], os_r.at[k], {"dp": sib})
-
-    def wx(k):
-        return send(wm, wbuf.at[dp, x], wx_s.at[k], wx_r.at[k], xdev(k))
-
-    def wx_in(k):
-        at = wbuf.at[dp, xa(NX - k)]
-        return send(at, at, wx_s.at[k], wx_r.at[k], xdev(k))
-
-    def wy(k, j):
-        at = wbuf.at[dp, xa(NX - k)]
-        return send(at, at, wy_s.at[k, j], wy_r.at[k, j], {"dp": ya(j)})
-
-    def wy_in(k, j):
-        at = wbuf.at[ya(NY - j), xa(NX - k)]
-        return send(at, at, wy_s.at[k, j], wy_r.at[k, j], {"dp": ya(j)})
-
-    def ws(k, j):
-        at = wbuf.at[ya(NY - j), xa(NX - k)]
-        return send(at, at, ws_s.at[k, j], ws_r.at[k, j], {"dp": sib})
-
-    def ws_in(k, j):
-        at = wbuf.at[lax.rem(sib + 2 * (NY - j), NDP), xa(NX - k)]
-        return send(at, at, ws_s.at[k, j], ws_r.at[k, j], {"dp": sib})
 
     def columns(at):
         return pl.ds(pl.multiple_of(at * PART, PART), PART)
@@ -256,6 +269,13 @@
         at = vall.at[key_rows(xa(NX - k))]
         return send(at, at, v_s.at[k], v_r.at[k], xdev(k))
 
+    def px(k):
+        return send(psend.at[xa(k)], precv.at[x], p_s.at[k], p_r.at[k], xdev(k))
+
+    def px_in(k):
+        at = precv.at[xa(NX - k)]
+        return send(at, at, p_s.at[k], p_r.at[k], xdev(k))
+
     def qz(k):
         return send(qpk, qrecv.at[z], q_s.at[k], q_r.at[k], zdev(k))
 
@@ -291,13 +311,6 @@
         at = orecv.at[za(NZ - k)]
         return send(at, at, o_s.at[k], o_r.at[k], zdev(k))
 
-    def tex(k):
-        return send(obst.at[za(k)], strecv.at[z], t_s.at[k], t_r.at[k], zdev(k))
-
-    def tex_in(k):
-        at = strecv.at[za(NZ - k)]
-        return send(at, at, t_s.at[k], t_r.at[k], zdev(k))
-
     def yx(k):
         return send(ysend.at[xa(k)], yrecv.at[x], y_s.at[k], y_r.at[k], xdev(k))
 
@@ -312,16 +325,18 @@
         at = hbuf.at[za(NZ - k)]
         return send(at, at, n_s.at[k], n_r.at[k], zdev(k))
 
-    def dz(k):
-        return send(dsend.at[za(k)], drecv.at[z], d_s.at[k], d_r.at[k], zdev(k))
-
-    def dz_in(k):
-        at = drecv.at[za(NZ - k)]
-        return send(at, at, d_s.at[k], d_r.at[k], zdev(k))
+    def dz(half, k):
+        return send(
+            dsend.at[half, za(k)], drecv.at[half, z], d_s.at[half, k], d_r.at[half, k], zdev(k)
+        )
+
+    def dz_in(half, k):
+        at = drecv.at[half, za(NZ - k)]
+        return send(at, at, d_s.at[half, k], d_r.at[half, k], zdev(k))
 
     own_copies = [
-        pltpu.make_async_copy(hidden, hid.at[z * NX + x], loc.at[0]),
-        pltpu.make_async_copy(w4, w4buf.at[dp], loc.at[1]),
+        pltpu.make_async_copy(hidden, hid.at[z], loc.at[0]),
+        pltpu.make_async_copy(w4, w4buf.at[dp, x], loc.at[1]),
         pltpu.make_async_copy(wo, wobuf.at[dp, z], loc.at[2]),
         pltpu.make_async_copy(wm, wbuf.at[dp, x], loc.at[3]),
         pltpu.make_async_copy(keys.at[:, columns(x)], kraw.at[x], loc.at[4]),
@@ -337,26 +352,25 @@
 
     each(1, NZ, lambda k: greet(zdev(k)))
     each(1, NX, lambda k: greet(xdev(k)))
-    each(1, NDP, lambda k: greet({"dp": da(k)}))
-    pl.semaphore_wait(barrier, NZ + NX + NDP - 3)
-
-    own_copies[0].wait()
+    greet({"dp": da(2)})
+    greet({"dp": da(6)})
+    greet({"dp": sib})
+    pl.semaphore_wait(barrier, NZ + NX + 1)
+
+    qkv_w.start()
+    own_copies[1].wait()
+    qkv_w.go_near(0)
     each(1, NZ, lambda k: hz(k).start())
-    each(1, NX, lambda j: hx(0, j).start())
-    each(1, NDP, lambda k: w4c(k).start())
-    each(1, NX, lambda k: wx(k).start())
-    each(1, NZ, lambda k: oz(k).start())
-
-    def forward(k):
-        hz_in(k).wait_recv()
-        each(1, NX, lambda j: hx(k, j).start())
-
-    each(1, NZ, forward)
-    own_copies[3].wait()
-    each(1, NY, lambda j: wy(0, j).start())
-    ws(0, 0).start()
+    ffn_w.start()
+
+    def qkv_on(k):
+        qkv_w.enter_in(k).wait_recv()
+        qkv_w.go_near(k)
+
+    each(1, NX, qkv_on)
     each(1, NX, lambda k: kx(k).start())
     each(1, NX, lambda k: vx(k).start())
+    out_w.start()
 
     for block in range(NX):
         first = (block * NZ + z) * CTX
@@ -374,50 +388,55 @@
     kall[CACHED:KEYS, :] = jnp.zeros((KEYS - CACHED, PART), BF16)
     vall[CACHED:KEYS, :] = jnp.zeros((KEYS - CACHED, PART), BF16)
 
-    def arrived(k):
-        each(1, NX, lambda j: hx_in(k, j).wait_recv())
-
-    each(0, NZ, arrived)
-    own_copies[1].wait()
-    each(1, NDP, lambda k: w4_in(k).wait_recv())
+    each(0, NX, qkv_w.step_near)
+    own_copies[2].wait()
+    own_copies[3].wait()
+    each(1, NZ, lambda k: out_w.enter_in(k).wait_recv())
+    each(0, NX, qkv_w.step_far)
+    each(0, 2, out_w.go_near)
+    ffn_w.go_near(0)
+
+    own_copies[0].wait()
+    each(1, NZ, lambda k: hz_in(k).wait_recv())
+    qkv_w.arrive()
+
+    def project(i):
+        k = lax.rem(i + 1, NX)
+        at = xa(k)
+        rows = hid[...].reshape(NZ * OWN, D)
+        got = jnp.dot(rows, w4buf[:, at].reshape(D, 256), preferred_element_type=F32)
+        psend[at] = got.astype(BF16)
+        return k
+
+    def project_send(i):
+        k = project(i)
+        px(k).start()
+
+    each(0, NX - 1, project_send)
+    project(NX - 1)
+    precv[pl.ds(x, 1)] = psend[pl.ds(x, 1)]
+
+    def ffn_on(k):
+        ffn_w.enter_in(k).wait_recv()
+        ffn_w.go_near(k)
+
+    each(1, NX, ffn_on)
+    each(1, NX, lambda k: px_in(k).wait_recv())
     low = lanes(SEL // 2) < HEAD_DIM // 2
-
-    def project(part):
-        rows = hid[pl.ds(part * 8, 8)].reshape(128, D)
-        got = jnp.dot(rows, w4buf[...].reshape(D, 256), preferred_element_type=F32)
-        got = got.astype(BF16)
-        kvs[pl.ds(part * 2, 2)] = got[:, :HEAD_DIM].reshape(2, GRP, HEAD_DIM)
-        return got[:, HEAD_DIM:]
-
-    for half in range(2):
-        first = project(half)
-        second = project(half + 2)
-        qpk[half * 128 : (half + 1) * 128, :] = jnp.where(
-            low[:128], first.astype(F32), second.astype(F32)
-        ).astype(BF16)
+    for g in range(NZ // 2):
+        two = []
+        for gg in (g, g + NZ // 2):
+            rows = jnp.concatenate(
+                [precv[p, gg * OWN : (gg + 1) * OWN] for p in range(NX)], axis=0
+            )
+            kvs[gg] = rows[:, :HEAD_DIM]
+            two.append(rows[:, HEAD_DIM:].astype(F32))
+        qpk[g * GRP : (g + 1) * GRP, :] = jnp.where(low[:GRP], two[0], two[1]).astype(BF16)
     each(1, NZ, lambda k: qz(k).start())
     each(1, NZ, lambda k: cz(k).start())
     qrecv[pl.ds(z, 1)] = qpk[...][None]
     kvrecv[pl.ds(z, 1)] = kvs[pl.ds(z, 1)]
-
-    own_copies[2].wait()
-    each(1, NZ, lambda k: oz_in(k).wait_recv())
-    each(1, NY, lambda k: oy(k).start())
-    osib(0).start()
-
-    def weights_on(k):
-        wx_in(k).wait_recv()
-        each(1, NY, lambda j: wy(k, j).start())
-        ws(k, 0).start()
-
-    each(1, NX, weights_on)
-
-    def weights_side(k):
-        def one(j):
-            wy_in(k, j).wait_recv()
-            ws(k, j).start()
-
-        each(1, NY, one)
+    each(0, 2, out_w.step_near)
 
     each(1, NZ, lambda k: qz_in(k).wait_recv())
     each(1, NZ, lambda k: cz_in(k).wait_recv())
@@ -448,6 +467,7 @@
         precision=HIGH, preferred_element_type=F32,
     )[None]
     each(1, NX, lambda k: stx(k).start())
+    each(0, 2, out_w.step_far)
     each(1, NX, lambda k: stx_in(k).wait_recv())
     total = stat[0] + stat[1] + stat[2] + stat[3]
     factor = lax.rsqrt(total * (1.0 / D) + EPSILON)
@@ -470,7 +490,7 @@
         kf[:, :, h * HEAD_DIM : (h + 1) * HEAD_DIM] = v.reshape(NX, OWN, HEAD_DIM)
     each(1, NX, lambda k: fx(k).start())
     frecv[pl.ds(x, 1)] = kf[pl.ds(x, 1)]
-    weights_side(0)
+    ffn_w.step_near(0)
 
     own_copies[4].wait()
     each(1, NX, lambda k: kx_in(k).wait_recv())
@@ -492,56 +512,72 @@
     own_copies[5].wait()
     each(1, NX, lambda k: vx_in(k).wait_recv())
 
-    obst[...] = jnp.zeros_like(obst)
     lane = lanes(128)
 
-    def attend(step):
-        h = lax.div(step, SEL // 128)
-        part = lax.rem(step, SEL // 128)
+    def attend(part):
         rows = pl.ds(pl.multiple_of(part * 128, 128), 128)
-        cols = pl.ds(pl.multiple_of(h * HEAD_DIM, HEAD_DIM), HEAD_DIM)
-        scores = lax.dot_general(
-            qh[h, rows], kall[:, cols], (((1,), (1,)), ((), ())), preferred_element_type=F32
-        )
-        code = kcode[...]
-        usable = (code <= qmeta[rows, 0:1]) & (code >= qmeta[rows, 1:2])
-        scores = jnp.where(usable, scores * SCORE, NEGATIVE)
-        most = jnp.maximum(jnp.max(scores, axis=1, keepdims=True), FLOOR)
-        weight = jnp.exp2(scores - most)
-        mass = jnp.sum(weight, axis=1, keepdims=True)
-        mixed = jnp.dot(weight.astype(BF16), vall[:, cols], preferred_element_type=F32)
         two = pl.ds(part * 2, 2)
-        obuf[two, :, cols] = mixed.astype(BF16).reshape(2, GRP, HEAD_DIM)
-        old = obst[two].reshape(128, HEAD_DIM)
-        new = jnp.where(lane == h, most, jnp.where(lane == h + HEADS, mass, old))
-        obst[two] = new.reshape(2, GRP, HEAD_DIM)
-
-    each(0, HEADS * (SEL // 128), attend)
-    each(1, NZ, lambda k: tex(k).start())
-    each(1, NZ, lambda k: oex(k).start())
+
+        def head(h, marks):
+            cols = pl.ds(pl.multiple_of(h * HEAD_DIM, HEAD_DIM), HEAD_DIM)
+            scores = lax.dot_general(
+                qh[h, rows], kall[:, cols], (((1,), (1,)), ((), ())), preferred_element_type=F32
+            )
+            code = kcode[...]
+            usable = (code <= qmeta[rows, 0:1]) & (code >= qmeta[rows, 1:2])
+            scores = jnp.where(usable, scores * SCORE, NEGATIVE)
+            most = jnp.maximum(jnp.max(scores, axis=1, keepdims=True), FLOOR)
+            most = most.astype(BF16).astype(F32)
+            weight = jnp.exp2(scores - most)
+            mass = jnp.sum(weight, axis=1, keepdims=True)
+            mixed = jnp.dot(weight.astype(BF16), vall[:, cols], preferred_element_type=F32)
+            obuf[two, :, cols] = mixed.astype(BF16).reshape(2, GRP, HEAD_DIM)
+            high = mass.astype(BF16).astype(F32)
+            marks = jnp.where(lane == h, most, marks)
+            marks = jnp.where(lane == h + HEADS, high, marks)
+            return jnp.where(lane == h + 2 * HEADS, mass - high, marks)
+
+        marks = lax.fori_loop(0, HEADS, head, jnp.zeros((128, HEAD_DIM), F32))
+        obuf[two, :, PART:] = marks.astype(BF16).reshape(2, GRP, HEAD_DIM)
+
+    for turn_at, shift in enumerate((2, 1, 3)):
+        part = lax.rem(lax.div(z, 2) + shift, NZ // 2)
+        attend(part)
+        offset = lax.rem(2 * part + NZ - z, NZ)
+        oex(offset).start()
+        oex(lax.rem(offset + 1, NZ)).start()
+        if turn_at > 0:
+            ffn_w.step_near(turn_at)
+    attend(lax.div(z, 2))
+    beside = lax.rem(NZ + 1 - 2 * lax.rem(z, 2), NZ)
+    oex(beside).start()
     orecv[pl.ds(z, 1)] = obuf[pl.ds(z, 1)]
-    strecv[pl.ds(z, 1)] = obst[pl.ds(z, 1)]
-    each(1, NY, lambda k: oy_in(k).wait_recv())
-    each(1, NY, lambda k: osib(k).start())
-    weights_side(1)
-    each(1, NZ, lambda k: tex_in(k).wait_recv())
+    out_w.arrive()
+    ffn_w.step_near(3)
     each(1, NZ, lambda k: oex_in(k).wait_recv())
-    peak = strecv[0]
+
+    def marks_of(p):
+        return orecv[p, :, PART:].astype(F32)
+
+    peak = marks_of(0)
     for p in range(1, NZ):
-        peak = jnp.maximum(peak, strecv[p])
+        peak = jnp.maximum(peak, marks_of(p))
     mass = jnp.zeros((GRP, HEAD_DIM), F32)
     for p in range(NZ):
-        mass += jnp.exp2(strecv[p] - peak) * pltpu.roll(strecv[p], HEAD_DIM - HEADS, 1)
+        marks = marks_of(p)
+        amount = pltpu.roll(marks, HEAD_DIM - HEADS, 1) + pltpu.roll(
+            marks, HEAD_DIM - 2 * HEADS, 1
+        )
+        mass += jnp.exp2(marks - peak) * amount
     valid = lanes(GRP) < HEADS
     inverse = 1.0 / jnp.where(valid, mass, 1.0)
     heads = [jnp.zeros((GRP, HEAD_DIM), F32) for _ in range(HEADS)]
     for p in range(NZ):
-        share = jnp.exp2(strecv[p] - peak) * inverse
+        share = jnp.exp2(marks_of(p) - peak) * inverse
         for h in range(HEADS):
             part = orecv[p, :, h * HEAD_DIM : (h + 1) * HEAD_DIM].astype(F32)
             heads[h] += part * share[:, h : h + 1]
     attn = jnp.concatenate(heads, axis=1).astype(BF16)
-    each(0, NY, lambda k: osib_in(k).wait_recv())
 
     def out_block(c):
         got = jnp.dot(attn, wobuf[c].reshape(PART, 256), preferred_element_type=F32)
@@ -551,24 +587,19 @@
     each(0, NDP, out_block)
     each(1, NX, lambda k: yx(k).start())
     yrecv[pl.ds(x, 1)] = ysend[pl.ds(x, 1)]
-    weights_side(2)
     each(1, NX, lambda k: yx_in(k).wait_recv())
     y = yrecv[0].astype(F32)
     for p in range(1, NX):
         y += yrecv[p].astype(F32)
     y = y * lax.rsqrt(jnp.mean(y * y, axis=1, keepdims=True) + EPSILON) * gains[2:3, :]
-    following = (hid[z * NX + x].astype(F32) + y).astype(BF16)
+    following = (hid[z].astype(F32) + y).astype(BF16)
     hn[...] = following
     each(1, NZ, lambda k: nz(k).start())
     hbuf[pl.ds(z, 1)] = following[None]
-    weights_side(3)
+    each(0, NX, ffn_w.step_far)
 
     each(1, NZ, lambda k: nz_in(k).wait_recv())
-
-    def sides(k):
-        each(0, NY, lambda j: ws_in(k, j).wait_recv())
-
-    each(0, NX, sides)
+    ffn_w.arrive()
 
     def gate(c):
         rows = hbuf[...].reshape(NZ * OWN, D)
@@ -579,36 +610,42 @@
 
     each(0, NX, gate)
 
-    def down(c):
-        got = jnp.dot(act[...], wbuf[c, :, 2].reshape(NX * 256, 256), preferred_element_type=F32)
-        cols = pl.ds(pl.multiple_of(c * 256, 256), 256)
-        dsend[:, :, cols] = got.astype(BF16).reshape(NZ, OWN, 256)
-
-    each(0, NDP, down)
-    each(1, NZ, lambda k: dz(k).start())
-    drecv[pl.ds(z, 1)] = dsend[pl.ds(z, 1)]
+    def down_half(half):
+        def down(c):
+            weights = wbuf[half * 4 + c, :, 2].reshape(NX * 256, 256)
+            got = jnp.dot(act[...], weights, preferred_element_type=F32)
+            cols = pl.ds(pl.multiple_of(c * 256, 256), 256)
+            dsend[half, :, :, cols] = got.astype(BF16).reshape(NZ, OWN, 256)
+
+        each(0, 4, down)
+        each(1, NZ, lambda k: dz(half, k).start())
+
+    each(0, 2, down_half)
+    for half in range(2):
+        drecv[half, pl.ds(z, 1)] = dsend[half, pl.ds(z, 1)]
 
     each(1, NX, lambda k: fx_in(k).wait_recv())
     for p in range(NX):
         fresh[:, p * PART : (p + 1) * PART] = frecv[p]
 
-    each(1, NZ, lambda k: dz_in(k).wait_recv())
-    t = drecv[0].astype(F32)
-    for p in range(1, NZ):
-        t += drecv[p].astype(F32)
+    each(0, 2, lambda half: each(1, NZ, lambda k: dz_in(half, k).wait_recv()))
+    halves = []
+    for half in range(2):
+        t = drecv[half, 0].astype(F32)
+        for p in range(1, NZ):
+            t += drecv[half, p].astype(F32)
+        halves.append(t)
+    t = jnp.concatenate(halves, axis=1)
     t = t * lax.rsqrt(jnp.mean(t * t, axis=1, keepdims=True) + EPSILON) * gains[3:4, :]
     out[...] = (hn[...].astype(F32) + t).astype(BF16)
 
-    for copy in (hz, oz, qz, cz, oex, tex, nz, dz):
+    for copy in (hz, qz, cz, oex, nz):
         each(1, NZ, lambda k, copy=copy: copy(k).wait_send())
-    for copy in (wx, kx, vx, stx, fx, yx):
+    for copy in (kx, vx, px, stx, fx, yx):
         each(1, NX, lambda k, copy=copy: copy(k).wait_send())
-    each(1, NDP, lambda k: w4c(k).wait_send())
-    each(1, NY, lambda k: oy(k).wait_send())
-    each(0, NY, lambda k: osib(k).wait_send())
-    each(0, NZ, lambda k: each(1, NX, lambda j: hx(k, j).wait_send()))
-    each(0, NX, lambda k: each(1, NY, lambda j: wy(k, j).wait_send()))
-    each(0, NX, lambda k: each(0, NY, lambda j: ws(k, j).wait_send()))
+    each(0, 2, lambda half: each(1, NZ, lambda k: dz(half, k).wait_send()))
+    for weights in (qkv_w, out_w, ffn_w):
+        weights.finish()
 
 
 def frequencies(index_float):
@@ -650,6 +687,13 @@
     far = pl.BlockSpec(memory_space=pl.ANY)
     smem = pl.BlockSpec(memory_space=pltpu.SMEM)
     dma = pltpu.SemaphoreType.DMA
+
+    def spread(peers, slots):
+        return (
+            dma((peers,)), dma((peers,)), dma((slots, NY)), dma((slots, NY)), dma((slots,)),
+            dma((slots, NY)), dma((slots, NY)),
+        )
+
     out, fresh = pl.pallas_call(
         kernel,
         out_shape=(
@@ -659,14 +703,16 @@
         in_specs=[vmem, far, far, far, far, far, vmem, vmem, vmem, vmem, vmem, vmem, vmem, smem],
         out_specs=(vmem, vmem),
         scratch_shapes=[
-            pltpu.VMEM((NZ * NX, OWN, D), BF16),
-            pltpu.VMEM((NDP, 256, 256), BF16),
+            pltpu.VMEM((NZ, OWN, D), BF16),
+            pltpu.VMEM((NDP, NX, 256, 256), BF16),
             pltpu.VMEM((NDP, NZ, 64, 256), BF16),
             pltpu.VMEM((NDP, NX, 3, 256, 256), BF16),
             pltpu.VMEM((NX, CTX, PART), BF16),
             pltpu.VMEM((KEYS, PART), BF16),
             pltpu.VMEM((KEYS, PART), BF16),
             pltpu.VMEM((1, KEYS), jnp.int32),
+            pltpu.VMEM((NX, NZ * OWN, 256), BF16),
+            pltpu.VMEM((NX, NZ * OWN, 256), BF16),
             pltpu.VMEM((SEL // 2, HEAD_DIM), BF16),
             pltpu.VMEM((NZ, GRP, HEAD_DIM), BF16),
             pltpu.VMEM((NZ, SEL // 2, HEAD_DIM), BF16),
@@ -676,26 +722,20 @@
             pltpu.VMEM((HEADS, SEL, HEAD_DIM), BF16),
             pltpu.VMEM((NX, OWN, PART), BF16),
             pltpu.VMEM((NX, OWN, PART), BF16),
-            pltpu.VMEM((NZ, GRP, PART), BF16),
-            pltpu.VMEM((NZ, GRP, HEAD_DIM), F32),
-            pltpu.VMEM((NZ, GRP, PART), BF16),
-            pltpu.VMEM((NZ, GRP, HEAD_DIM), F32),
+            pltpu.VMEM((NZ, GRP, PART + HEAD_DIM), BF16),
+            pltpu.VMEM((NZ, GRP, PART + HEAD_DIM), BF16),
             pltpu.VMEM((NX, OWN, D), BF16),
             pltpu.VMEM((NX, OWN, D), BF16),
             pltpu.VMEM((OWN, D), BF16),
             pltpu.VMEM((NZ, OWN, D), BF16),
             pltpu.VMEM((NZ * OWN, NX * 256), BF16),
-            pltpu.VMEM((NZ, OWN, D), BF16),
-            pltpu.VMEM((NZ, OWN, D), BF16),
+            pltpu.VMEM((2, NZ, OWN, D // 2), BF16),
+            pltpu.VMEM((2, NZ, OWN, D // 2), BF16),
             dma((NZ,)), dma((NZ,)),
-            dma((NZ, NX)), dma((NZ, NX)),
-            dma((NDP,)), dma((NDP,)),
-            dma((NZ,)), dma((NZ,)),
-            dma((NY,)), dma((NY,)),
-            dma((NY,)), dma((NY,)),
+            spread(NX, NX),
+            spread(NZ, 2),
+            spread(NX, NX),
             dma((NX,)), dma((NX,)),
-            dma((NX, NY)), dma((NX, NY)),
-            dma((NX, NY)), dma((NX, NY)),
             dma((NX,)), dma((NX,)),
             dma((NX,)), dma((NX,)),
             dma((NZ,)), dma((NZ,)),
@@ -703,10 +743,9 @@
             dma((NX,)), dma((NX,)),
             dma((NX,)), dma((NX,)),
             dma((NZ,)), dma((NZ,)),
-            dma((NZ,)), dma((NZ,)),
             dma((NX,)), dma((NX,)),
             dma((NZ,)), dma((NZ,)),
-            dma((NZ,)), dma((NZ,)),
+            dma((2, NZ)), dma((2, NZ)),
             dma((6,)),
         ],
         compiler_params=pltpu.CompilerParams(

time: 178 us -> 168 us (0.944); the launches traced: 178 us -> 166 us
  Pallas kernels: 161 us -> 149 us
    pallas_call x1, Pallas kernels: 161 us -> 149 us  [layer(): pl.pallas_call(kernel, out_shape=(jax.ShapeDtypeStruct((OWN, D), BF16), j...]
where the time goes in v3:
time: 168 us; the launch traced here: 166 us
  Pallas kernels  149 us (89%)
  other arithmetic  10.1 us (6%)
  local copies, waits for them, and re-layouts  5.7 us (3%)
    pallas_call x1, Pallas kernels, layer(): pl.pallas_call(kernel, out_shape=(jax.ShapeDtypeStruct((OWN, D), BF16), j...  149 us
    unnamed x14, local copies, waits for them, and re-layouts  3.83 us

profile of v3, /device:TPU:6, one launch (start us, length us, event | category | flops | bytes accessed | tf_op | source)
XLA Modules:
  0.0 166.0 jit_solution(8389718804297264407)
XLA Ops:
  0.6 0.0 copy-start.3
  0.7 0.9 reduce-window.4
  1.5 0.7 convert_reduce_fusion
  2.3 0.7 fusion.17
  2.9 0.7 select_reduce_fusion.2
  3.7 0.7 fusion.18
  4.3 0.5 broadcast.251
  4.8 1.3 reduce.3
  6.2 0.1 reshape_squeeze.3
  6.3 0.1 reshape.204
  6.4 0.1 select_reduce_fusion
  6.5 0.0 copy-start
  6.5 0.0 copy-start.1
  6.5 1.0 fusion
  7.5 1.0 pad_maximum_fusion.1
  8.5 0.6 multiply_add_fusion.1
  9.1 0.1 fusion.3
  9.2 0.7 pad_maximum_fusion.4
  9.9 0.1 reshape.207
  10.0 0.9 copy.37.qmeta
  10.9 0.1 reduce_sum.51
  11.0 0.1 reshape.208
  11.1 0.6 pad.8.fcode
  11.7 0.1 copy.38
  11.8 0.1 copy.39
  11.9 0.1 copy.40
  12.0 0.8 pad_maximum_fusion.3.w4
  12.8 0.0 copy-done
  12.8 0.8 pad_maximum_fusion.wm
  13.6 149.4 %shard_map.131 = (bf16[16,2048]{1,0:T(8,128)(2,1)}, bf16[16,2048]{1,0:T(8,128)(2,1)}) custom-call(bf16[16,2048]{1,0:T(8,128)(2,1)} %bitcast.54, bf16[384,2048]{1,0:T(8,128)(2,1)} %bitcast.45, bf16[384,2048]{1,0:T(8,128)(2,1)} %bitcast.46, bf16[256,256]{1,0:T(8,128)(2,1)} %pad_maximum_fusion.3.w4, bf16[64,256]{1,0:T(8,128)(2,1)} %wo.1, ...), custom_call_target="tpu_custom_call" | custom-call | tf_op jit(solution)/shard_map/pallas_call | solution.py:697
  163.0 1.5 copy.45
  164.5 1.5 copy.46
  (13 shorter events, 0.1 us)
Async XLA Ops:
  0.6 7.9 %copy-start.3 = (s32[1,12]{1,0:T(1,128)S(1)}, s32[1,12]{1,0:T(1,128)}, u32[]{:S(2)}) copy-start(s32[1,12]{1,0:T(1,128)} %param.14) | copy-start | bytes 148
  0.6 11.0 %copy-start.2 = (bf16[3,256,64]{1,2,0:T(8,128)(2,1)S(1)}, bf16[3,256,64]{1,2,0:T(8,128)(2,1)}, u32[]{:S(2)}) copy-start(bf16[3,256,64]{1,2,0:T(8,128)(2,1)} %param.19) | copy-start | bytes 294916
  6.5 6.3 %copy-start = (bf16[2,256,256]{2,1,0:T(8,128)(2,1)S(1)}, bf16[2,256,256]{2,1,0:T(8,128)(2,1)}, u32[]{:S(2)}) copy-start(bf16[2,256,256]{2,1,0:T(8,128)(2,1)} %param.21) | copy-start | bytes 786436
  6.5 6.3 %copy-start.1 = (bf16[256,256]{1,0:T(8,128)(2,1)S(1)}, bf16[256,256]{1,0:T(8,128)(2,1)}, u32[]{:S(2)}) copy-start(bf16[256,256]{1,0:T(8,128)(2,1)} %param.22) | copy-start | bytes 393220

commit v4 on v3

--- a/solution.py
+++ b/solution.py
@@ -2,6 +2,7 @@
 
 import jax
 import jax.numpy as jnp
+import numpy as np
 from jax import lax
 from jax.experimental import pallas as pl
 from jax.experimental.pallas import tpu as pltpu
@@ -32,6 +33,9 @@
 NEGATIVE = -1e30
 FLOOR = -1e20
 SCORE = HEAD_DIM ** (-0.5) * math.log2(math.e)
+LAP_A = 6.28125
+LAP_B = 0.0019340515136718750
+LAP_C = 2.0 * math.pi - LAP_A - LAP_B
 MESH = pl.DeviceIdType.MESH
 F32, BF16 = jnp.float32, jnp.bfloat16
 HIGH = lax.Precision.HIGHEST
@@ -47,15 +51,14 @@
     values,
     w4,
     wo,
-    wm,
+    wgu,
+    wd,
     gains,
-    qmeta,
-    fcode,
-    qcos,
-    qsin,
-    scos,
-    ssin,
-    sbase,
+    picked,
+    rates,
+    order,
+    lengths,
+    offsets,
     out,
     fresh,
     hid,
@@ -86,6 +89,16 @@
     act,
     dsend,
     drecv,
+    natural,
+    rows_of,
+    codes,
+    lows,
+    qcos,
+    qsin,
+    scos,
+    ssin,
+    sbase,
+    bias,
     hz_s,
     hz_r,
     w4_sems,
@@ -232,7 +245,7 @@
         x_slot(w4buf),
     )
     ffn_w = Spread(
-        wm_sems, NX, wm, xdev, NX, wbuf.at[dp, x], lambda k: wbuf.at[dp, xa(NX - k)],
+        wm_sems, NX, wbuf.at[dp, x], xdev, NX, wbuf.at[dp, x], lambda k: wbuf.at[dp, xa(NX - k)],
         x_slot(wbuf),
     )
     out_w = Spread(
@@ -338,9 +351,10 @@
         pltpu.make_async_copy(hidden, hid.at[z], loc.at[0]),
         pltpu.make_async_copy(w4, w4buf.at[dp, x], loc.at[1]),
         pltpu.make_async_copy(wo, wobuf.at[dp, z], loc.at[2]),
-        pltpu.make_async_copy(wm, wbuf.at[dp, x], loc.at[3]),
+        pltpu.make_async_copy(wgu, wbuf.at[dp, x, pl.ds(0, 2)], loc.at[3]),
         pltpu.make_async_copy(keys.at[:, columns(x)], kraw.at[x], loc.at[4]),
         pltpu.make_async_copy(values.at[:, columns(x)], vall.at[key_rows(x)], loc.at[5]),
+        pltpu.make_async_copy(wd, wbuf.at[dp, x, 2], loc.at[6]),
     ]
     for copy in own_copies:
         copy.start()
@@ -361,36 +375,95 @@
     own_copies[1].wait()
     qkv_w.go_near(0)
     each(1, NZ, lambda k: hz(k).start())
-    ffn_w.start()
+    own_copies[3].wait()
+    own_copies[6].wait()
+    ffn_w.enter(1).start()
+    ffn_w.enter(3).start()
+    each(1, NX, lambda k: kx(k).start())
+    out_w.start()
+
+    end_a = lengths[0, 0]
+    end_b = end_a + lengths[0, 1]
+    span = lax.broadcasted_iota(jnp.int32, (16, HEAD_DIM), 0)
+    turns = jnp.zeros((16, HEAD_DIM), jnp.int32)
+    shifts, bottoms = [], []
+    for slot in range(NCH):
+        place = order[0, slot]
+        second, third = place >= end_a, place >= end_b
+        start = jnp.where(third, end_b, jnp.where(second, end_a, 0))
+        moved = jnp.where(third, offsets[0, 2], jnp.where(second, offsets[0, 1], offsets[0, 0]))
+        bottom = jnp.where(third, 2 * SPAN, jnp.where(second, SPAN, 0))
+        base = moved + (place - start) * CH
+        sbase[slot] = base + bottom - slot * CH
+        shifts.append(base + bottom - slot * CH)
+        bottoms.append(bottom)
+        turns = jnp.where(span == slot, base, turns)
+
+    def circle(position):
+        angle = position.astype(F32) * rates[0:1, :]
+        laps = jnp.floor(angle * (0.5 / math.pi) + 0.5)
+        angle = ((angle - laps * LAP_A) - laps * LAP_B) - laps * LAP_C
+        sine = jnp.sin(angle)
+        left = lax.broadcasted_iota(jnp.int32, position.shape, 1) < HEAD_DIM // 2
+        return jnp.cos(angle), jnp.where(left, -sine, sine)
+
+    scos[...], ssin[...] = circle(turns)
 
     def qkv_on(k):
         qkv_w.enter_in(k).wait_recv()
         qkv_w.go_near(k)
 
     each(1, NX, qkv_on)
-    each(1, NX, lambda k: kx(k).start())
-    each(1, NX, lambda k: vx(k).start())
-    out_w.start()
+
+    natural[...] = lax.dot_general(
+        jnp.broadcast_to(picked[...].astype(F32), (8, SEL)),
+        jnp.full((8, HEAD_DIM), 0.125, F32), (((0,), (0,)), ((), ())),
+        precision=HIGH, preferred_element_type=F32,
+    )
+    for zz in range(NZ):
+        for xx in range(NX):
+            at = (zz * NX + xx) * OWN
+            back = (xx * NZ + zz) * OWN
+            rows_of[at : at + OWN] = natural[back : back + OWN].astype(jnp.int32)
+
+    def tokens(i):
+        rows = pl.ds(pl.multiple_of(i * 128, 128), 128)
+        row = rows_of[rows]
+        slot_of = lax.shift_right_logical(row, 10)
+        shift = jnp.zeros_like(row)
+        bottom = jnp.zeros_like(row)
+        for slot in range(NCH):
+            mine = slot_of == slot
+            shift = jnp.where(mine, shifts[slot], shift)
+            bottom = jnp.where(mine, bottoms[slot], bottom)
+        codes[rows] = row + shift
+        lows[rows] = bottom
+        qcos[rows], qsin[rows] = circle(row + shift - bottom)
+
+    each(0, SEL // 128, tokens)
+    grp_rows = pl.ds(pl.multiple_of(z * GRP, GRP), GRP)
 
     for block in range(NX):
         first = (block * NZ + z) * CTX
         slot = lax.div(first, CH)
         later = lax.min(slot + 1, NCH - 1)
         row = first + lax.broadcasted_iota(jnp.int32, (1, CTX), 1)
-        code = jnp.where(
-            row < (slot + 1) * CH, sbase[slot] - slot * CH, sbase[later] - (slot + 1) * CH
-        ) + row
+        code = jnp.where(row < (slot + 1) * CH, sbase[slot], sbase[later]) + row
         hit = jnp.max(
-            jnp.where(qmeta[:, 2:3] == row, 1, 0), axis=0, keepdims=True
+            jnp.where(rows_of[:, 0:1] == row, 1, 0), axis=0, keepdims=True
         )
         kcode[:, block * CTX : (block + 1) * CTX] = jnp.where(hit > 0, DEAD, code)
-    kcode[:, CACHED:KEYS] = fcode[pl.ds(z, 1), :]
+    corner = lax.broadcasted_iota(jnp.int32, (GRP, HEAD_DIM), 0) == lanes(GRP)
+    kcode[:, CACHED:KEYS] = jnp.where(
+        lanes(1) < GRP,
+        jnp.sum(jnp.where(corner, codes[grp_rows], 0), axis=0, keepdims=True),
+        DEAD,
+    )
     kall[CACHED:KEYS, :] = jnp.zeros((KEYS - CACHED, PART), BF16)
     vall[CACHED:KEYS, :] = jnp.zeros((KEYS - CACHED, PART), BF16)
 
     each(0, NX, qkv_w.step_near)
     own_copies[2].wait()
-    own_copies[3].wait()
     each(1, NZ, lambda k: out_w.enter_in(k).wait_recv())
     each(0, NX, qkv_w.step_far)
     each(0, 2, out_w.go_near)
@@ -416,11 +489,11 @@
     project(NX - 1)
     precv[pl.ds(x, 1)] = psend[pl.ds(x, 1)]
 
-    def ffn_on(k):
+    each(1, NX, lambda k: vx(k).start())
+    ffn_w.enter(2).start()
+    for k in (1, 3):
         ffn_w.enter_in(k).wait_recv()
         ffn_w.go_near(k)
-
-    each(1, NX, ffn_on)
     each(1, NX, lambda k: px_in(k).wait_recv())
     low = lanes(SEL // 2) < HEAD_DIM // 2
     for g in range(NZ // 2):
@@ -475,13 +548,12 @@
         factor, jnp.full((8, HEAD_DIM), 0.125, F32), (((0,), (0,)), ((), ())),
         precision=HIGH, preferred_element_type=F32,
     )
-    grp_rows = pl.ds(pl.multiple_of(z * GRP, GRP), GRP)
     for h in range(HEADS):
         cols = pl.ds(pl.multiple_of(x * PART + h * HEAD_DIM, HEAD_DIM), HEAD_DIM)
         top, bottom = q_head(h)
         gain = gains[0:1, cols]
         for part, rows in ((top, slice(0, SEL // 2)), (bottom, slice(SEL // 2, SEL))):
-            v = part * sq[rows] * gain
+            v = part * (sq[rows] * SCORE) * gain
             qh[h, rows] = (v * qcos[rows] + pltpu.roll(v, 64, 1) * qsin[rows]).astype(BF16)
         key, _ = f_head(h)
         v = key * sq[SEL : SEL + GRP] * gains[1:2, cols]
@@ -490,7 +562,6 @@
         kf[:, :, h * HEAD_DIM : (h + 1) * HEAD_DIM] = v.reshape(NX, OWN, HEAD_DIM)
     each(1, NX, lambda k: fx(k).start())
     frecv[pl.ds(x, 1)] = kf[pl.ds(x, 1)]
-    ffn_w.step_near(0)
 
     own_copies[4].wait()
     each(1, NX, lambda k: kx_in(k).wait_recv())
@@ -517,15 +588,15 @@
     def attend(part):
         rows = pl.ds(pl.multiple_of(part * 128, 128), 128)
         two = pl.ds(part * 2, 2)
-
-        def head(h, marks):
-            cols = pl.ds(pl.multiple_of(h * HEAD_DIM, HEAD_DIM), HEAD_DIM)
+        code = kcode[...]
+        usable = (code <= codes[rows, 0:1]) & (code >= lows[rows, 0:1])
+        bias[...] = jnp.where(usable, 0.0, NEGATIVE)
+        marks = jnp.zeros((128, HEAD_DIM), F32)
+        for h in range(HEADS):
+            cols = slice(h * HEAD_DIM, (h + 1) * HEAD_DIM)
             scores = lax.dot_general(
                 qh[h, rows], kall[:, cols], (((1,), (1,)), ((), ())), preferred_element_type=F32
-            )
-            code = kcode[...]
-            usable = (code <= qmeta[rows, 0:1]) & (code >= qmeta[rows, 1:2])
-            scores = jnp.where(usable, scores * SCORE, NEGATIVE)
+            ) + bias[...]
             most = jnp.maximum(jnp.max(scores, axis=1, keepdims=True), FLOOR)
             most = most.astype(BF16).astype(F32)
             weight = jnp.exp2(scores - most)
@@ -535,25 +606,25 @@
             high = mass.astype(BF16).astype(F32)
             marks = jnp.where(lane == h, most, marks)
             marks = jnp.where(lane == h + HEADS, high, marks)
-            return jnp.where(lane == h + 2 * HEADS, mass - high, marks)
-
-        marks = lax.fori_loop(0, HEADS, head, jnp.zeros((128, HEAD_DIM), F32))
+            marks = jnp.where(lane == h + 2 * HEADS, mass - high, marks)
         obuf[two, :, PART:] = marks.astype(BF16).reshape(2, GRP, HEAD_DIM)
 
-    for turn_at, shift in enumerate((2, 1, 3)):
-        part = lax.rem(lax.div(z, 2) + shift, NZ // 2)
+    def attend_far(i):
+        part = lax.rem(lax.div(z, 2) + 1 + lax.rem(i + 1, 3), NZ // 2)
         attend(part)
         offset = lax.rem(2 * part + NZ - z, NZ)
         oex(offset).start()
         oex(lax.rem(offset + 1, NZ)).start()
-        if turn_at > 0:
-            ffn_w.step_near(turn_at)
+        ffn_w.step_near(i + lax.div(i, 2))
+
+    each(0, 3, attend_far)
     attend(lax.div(z, 2))
     beside = lax.rem(NZ + 1 - 2 * lax.rem(z, 2), NZ)
     oex(beside).start()
     orecv[pl.ds(z, 1)] = obuf[pl.ds(z, 1)]
+    ffn_w.enter_in(2).wait_recv()
+    ffn_w.go_near(2)
     out_w.arrive()
-    ffn_w.step_near(3)
     each(1, NZ, lambda k: oex_in(k).wait_recv())
 
     def marks_of(p):
@@ -587,6 +658,8 @@
     each(0, NDP, out_block)
     each(1, NX, lambda k: yx(k).start())
     yrecv[pl.ds(x, 1)] = ysend[pl.ds(x, 1)]
+    for k in (0, 1, 3):
+        ffn_w.step_far(k)
     each(1, NX, lambda k: yx_in(k).wait_recv())
     y = yrecv[0].astype(F32)
     for p in range(1, NX):
@@ -596,7 +669,8 @@
     hn[...] = following
     each(1, NZ, lambda k: nz(k).start())
     hbuf[pl.ds(z, 1)] = following[None]
-    each(0, NX, ffn_w.step_far)
+    ffn_w.step_near(2)
+    ffn_w.step_far(2)
 
     each(1, NZ, lambda k: nz_in(k).wait_recv())
     ffn_w.arrive()
@@ -648,40 +722,14 @@
         weights.finish()
 
 
-def frequencies(index_float):
-    return jnp.exp(index_float * (-2.0 * math.log(THETA) / HEAD_DIM))
-
-
-def tables(position):
-    half = jnp.arange(HEAD_DIM // 2, dtype=jnp.int32).astype(F32)
-    angles = position.astype(F32)[:, None] * frequencies(half)[None, :]
-    cosine, sine = jnp.cos(angles), jnp.sin(angles)
-    return jnp.concatenate([cosine, cosine], axis=1), jnp.concatenate([-sine, sine], axis=1)
-
-
 def layer(
     hidden_sel, picked, order, lengths, offsets, cache_keys, cache_values, w_qkv, w_out,
     w_gate_up, w_down, gains,
 ):
-    order_row, length_row, offset_row = order[0], lengths[0], offsets[0]
-    ends = jnp.cumsum(length_row)
-    request = jnp.sum((order_row[:, None] >= ends[None, :]).astype(jnp.int32), axis=1)
-    mine = request[:, None] == jnp.arange(REQS, dtype=jnp.int32)[None, :]
-    start = jnp.sum(jnp.where(mine, (ends - length_row)[None, :], 0), axis=1)
-    shift = jnp.sum(jnp.where(mine, offset_row[None, :], 0), axis=1)
-    base = shift + (order_row - start) * CH
-    code = request * SPAN + base
-    scos, ssin = tables(jnp.pad(base, (0, 16 - NCH)))
-    rows = picked[0].reshape(NX, NZ, OWN).transpose(1, 0, 2).reshape(SEL)
-    chosen = (rows // CH)[:, None] == jnp.arange(NCH, dtype=jnp.int32)[None, :]
-    in_span = rows % CH
-    q_code = jnp.sum(jnp.where(chosen, code[None, :], 0), axis=1) + in_span
-    q_low = (q_code // SPAN) * SPAN
-    qcos, qsin = tables(q_code - q_low)
-    qmeta = jnp.stack([q_code, q_low, rows, rows], axis=1)
-    fcode = jnp.pad(q_code.reshape(NZ, GRP), ((0, 0), (0, HEAD_DIM - GRP)), constant_values=DEAD)
     w4 = jnp.concatenate([w_qkv[1], w_qkv[2], w_qkv[0], w_qkv[0]], axis=1)
-    wm = jnp.concatenate([w_gate_up, w_down[None]], axis=0)
+    half = np.arange(HEAD_DIM // 2, dtype=np.float64)
+    rate = np.exp(half * (-2.0 * math.log(THETA) / HEAD_DIM)).astype(np.float32)
+    rates = jnp.asarray(np.broadcast_to(np.concatenate([rate, rate]), (8, HEAD_DIM)))
 
     vmem = pl.BlockSpec(memory_space=pltpu.VMEM)
     far = pl.BlockSpec(memory_space=pl.ANY)
@@ -700,7 +748,7 @@
             jax.ShapeDtypeStruct((OWN, D), BF16),
             jax.ShapeDtypeStruct((OWN, D), BF16),
         ),
-        in_specs=[vmem, far, far, far, far, far, vmem, vmem, vmem, vmem, vmem, vmem, vmem, smem],
+        in_specs=[vmem, far, far, far, far, far, far, vmem, vmem, vmem, smem, smem, smem],
         out_specs=(vmem, vmem),
         scratch_shapes=[
             pltpu.VMEM((NZ, OWN, D), BF16),
@@ -731,6 +779,16 @@
             pltpu.VMEM((NZ * OWN, NX * 256), BF16),
             pltpu.VMEM((2, NZ, OWN, D // 2), BF16),
             pltpu.VMEM((2, NZ, OWN, D // 2), BF16),
+            pltpu.VMEM((SEL, HEAD_DIM), F32),
+            pltpu.VMEM((SEL, HEAD_DIM), jnp.int32),
+            pltpu.VMEM((SEL, HEAD_DIM), jnp.int32),
+            pltpu.VMEM((SEL, HEAD_DIM), jnp.int32),
+            pltpu.VMEM((SEL, HEAD_DIM), F32),
+            pltpu.VMEM((SEL, HEAD_DIM), F32),
+            pltpu.VMEM((16, HEAD_DIM), F32),
+            pltpu.VMEM((16, HEAD_DIM), F32),
+            pltpu.SMEM((16,), jnp.int32),
+            pltpu.VMEM((128, KEYS), F32),
             dma((NZ,)), dma((NZ,)),
             spread(NX, NX),
             spread(NZ, 2),
@@ -746,14 +804,14 @@
             dma((NX,)), dma((NX,)),
             dma((NZ,)), dma((NZ,)),
             dma((2, NZ)), dma((2, NZ)),
-            dma((6,)),
+            dma((7,)),
         ],
         compiler_params=pltpu.CompilerParams(
             collective_id=0, has_side_effects=True, vmem_limit_bytes=56 << 20
         ),
     )(
-        hidden_sel[0], cache_keys[0], cache_values[0], w4, w_out, wm, gains, qmeta, fcode,
-        qcos, qsin, scos, ssin, code,
+        hidden_sel[0], cache_keys[0], cache_values[0], w4, w_out, w_gate_up, w_down, gains,
+        picked, rates, order, lengths, offsets,
     )
     return (out[None], fresh[None])
 

time: 168 us -> 143 us (0.85)
  the two profiles are of different devices: /device:TPU:6 before, /device:TPU:1 now
where the time goes in v4:
time: 143 us
  Pallas kernels  136 us (95%)
  local copies, waits for them, and re-layouts  5.34 us (4%)
    pallas_call x1, Pallas kernels, layer(): pl.pallas_call(kernel, out_shape=(jax.ShapeDtypeStruct((OWN, D), BF16), j...  136 us
    unnamed x5, local copies, waits for them, and re-layouts  3.29 us

profile of v4, /device:TPU:1, one launch (start us, length us, event | category | flops | bytes accessed | tf_op | source)
XLA Modules:
  0.0 142.6 jit_solution(16810814766878392345)
XLA Ops:
  0.6 0.8 fusion
  1.4 0.1 copy.18
  1.5 0.1 copy.19
  1.7 0.1 copy.20
  1.8 0.8 pad_maximum_fusion.w4
  2.6 1.2 jit_solution_.3.rates
  3.8 135.9 %shard_map.140 = (bf16[16,2048]{1,0:T(8,128)(2,1)}, bf16[16,2048]{1,0:T(8,128)(2,1)}) custom-call(bf16[16,2048]{1,0:T(8,128)(2,1)} %bitcast.13, bf16[384,2048]{1,0:T(8,128)(2,1)} %bitcast.8, bf16[384,2048]{1,0:T(8,128)(2,1)} %bitcast.9, bf16[256,256]{1,0:T(8,128)(2,1)} %pad_maximum_fusion.w4, bf16[64,256]{1,0:T(8,128)(2,1)} %wo.1, bf16[2,256,256]{2,1,0:T(8,128)(2,1)} %wgu.1, ...), custom_call_target="tpu_custom_call" | custom-call | tf_op jit(solution)/shard_map/pallas_call | solution.py:745
  139.7 1.5 %copy.23 = bf16[1,16,2048]{2,1,0:T(8,128)(2,1)} copy(bf16[1,16,2048]{2,1,0:T(8,128)(2,1)} %bitcast.15) | data formatting | bytes 131072
  141.2 1.5 %copy.24 = bf16[1,16,2048]{2,1,0:T(8,128)(2,1)} copy(bf16[1,16,2048]{2,1,0:T(8,128)(2,1)} %bitcast.14) | data formatting | bytes 131072

commit v5 on v4

--- a/solution.py
+++ b/solution.py
@@ -36,6 +36,9 @@
 LAP_A = 6.28125
 LAP_B = 0.0019340515136718750
 LAP_C = 2.0 * math.pi - LAP_A - LAP_B
+RATES = [
+    float(np.float32(math.exp(-2.0 * j / HEAD_DIM * math.log(THETA)))) for j in range(HEAD_DIM // 2)
+]
 MESH = pl.DeviceIdType.MESH
 F32, BF16 = jnp.float32, jnp.bfloat16
 HIGH = lax.Precision.HIGHEST
@@ -55,7 +58,6 @@
     wd,
     gains,
     picked,
-    rates,
     order,
     lengths,
     offsets,
@@ -99,6 +101,7 @@
     ssin,
     sbase,
     bias,
+    squares,
     hz_s,
     hz_r,
     w4_sems,
@@ -399,6 +402,11 @@
         bottoms.append(bottom)
         turns = jnp.where(span == slot, base, turns)
 
+    turn_lane = lax.rem(lanes(8), HEAD_DIM // 2)
+    rates = jnp.zeros((8, HEAD_DIM), F32)
+    for j in range(HEAD_DIM // 2):
+        rates = jnp.where(turn_lane == j, RATES[j], rates)
+
     def circle(position):
         angle = position.astype(F32) * rates[0:1, :]
         laps = jnp.floor(angle * (0.5 / math.pi) + 0.5)
@@ -473,20 +481,46 @@
     each(1, NZ, lambda k: hz_in(k).wait_recv())
     qkv_w.arrive()
 
+    low_x = lanes(NZ * OWN) < HEAD_DIM // 2
+
     def project(i):
         k = lax.rem(i + 1, NX)
         at = xa(k)
         rows = hid[...].reshape(NZ * OWN, D)
-        got = jnp.dot(rows, w4buf[:, at].reshape(D, 256), preferred_element_type=F32)
-        psend[at] = got.astype(BF16)
+        kv = jnp.dot(
+            rows, w4buf[:, at, :256].reshape(D, HEAD_DIM), preferred_element_type=F32
+        )
+        packed = w4buf[:, at, 256:].reshape(D // 2, HEAD_DIM)
+        upper = jnp.concatenate(
+            [rows[:, c * 256 : c * 256 + 128] for c in range(NDP)], axis=1
+        )
+        lower = jnp.concatenate(
+            [rows[:, c * 256 + 128 : (c + 1) * 256] for c in range(NDP)], axis=1
+        )
+        a = jnp.dot(upper, packed, preferred_element_type=F32)
+        b = jnp.dot(lower, packed, preferred_element_type=F32)
+        q = a + pltpu.roll(b, 64, 1)
+        psend[at, :, :HEAD_DIM] = kv.astype(BF16)
+        psend[at, :, HEAD_DIM:] = jnp.where(low_x, q, pltpu.roll(q, 64, 1)).astype(BF16)
+        squares[0] += jnp.where(low_x, q * q, 0.0)
+        squares[1] += jnp.where(low_x, kv * kv, 0.0)
         return k
 
     def project_send(i):
         k = project(i)
         px(k).start()
 
+    squares[...] = jnp.zeros_like(squares)
     each(0, NX - 1, project_send)
     project(NX - 1)
+    lane_own = lanes(OWN)
+    mine = jnp.zeros((OWN, HEAD_DIM), F32)
+    for kind in range(2):
+        sums = jnp.sum(squares[kind], axis=1, keepdims=True)
+        for g in range(NZ):
+            mine = jnp.where(lane_own == 4 * g + 2 * kind, sums[g * OWN : (g + 1) * OWN], mine)
+    stat[pl.ds(x, 1)] = mine[None]
+    each(1, NX, lambda k: stx(k).start())
     precv[pl.ds(x, 1)] = psend[pl.ds(x, 1)]
 
     each(1, NX, lambda k: vx(k).start())
@@ -505,63 +539,17 @@
             kvs[gg] = rows[:, :HEAD_DIM]
             two.append(rows[:, HEAD_DIM:].astype(F32))
         qpk[g * GRP : (g + 1) * GRP, :] = jnp.where(low[:GRP], two[0], two[1]).astype(BF16)
+    each(1, NX, lambda k: stx_in(k).wait_recv())
+    both = stat[0]
+    for p in range(1, NX):
+        both += pltpu.roll(stat[p], 32 * p, 1)
+    high = both.astype(BF16).astype(F32)
+    qpk[SEL // 2 :, :] = (high + pltpu.roll(both - high, 1, 1)).astype(BF16)
     each(1, NZ, lambda k: qz(k).start())
     each(1, NZ, lambda k: cz(k).start())
     qrecv[pl.ds(z, 1)] = qpk[...][None]
     kvrecv[pl.ds(z, 1)] = kvs[pl.ds(z, 1)]
     each(0, 2, out_w.step_near)
-
-    each(1, NZ, lambda k: qz_in(k).wait_recv())
-    each(1, NZ, lambda k: cz_in(k).wait_recv())
-    low_f = lanes(GRP) < HEAD_DIM // 2
-
-    def q_head(h):
-        a = qrecv[2 * h].astype(F32)
-        b = qrecv[2 * h + 1].astype(F32)
-        top = jnp.where(low, a, pltpu.roll(b, 64, 1))
-        bottom = jnp.where(low, pltpu.roll(a, 64, 1), b)
-        return top, bottom
-
-    def f_head(h):
-        a = kvrecv[2 * h].astype(F32)
-        b = kvrecv[2 * h + 1].astype(F32)
-        return jnp.where(low_f, a, pltpu.roll(b, 64, 1)), jnp.where(low_f, pltpu.roll(a, 64, 1), b)
-
-    sq[...] = jnp.zeros_like(sq)
-    for h in range(HEADS):
-        top, bottom = q_head(h)
-        sq[: SEL // 2] += top * top
-        sq[SEL // 2 : SEL] += bottom * bottom
-        key, value = f_head(h)
-        sq[SEL : SEL + GRP] += key * key
-        vall[CACHED : CACHED + GRP, h * HEAD_DIM : (h + 1) * HEAD_DIM] = value.astype(BF16)
-    stat[pl.ds(x, 1)] = lax.dot_general(
-        jnp.ones((8, HEAD_DIM), F32), sq[...], (((1,), (1,)), ((), ())),
-        precision=HIGH, preferred_element_type=F32,
-    )[None]
-    each(1, NX, lambda k: stx(k).start())
-    each(0, 2, out_w.step_far)
-    each(1, NX, lambda k: stx_in(k).wait_recv())
-    total = stat[0] + stat[1] + stat[2] + stat[3]
-    factor = lax.rsqrt(total * (1.0 / D) + EPSILON)
-    sq[...] = lax.dot_general(
-        factor, jnp.full((8, HEAD_DIM), 0.125, F32), (((0,), (0,)), ((), ())),
-        precision=HIGH, preferred_element_type=F32,
-    )
-    for h in range(HEADS):
-        cols = pl.ds(pl.multiple_of(x * PART + h * HEAD_DIM, HEAD_DIM), HEAD_DIM)
-        top, bottom = q_head(h)
-        gain = gains[0:1, cols]
-        for part, rows in ((top, slice(0, SEL // 2)), (bottom, slice(SEL // 2, SEL))):
-            v = part * (sq[rows] * SCORE) * gain
-            qh[h, rows] = (v * qcos[rows] + pltpu.roll(v, 64, 1) * qsin[rows]).astype(BF16)
-        key, _ = f_head(h)
-        v = key * sq[SEL : SEL + GRP] * gains[1:2, cols]
-        v = (v * qcos[grp_rows] + pltpu.roll(v, 64, 1) * qsin[grp_rows]).astype(BF16)
-        kall[CACHED : CACHED + GRP, h * HEAD_DIM : (h + 1) * HEAD_DIM] = v
-        kf[:, :, h * HEAD_DIM : (h + 1) * HEAD_DIM] = v.reshape(NX, OWN, HEAD_DIM)
-    each(1, NX, lambda k: fx(k).start())
-    frecv[pl.ds(x, 1)] = kf[pl.ds(x, 1)]
 
     own_copies[4].wait()
     each(1, NX, lambda k: kx_in(k).wait_recv())
@@ -580,6 +568,61 @@
             kall[key_rows(block), cols] = (v * cosine + pltpu.roll(v, 64, 1) * sine).astype(BF16)
 
     each(0, NX, turn)
+    def mask(i):
+        rows = pl.ds(pl.multiple_of(i * 128, 128), 128)
+        code = kcode[...]
+        usable = (code <= codes[rows, 0:1]) & (code >= lows[rows, 0:1])
+        bias[rows] = jnp.where(usable, 0.0, NEGATIVE)
+
+    each(0, SEL // 128, mask)
+
+    each(1, NZ, lambda k: qz_in(k).wait_recv())
+    each(1, NZ, lambda k: cz_in(k).wait_recv())
+    low_f = lanes(GRP) < HEAD_DIM // 2
+
+    def q_head(h):
+        a = qrecv[2 * h, : SEL // 2].astype(F32)
+        b = qrecv[2 * h + 1, : SEL // 2].astype(F32)
+        top = jnp.where(low, a, pltpu.roll(b, 64, 1))
+        bottom = jnp.where(low, pltpu.roll(a, 64, 1), b)
+        return top, bottom
+
+    def f_head(h):
+        a = kvrecv[2 * h].astype(F32)
+        b = kvrecv[2 * h + 1].astype(F32)
+        return jnp.where(low_f, a, pltpu.roll(b, 64, 1)), jnp.where(low_f, pltpu.roll(a, 64, 1), b)
+
+    each(0, 2, out_w.step_far)
+    total = jnp.zeros((OWN, HEAD_DIM), F32)
+    for p in range(NZ):
+        total += qrecv[p, SEL // 2 :].astype(F32)
+    total = total + pltpu.roll(total, HEAD_DIM - 1, 1)
+    even = lax.rem(lane_own, 2) == 0
+    factor = lax.rsqrt(jnp.where(even, total, 1.0) * (1.0 / D) + EPSILON)
+    for g in range(NZ):
+        for p in range(NX):
+            at = (g * NX + p) * OWN
+            col = 32 * p + 4 * g
+            sq[0, at : at + OWN] = jnp.broadcast_to(
+                factor[:, col : col + 1] * SCORE, (OWN, HEAD_DIM)
+            )
+            sq[1, at : at + OWN] = jnp.broadcast_to(factor[:, col + 2 : col + 3], (OWN, HEAD_DIM))
+    for h in range(HEADS):
+        cols = pl.ds(pl.multiple_of(x * PART + h * HEAD_DIM, HEAD_DIM), HEAD_DIM)
+        top, bottom = q_head(h)
+        gain = gains[0:1, cols]
+        for part, rows in ((top, slice(0, SEL // 2)), (bottom, slice(SEL // 2, SEL))):
+            v = part * sq[0, rows] * gain
+            qh[h, rows] = (v * qcos[rows] + pltpu.roll(v, 64, 1) * qsin[rows]).astype(BF16)
+        key, value = f_head(h)
+        vall[CACHED : CACHED + GRP, h * HEAD_DIM : (h + 1) * HEAD_DIM] = value.astype(BF16)
+        v = key * sq[1, grp_rows] * gains[1:2, cols]
+        v = (v * qcos[grp_rows] + pltpu.roll(v, 64, 1) * qsin[grp_rows]).astype(BF16)
+        kall[CACHED : CACHED + GRP, h * HEAD_DIM : (h + 1) * HEAD_DIM] = v
+        kf[:, :, h * HEAD_DIM : (h + 1) * HEAD_DIM] = v.reshape(NX, OWN, HEAD_DIM)
+    each(1, NX, lambda k: fx(k).start())
+    frecv[pl.ds(x, 1)] = kf[pl.ds(x, 1)]
+
     own_copies[5].wait()
     each(1, NX, lambda k: vx_in(k).wait_recv())
 
@@ -588,26 +631,28 @@
     def attend(part):
         rows = pl.ds(pl.multiple_of(part * 128, 128), 128)
         two = pl.ds(part * 2, 2)
-        code = kcode[...]
-        usable = (code <= codes[rows, 0:1]) & (code >= lows[rows, 0:1])
-        bias[...] = jnp.where(usable, 0.0, NEGATIVE)
         marks = jnp.zeros((128, HEAD_DIM), F32)
         for h in range(HEADS):
             cols = slice(h * HEAD_DIM, (h + 1) * HEAD_DIM)
             scores = lax.dot_general(
                 qh[h, rows], kall[:, cols], (((1,), (1,)), ((), ())), preferred_element_type=F32
-            ) + bias[...]
+            ) + bias[rows]
             most = jnp.maximum(jnp.max(scores, axis=1, keepdims=True), FLOOR)
             most = most.astype(BF16).astype(F32)
             weight = jnp.exp2(scores - most)
             mass = jnp.sum(weight, axis=1, keepdims=True)
             mixed = jnp.dot(weight.astype(BF16), vall[:, cols], preferred_element_type=F32)
-            obuf[two, :, cols] = mixed.astype(BF16).reshape(2, GRP, HEAD_DIM)
+            obuf[two, h * GRP : (h + 1) * GRP, :] = mixed.astype(BF16).reshape(2, GRP, HEAD_DIM)
             high = mass.astype(BF16).astype(F32)
             marks = jnp.where(lane == h, most, marks)
             marks = jnp.where(lane == h + HEADS, high, marks)
             marks = jnp.where(lane == h + 2 * HEADS, mass - high, marks)
-        obuf[two, :, PART:] = marks.astype(BF16).reshape(2, GRP, HEAD_DIM)
+        for side in range(2):
+            packed = marks[side * GRP : side * GRP + OWN]
+            for g in range(1, NX):
+                at = side * GRP + g * OWN
+                packed += pltpu.roll(marks[at : at + OWN], 32 * g, 1)
+            obuf[part * 2 + side, HEADS * GRP :, :] = packed.astype(BF16)
 
     def attend_far(i):
         part = lax.rem(lax.div(z, 2) + 1 + lax.rem(i + 1, 3), NZ // 2)
@@ -628,26 +673,35 @@
     each(1, NZ, lambda k: oex_in(k).wait_recv())
 
     def marks_of(p):
-        return orecv[p, :, PART:].astype(F32)
+        return orecv[p, HEADS * GRP :, :].astype(F32)
 
     peak = marks_of(0)
     for p in range(1, NZ):
         peak = jnp.maximum(peak, marks_of(p))
-    mass = jnp.zeros((GRP, HEAD_DIM), F32)
+    mass = jnp.zeros((OWN, HEAD_DIM), F32)
     for p in range(NZ):
         marks = marks_of(p)
         amount = pltpu.roll(marks, HEAD_DIM - HEADS, 1) + pltpu.roll(
             marks, HEAD_DIM - 2 * HEADS, 1
         )
         mass += jnp.exp2(marks - peak) * amount
-    valid = lanes(GRP) < HEADS
+    valid = lax.rem(lane_own, 32) < HEADS
     inverse = 1.0 / jnp.where(valid, mass, 1.0)
     heads = [jnp.zeros((GRP, HEAD_DIM), F32) for _ in range(HEADS)]
     for p in range(NZ):
         share = jnp.exp2(marks_of(p) - peak) * inverse
         for h in range(HEADS):
-            part = orecv[p, :, h * HEAD_DIM : (h + 1) * HEAD_DIM].astype(F32)
-            heads[h] += part * share[:, h : h + 1]
+            part = orecv[p, h * GRP : (h + 1) * GRP, :].astype(F32)
+            weight = jnp.concatenate(
+                [
+                    jnp.broadcast_to(
+                        share[:, 32 * g + h : 32 * g + h + 1], (OWN, HEAD_DIM)
+                    )
+                    for g in range(NX)
+                ],
+                axis=0,
+            )
+            heads[h] += part * weight
     attn = jnp.concatenate(heads, axis=1).astype(BF16)
 
     def out_block(c):
@@ -726,10 +780,13 @@
     hidden_sel, picked, order, lengths, offsets, cache_keys, cache_values, w_qkv, w_out,
     w_gate_up, w_down, gains,
 ):
-    w4 = jnp.concatenate([w_qkv[1], w_qkv[2], w_qkv[0], w_qkv[0]], axis=1)
-    half = np.arange(HEAD_DIM // 2, dtype=np.float64)
-    rate = np.exp(half * (-2.0 * math.log(THETA) / HEAD_DIM)).astype(np.float32)
-    rates = jnp.asarray(np.broadcast_to(np.concatenate([rate, rate]), (8, HEAD_DIM)))
+    w4 = jnp.concatenate(
+        [
+            jnp.concatenate([w_qkv[1], w_qkv[2]], axis=1),
+            jnp.concatenate([w_qkv[0, :128], w_qkv[0, 128:]], axis=1),
+        ],
+        axis=0,
+    )
 
     vmem = pl.BlockSpec(memory_space=pltpu.VMEM)
     far = pl.BlockSpec(memory_space=pl.ANY)
@@ -748,11 +805,11 @@
             jax.ShapeDtypeStruct((OWN, D), BF16),
             jax.ShapeDtypeStruct((OWN, D), BF16),
         ),
-        in_specs=[vmem, far, far, far, far, far, far, vmem, vmem, vmem, smem, smem, smem],
+        in_specs=[vmem, far, far, far, far, far, far, vmem, vmem, smem, smem, smem],
         out_specs=(vmem, vmem),
         scratch_shapes=[
             pltpu.VMEM((NZ, OWN, D), BF16),
-            pltpu.VMEM((NDP, NX, 256, 256), BF16),
+            pltpu.VMEM((NDP, NX, 384, HEAD_DIM), BF16),
             pltpu.VMEM((NDP, NZ, 64, 256), BF16),
             pltpu.VMEM((NDP, NX, 3, 256, 256), BF16),
             pltpu.VMEM((NX, CTX, PART), BF16),
@@ -761,17 +818,17 @@
             pltpu.VMEM((1, KEYS), jnp.int32),
             pltpu.VMEM((NX, NZ * OWN, 256), BF16),
             pltpu.VMEM((NX, NZ * OWN, 256), BF16),
-            pltpu.VMEM((SEL // 2, HEAD_DIM), BF16),
+            pltpu.VMEM((SEL // 2 + OWN, HEAD_DIM), BF16),
             pltpu.VMEM((NZ, GRP, HEAD_DIM), BF16),
-            pltpu.VMEM((NZ, SEL // 2, HEAD_DIM), BF16),
+            pltpu.VMEM((NZ, SEL // 2 + OWN, HEAD_DIM), BF16),
             pltpu.VMEM((NZ, GRP, HEAD_DIM), BF16),
-            pltpu.VMEM((SEL + 128, HEAD_DIM), F32),
-            pltpu.VMEM((NX, 8, SEL + 128), F32),
+            pltpu.VMEM((2, SEL, HEAD_DIM), F32),
+            pltpu.VMEM((NX, OWN, HEAD_DIM), F32),
             pltpu.VMEM((HEADS, SEL, HEAD_DIM), BF16),
             pltpu.VMEM((NX, OWN, PART), BF16),
             pltpu.VMEM((NX, OWN, PART), BF16),
-            pltpu.VMEM((NZ, GRP, PART + HEAD_DIM), BF16),
-            pltpu.VMEM((NZ, GRP, PART + HEAD_DIM), BF16),
+            pltpu.VMEM((NZ, HEADS * GRP + OWN, HEAD_DIM), BF16),
+            pltpu.VMEM((NZ, HEADS * GRP + OWN, HEAD_DIM), BF16),
             pltpu.VMEM((NX, OWN, D), BF16),
             pltpu.VMEM((NX, OWN, D), BF16),
             pltpu.VMEM((OWN, D), BF16),
@@ -788,7 +845,8 @@
             pltpu.VMEM((16, HEAD_DIM), F32),
             pltpu.VMEM((16, HEAD_DIM), F32),
             pltpu.SMEM((16,), jnp.int32),
-            pltpu.VMEM((128, KEYS), F32),
+            pltpu.VMEM((SEL, KEYS), F32),
+            pltpu.VMEM((2, NZ * OWN, HEAD_DIM), F32),
             dma((NZ,)), dma((NZ,)),
             spread(NX, NX),
             spread(NZ, 2),
@@ -811,7 +869,7 @@
         ),
     )(
         hidden_sel[0], cache_keys[0], cache_values[0], w4, w_out, w_gate_up, w_down, gains,
-        picked, rates, order, lengths, offsets,
+        picked, order, lengths, offsets,
     )
     return (out[None], fresh[None])
 

time: 143 us -> 129 us (0.902)
  the two profiles are of different devices: /device:TPU:1 before, /device:TPU:6 now
where the time goes in v5:
time: 129 us; the launch traced here: 127 us
  Pallas kernels  120 us (93%)
  local copies, waits for them, and re-layouts  4.94 us (4%)
    pallas_call x1, Pallas kernels, layer(): pl.pallas_call(kernel, out_shape=(jax.ShapeDtypeStruct((OWN, D), BF16), j...  120 us
    unnamed x6, local copies, waits for them, and re-layouts  3.41 us

profile of v5, /device:TPU:6, one launch (start us, length us, event | category | flops | bytes accessed | tf_op | source)
XLA Modules:
  0.0 126.7 jit_solution(4894624093049610186)
XLA Ops:
  0.6 0.7 fusion.1
  1.4 0.1 copy.20
  1.5 0.1 copy.21
  1.6 0.8 fusion
  2.4 0.1 copy.18
  2.5 0.1 copy.19
  2.6 0.7 maximum_maximum_fusion.w4
  3.4 120.4 %shard_map.131 = (bf16[16,2048]{1,0:T(8,128)(2,1)}, bf16[16,2048]{1,0:T(8,128)(2,1)}) custom-call(bf16[16,2048]{1,0:T(8,128)(2,1)} %bitcast.15, bf16[384,2048]{1,0:T(8,128)(2,1)} %bitcast.9, bf16[384,2048]{1,0:T(8,128)(2,1)} %bitcast.10, bf16[384,128]{1,0:T(8,128)(2,1)} %maximum_maximum_fusion.w4, bf16[64,256]{1,0:T(8,128)(2,1)} %wo.1, ...), custom_call_target="tpu_custom_call" | custom-call | tf_op jit(solution)/shard_map/pallas_call | solution.py:802
  123.8 1.5 %copy.24 = bf16[1,16,2048]{2,1,0:T(8,128)(2,1)} copy(bf16[1,16,2048]{2,1,0:T(8,128)(2,1)} %bitcast.17) | data formatting | bytes 131072
  125.2 1.5 %copy.25 = bf16[1,16,2048]{2,1,0:T(8,128)(2,1)} copy(bf16[1,16,2048]{2,1,0:T(8,128)(2,1)} %bitcast.16) | data formatting | bytes 131072

commit v6 on v5

--- a/solution.py
+++ b/solution.py
@@ -292,12 +292,13 @@
         at = precv.at[xa(NX - k)]
         return send(at, at, p_s.at[k], p_r.at[k], xdev(k))
 
-    def qz(k):
-        return send(qpk, qrecv.at[z], q_s.at[k], q_r.at[k], zdev(k))
-
-    def qz_in(k):
-        at = qrecv.at[za(NZ - k)]
-        return send(at, at, q_s.at[k], q_r.at[k], zdev(k))
+    def qz(j, k):
+        p = xa(NX - j)
+        return send(qpk.at[p], qrecv.at[z, p], q_s.at[j, k], q_r.at[j, k], zdev(k))
+
+    def qz_in(j, k):
+        at = qrecv.at[za(NZ - k), xa(NX - j)]
+        return send(at, at, q_s.at[j, k], q_r.at[j, k], zdev(k))
 
     def cz(k):
         return send(kvs.at[za(k)], kvrecv.at[z], c_s.at[k], c_r.at[k], zdev(k))
@@ -417,12 +418,6 @@
 
     scos[...], ssin[...] = circle(turns)
 
-    def qkv_on(k):
-        qkv_w.enter_in(k).wait_recv()
-        qkv_w.go_near(k)
-
-    each(1, NX, qkv_on)
-
     natural[...] = lax.dot_general(
         jnp.broadcast_to(picked[...].astype(F32), (8, SEL)),
         jnp.full((8, HEAD_DIM), 0.125, F32), (((0,), (0,)), ((), ())),
@@ -449,26 +444,12 @@
         qcos[rows], qsin[rows] = circle(row + shift - bottom)
 
     each(0, SEL // 128, tokens)
-    grp_rows = pl.ds(pl.multiple_of(z * GRP, GRP), GRP)
-
-    for block in range(NX):
-        first = (block * NZ + z) * CTX
-        slot = lax.div(first, CH)
-        later = lax.min(slot + 1, NCH - 1)
-        row = first + lax.broadcasted_iota(jnp.int32, (1, CTX), 1)
-        code = jnp.where(row < (slot + 1) * CH, sbase[slot], sbase[later]) + row
-        hit = jnp.max(
-            jnp.where(rows_of[:, 0:1] == row, 1, 0), axis=0, keepdims=True
-        )
-        kcode[:, block * CTX : (block + 1) * CTX] = jnp.where(hit > 0, DEAD, code)
-    corner = lax.broadcasted_iota(jnp.int32, (GRP, HEAD_DIM), 0) == lanes(GRP)
-    kcode[:, CACHED:KEYS] = jnp.where(
-        lanes(1) < GRP,
-        jnp.sum(jnp.where(corner, codes[grp_rows], 0), axis=0, keepdims=True),
-        DEAD,
-    )
-    kall[CACHED:KEYS, :] = jnp.zeros((KEYS - CACHED, PART), BF16)
-    vall[CACHED:KEYS, :] = jnp.zeros((KEYS - CACHED, PART), BF16)
+
+    def qkv_on(k):
+        qkv_w.enter_in(k).wait_recv()
+        qkv_w.go_near(k)
+
+    each(1, NX, qkv_on)
 
     each(0, NX, qkv_w.step_near)
     own_copies[2].wait()
@@ -483,8 +464,7 @@
 
     low_x = lanes(NZ * OWN) < HEAD_DIM // 2
 
-    def project(i):
-        k = lax.rem(i + 1, NX)
+    def project(k):
         at = xa(k)
         rows = hid[...].reshape(NZ * OWN, D)
         kv = jnp.dot(
@@ -504,15 +484,26 @@
         psend[at, :, HEAD_DIM:] = jnp.where(low_x, q, pltpu.roll(q, 64, 1)).astype(BF16)
         squares[0] += jnp.where(low_x, q * q, 0.0)
         squares[1] += jnp.where(low_x, kv * kv, 0.0)
-        return k
-
-    def project_send(i):
-        k = project(i)
+
+    low_f = lanes(GRP) < HEAD_DIM // 2
+
+    def take(j, blocks):
+        p = xa(NX - j)
+        rows = blocks[p]
+        q = rows[:, HEAD_DIM:].astype(F32)
+        qpk[p] = jnp.where(low_f, q[:GRP], q[GRP:]).astype(BF16)
+        at = pl.ds(pl.multiple_of(p * OWN, OWN), OWN)
+        kvs[:, at] = rows[:, :HEAD_DIM].reshape(NZ, OWN, HEAD_DIM)
+        each(1, NZ, lambda k: qz(j, k).start())
+
+    def project_send(k):
+        project(k)
         px(k).start()
 
     squares[...] = jnp.zeros_like(squares)
-    each(0, NX - 1, project_send)
-    project(NX - 1)
+    project(0)
+    take(0, psend)
+    each(1, NX, project_send)
     lane_own = lanes(OWN)
     mine = jnp.zeros((OWN, HEAD_DIM), F32)
     for kind in range(2):
@@ -521,35 +512,49 @@
             mine = jnp.where(lane_own == 4 * g + 2 * kind, sums[g * OWN : (g + 1) * OWN], mine)
     stat[pl.ds(x, 1)] = mine[None]
     each(1, NX, lambda k: stx(k).start())
-    precv[pl.ds(x, 1)] = psend[pl.ds(x, 1)]
-
     each(1, NX, lambda k: vx(k).start())
     ffn_w.enter(2).start()
     for k in (1, 3):
         ffn_w.enter_in(k).wait_recv()
         ffn_w.go_near(k)
-    each(1, NX, lambda k: px_in(k).wait_recv())
-    low = lanes(SEL // 2) < HEAD_DIM // 2
-    for g in range(NZ // 2):
-        two = []
-        for gg in (g, g + NZ // 2):
-            rows = jnp.concatenate(
-                [precv[p, gg * OWN : (gg + 1) * OWN] for p in range(NX)], axis=0
-            )
-            kvs[gg] = rows[:, :HEAD_DIM]
-            two.append(rows[:, HEAD_DIM:].astype(F32))
-        qpk[g * GRP : (g + 1) * GRP, :] = jnp.where(low[:GRP], two[0], two[1]).astype(BF16)
+
+    def taken(j):
+        px_in(j).wait_recv()
+        take(j, precv)
+
+    each(1, NX, taken)
     each(1, NX, lambda k: stx_in(k).wait_recv())
     both = stat[0]
     for p in range(1, NX):
         both += pltpu.roll(stat[p], 32 * p, 1)
     high = both.astype(BF16).astype(F32)
-    qpk[SEL // 2 :, :] = (high + pltpu.roll(both - high, 1, 1)).astype(BF16)
-    each(1, NZ, lambda k: qz(k).start())
+    kvs[:, GRP:] = jnp.broadcast_to(
+        (high + pltpu.roll(both - high, 1, 1)).astype(BF16)[None], (NZ, OWN, HEAD_DIM)
+    )
     each(1, NZ, lambda k: cz(k).start())
     qrecv[pl.ds(z, 1)] = qpk[...][None]
     kvrecv[pl.ds(z, 1)] = kvs[pl.ds(z, 1)]
     each(0, 2, out_w.step_near)
+
+    grp_rows = pl.ds(pl.multiple_of(z * GRP, GRP), GRP)
+    for block in range(NX):
+        first = (block * NZ + z) * CTX
+        slot = lax.div(first, CH)
+        later = lax.min(slot + 1, NCH - 1)
+        row = first + lax.broadcasted_iota(jnp.int32, (1, CTX), 1)
+        code = jnp.where(row < (slot + 1) * CH, sbase[slot], sbase[later]) + row
+        hit = jnp.max(
+            jnp.where(rows_of[:, 0:1] == row, 1, 0), axis=0, keepdims=True
+        )
+        kcode[:, block * CTX : (block + 1) * CTX] = jnp.where(hit > 0, DEAD, code)
+    corner = lax.broadcasted_iota(jnp.int32, (GRP, HEAD_DIM), 0) == lanes(GRP)
+    kcode[:, CACHED:KEYS] = jnp.where(
+        lanes(1) < GRP,
+        jnp.sum(jnp.where(corner, codes[grp_rows], 0), axis=0, keepdims=True),
+        DEAD,
+    )
+    kall[CACHED:KEYS, :] = jnp.zeros((KEYS - CACHED, PART), BF16)
+    vall[CACHED:KEYS, :] = jnp.zeros((KEYS - CACHED, PART), BF16)
 
     own_copies[4].wait()
     each(1, NX, lambda k: kx_in(k).wait_recv())
@@ -576,26 +581,36 @@
 
     each(0, SEL // 128, mask)
 
-    each(1, NZ, lambda k: qz_in(k).wait_recv())
+    each(0, NX, lambda j: each(1, NZ, lambda k: qz_in(j, k).wait_recv()))
     each(1, NZ, lambda k: cz_in(k).wait_recv())
-    low_f = lanes(GRP) < HEAD_DIM // 2
+    low = lanes(SEL // 2) < HEAD_DIM // 2
+
+    def in_order(t):
+        return jnp.concatenate(
+            [
+                t[p * GRP + g * OWN : p * GRP + (g + 1) * OWN]
+                for g in range(NZ // 2)
+                for p in range(NX)
+            ],
+            axis=0,
+        )
 
     def q_head(h):
-        a = qrecv[2 * h, : SEL // 2].astype(F32)
-        b = qrecv[2 * h + 1, : SEL // 2].astype(F32)
+        a = qrecv[2 * h].reshape(SEL // 2, HEAD_DIM).astype(F32)
+        b = qrecv[2 * h + 1].reshape(SEL // 2, HEAD_DIM).astype(F32)
         top = jnp.where(low, a, pltpu.roll(b, 64, 1))
         bottom = jnp.where(low, pltpu.roll(a, 64, 1), b)
-        return top, bottom
+        return in_order(top), in_order(bottom)
 
     def f_head(h):
-        a = kvrecv[2 * h].astype(F32)
-        b = kvrecv[2 * h + 1].astype(F32)
+        a = kvrecv[2 * h, :GRP].astype(F32)
+        b = kvrecv[2 * h + 1, :GRP].astype(F32)
         return jnp.where(low_f, a, pltpu.roll(b, 64, 1)), jnp.where(low_f, pltpu.roll(a, 64, 1), b)
 
     each(0, 2, out_w.step_far)
     total = jnp.zeros((OWN, HEAD_DIM), F32)
     for p in range(NZ):
-        total += qrecv[p, SEL // 2 :].astype(F32)
+        total += kvrecv[p, GRP:].astype(F32)
     total = total + pltpu.roll(total, HEAD_DIM - 1, 1)
     even = lax.rem(lane_own, 2) == 0
     factor = lax.rsqrt(jnp.where(even, total, 1.0) * (1.0 / D) + EPSILON)
@@ -662,13 +677,14 @@
         oex(lax.rem(offset + 1, NZ)).start()
         ffn_w.step_near(i + lax.div(i, 2))
 
-    each(0, 3, attend_far)
+    attend_far(0)
+    ffn_w.enter_in(2).wait_recv()
+    ffn_w.go_near(2)
+    each(1, 3, attend_far)
     attend(lax.div(z, 2))
     beside = lax.rem(NZ + 1 - 2 * lax.rem(z, 2), NZ)
     oex(beside).start()
     orecv[pl.ds(z, 1)] = obuf[pl.ds(z, 1)]
-    ffn_w.enter_in(2).wait_recv()
-    ffn_w.go_near(2)
     out_w.arrive()
     each(1, NZ, lambda k: oex_in(k).wait_recv())
 
@@ -712,6 +728,7 @@
     each(0, NDP, out_block)
     each(1, NX, lambda k: yx(k).start())
     yrecv[pl.ds(x, 1)] = ysend[pl.ds(x, 1)]
+    ffn_w.step_near(2)
     for k in (0, 1, 3):
         ffn_w.step_far(k)
     each(1, NX, lambda k: yx_in(k).wait_recv())
@@ -723,7 +740,6 @@
     hn[...] = following
     each(1, NZ, lambda k: nz(k).start())
     hbuf[pl.ds(z, 1)] = following[None]
-    ffn_w.step_near(2)
     ffn_w.step_far(2)
 
     each(1, NZ, lambda k: nz_in(k).wait_recv())
@@ -767,7 +783,8 @@
     t = t * lax.rsqrt(jnp.mean(t * t, axis=1, keepdims=True) + EPSILON) * gains[3:4, :]
     out[...] = (hn[...].astype(F32) + t).astype(BF16)
 
-    for copy in (hz, qz, cz, oex, nz):
+    each(0, NX, lambda j: each(1, NZ, lambda k: qz(j, k).wait_send()))
+    for copy in (hz, cz, oex, nz):
         each(1, NZ, lambda k, copy=copy: copy(k).wait_send())
     for copy in (kx, vx, px, stx, fx, yx):
         each(1, NX, lambda k, copy=copy: copy(k).wait_send())
@@ -818,10 +835,10 @@
             pltpu.VMEM((1, KEYS), jnp.int32),
             pltpu.VMEM((NX, NZ * OWN, 256), BF16),
             pltpu.VMEM((NX, NZ * OWN, 256), BF16),
-            pltpu.VMEM((SEL // 2 + OWN, HEAD_DIM), BF16),
-            pltpu.VMEM((NZ, GRP, HEAD_DIM), BF16),
-            pltpu.VMEM((NZ, SEL // 2 + OWN, HEAD_DIM), BF16),
-            pltpu.VMEM((NZ, GRP, HEAD_DIM), BF16),
+            pltpu.VMEM((NX, GRP, HEAD_DIM), BF16),
+            pltpu.VMEM((NZ, GRP + OWN, HEAD_DIM), BF16),
+            pltpu.VMEM((NZ, NX, GRP, HEAD_DIM), BF16),
+            pltpu.VMEM((NZ, GRP + OWN, HEAD_DIM), BF16),
             pltpu.VMEM((2, SEL, HEAD_DIM), F32),
             pltpu.VMEM((NX, OWN, HEAD_DIM), F32),
             pltpu.VMEM((HEADS, SEL, HEAD_DIM), BF16),
@@ -854,7 +871,7 @@
             dma((NX,)), dma((NX,)),
             dma((NX,)), dma((NX,)),
             dma((NX,)), dma((NX,)),
-            dma((NZ,)), dma((NZ,)),
+            dma((NX, NZ)), dma((NX, NZ)),
             dma((NZ,)), dma((NZ,)),
             dma((NX,)), dma((NX,)),
             dma((NX,)), dma((NX,)),

time: 129 us -> 132 us (1.023); the launches traced: 127 us -> 132 us
  Pallas kernels: 120 us -> 126 us
    pallas_call x1, Pallas kernels: 120 us -> 126 us  [layer(): pl.pallas_call(kernel, out_shape=(jax.ShapeDtypeStruct((OWN, D), BF16), j...]
where the time goes in v6:
time: 132 us
  Pallas kernels  126 us (95%)
  local copies, waits for them, and re-layouts  4.94 us (4%)
    pallas_call x1, Pallas kernels, layer(): pl.pallas_call(kernel, out_shape=(jax.ShapeDtypeStruct((OWN, D), BF16), j...  126 us
    unnamed x6, local copies, waits for them, and re-layouts  3.41 us

profile of v6, /device:TPU:6, one launch (start us, length us, event | category | flops | bytes accessed | tf_op | source)
XLA Modules:
  0.0 131.8 jit_solution(941411048851873810)
XLA Ops:
  0.6 0.7 fusion.1
  1.4 0.1 copy.20
  1.5 0.1 copy.21
  1.6 0.8 fusion
  2.4 0.1 copy.18
  2.5 0.1 copy.19
  2.6 0.7 maximum_maximum_fusion.w4
  3.4 125.5 %shard_map.131 = (bf16[16,2048]{1,0:T(8,128)(2,1)}, bf16[16,2048]{1,0:T(8,128)(2,1)}) custom-call(bf16[16,2048]{1,0:T(8,128)(2,1)} %bitcast.15, bf16[384,2048]{1,0:T(8,128)(2,1)} %bitcast.9, bf16[384,2048]{1,0:T(8,128)(2,1)} %bitcast.10, bf16[384,128]{1,0:T(8,128)(2,1)} %maximum_maximum_fusion.w4, bf16[64,256]{1,0:T(8,128)(2,1)} %wo.1, ...), custom_call_target="tpu_custom_call" | custom-call | tf_op jit(solution)/shard_map/pallas_call | solution.py:819
  128.9 1.5 %copy.24 = bf16[1,16,2048]{2,1,0:T(8,128)(2,1)} copy(bf16[1,16,2048]{2,1,0:T(8,128)(2,1)} %bitcast.17) | data formatting | bytes 131072
  130.4 1.5 %copy.25 = bf16[1,16,2048]{2,1,0:T(8,128)(2,1)} copy(bf16[1,16,2048]{2,1,0:T(8,128)(2,1)} %bitcast.16) | data formatting | bytes 131072

commit v7 on v6

--- a/solution.py
+++ b/solution.py
@@ -61,8 +61,7 @@
     order,
     lengths,
     offsets,
-    out,
-    fresh,
+    both_out,
     hid,
     w4buf,
     wobuf,
@@ -467,22 +466,20 @@
     def project(k):
         at = xa(k)
         rows = hid[...].reshape(NZ * OWN, D)
-        kv = jnp.dot(
-            rows, w4buf[:, at, :256].reshape(D, HEAD_DIM), preferred_element_type=F32
-        )
-        packed = w4buf[:, at, 256:].reshape(D // 2, HEAD_DIM)
-        upper = jnp.concatenate(
-            [rows[:, c * 256 : c * 256 + 128] for c in range(NDP)], axis=1
-        )
-        lower = jnp.concatenate(
-            [rows[:, c * 256 + 128 : (c + 1) * 256] for c in range(NDP)], axis=1
-        )
-        a = jnp.dot(upper, packed, preferred_element_type=F32)
-        b = jnp.dot(lower, packed, preferred_element_type=F32)
-        q = a + pltpu.roll(b, 64, 1)
+        kv = jnp.zeros((NZ * OWN, HEAD_DIM), F32)
+        qk = jnp.zeros((NZ * OWN, HEAD_DIM), F32)
+        for c in range(NDP):
+            left = rows[:, c * 256 : (c + 1) * 256]
+            across = (((1,), (1,)), ((), ()))
+            kv += lax.dot_general(
+                left, w4buf[c, at, 1:].reshape(HEAD_DIM, 256), across, preferred_element_type=F32
+            )
+            qk += lax.dot_general(
+                left, w4buf[c, at, :2].reshape(HEAD_DIM, 256), across, preferred_element_type=F32
+            )
         psend[at, :, :HEAD_DIM] = kv.astype(BF16)
-        psend[at, :, HEAD_DIM:] = jnp.where(low_x, q, pltpu.roll(q, 64, 1)).astype(BF16)
-        squares[0] += jnp.where(low_x, q * q, 0.0)
+        psend[at, :, HEAD_DIM:] = jnp.where(low_x, qk, pltpu.roll(qk, 64, 1)).astype(BF16)
+        squares[0] += jnp.where(low_x, qk * qk, 0.0)
         squares[1] += jnp.where(low_x, kv * kv, 0.0)
 
     low_f = lanes(GRP) < HEAD_DIM // 2
@@ -677,14 +674,13 @@
         oex(lax.rem(offset + 1, NZ)).start()
         ffn_w.step_near(i + lax.div(i, 2))
 
-    attend_far(0)
-    ffn_w.enter_in(2).wait_recv()
-    ffn_w.go_near(2)
-    each(1, 3, attend_far)
+    each(0, 3, attend_far)
     attend(lax.div(z, 2))
     beside = lax.rem(NZ + 1 - 2 * lax.rem(z, 2), NZ)
     oex(beside).start()
     orecv[pl.ds(z, 1)] = obuf[pl.ds(z, 1)]
+    ffn_w.enter_in(2).wait_recv()
+    ffn_w.go_near(2)
     out_w.arrive()
     each(1, NZ, lambda k: oex_in(k).wait_recv())
 
@@ -728,7 +724,6 @@
     each(0, NDP, out_block)
     each(1, NX, lambda k: yx(k).start())
     yrecv[pl.ds(x, 1)] = ysend[pl.ds(x, 1)]
-    ffn_w.step_near(2)
     for k in (0, 1, 3):
         ffn_w.step_far(k)
     each(1, NX, lambda k: yx_in(k).wait_recv())
@@ -740,6 +735,7 @@
     hn[...] = following
     each(1, NZ, lambda k: nz(k).start())
     hbuf[pl.ds(z, 1)] = following[None]
+    ffn_w.step_near(2)
     ffn_w.step_far(2)
 
     each(1, NZ, lambda k: nz_in(k).wait_recv())
@@ -770,7 +766,7 @@
 
     each(1, NX, lambda k: fx_in(k).wait_recv())
     for p in range(NX):
-        fresh[:, p * PART : (p + 1) * PART] = frecv[p]
+        both_out[1, :, p * PART : (p + 1) * PART] = frecv[p]
 
     each(0, 2, lambda half: each(1, NZ, lambda k: dz_in(half, k).wait_recv()))
     halves = []
@@ -781,7 +777,7 @@
         halves.append(t)
     t = jnp.concatenate(halves, axis=1)
     t = t * lax.rsqrt(jnp.mean(t * t, axis=1, keepdims=True) + EPSILON) * gains[3:4, :]
-    out[...] = (hn[...].astype(F32) + t).astype(BF16)
+    both_out[0] = (hn[...].astype(F32) + t).astype(BF16)
 
     each(0, NX, lambda j: each(1, NZ, lambda k: qz(j, k).wait_send()))
     for copy in (hz, cz, oex, nz):
@@ -797,13 +793,7 @@
     hidden_sel, picked, order, lengths, offsets, cache_keys, cache_values, w_qkv, w_out,
     w_gate_up, w_down, gains,
 ):
-    w4 = jnp.concatenate(
-        [
-            jnp.concatenate([w_qkv[1], w_qkv[2]], axis=1),
-            jnp.concatenate([w_qkv[0, :128], w_qkv[0, 128:]], axis=1),
-        ],
-        axis=0,
-    )
+    w4 = w_qkv.transpose(0, 2, 1)
 
     vmem = pl.BlockSpec(memory_space=pltpu.VMEM)
     far = pl.BlockSpec(memory_space=pl.ANY)
@@ -816,17 +806,14 @@
             dma((slots, NY)), dma((slots, NY)),
         )
 
-    out, fresh = pl.pallas_call(
+    both = pl.pallas_call(
         kernel,
-        out_shape=(
-            jax.ShapeDtypeStruct((OWN, D), BF16),
-            jax.ShapeDtypeStruct((OWN, D), BF16),
-        ),
+        out_shape=jax.ShapeDtypeStruct((2, OWN, D), BF16),
         in_specs=[vmem, far, far, far, far, far, far, vmem, vmem, smem, smem, smem],
-        out_specs=(vmem, vmem),
+        out_specs=vmem,
         scratch_shapes=[
             pltpu.VMEM((NZ, OWN, D), BF16),
-            pltpu.VMEM((NDP, NX, 384, HEAD_DIM), BF16),
+            pltpu.VMEM((NDP, NX, 3, 64, 256), BF16),
             pltpu.VMEM((NDP, NZ, 64, 256), BF16),
             pltpu.VMEM((NDP, NX, 3, 256, 256), BF16),
             pltpu.VMEM((NX, CTX, PART), BF16),
@@ -888,7 +875,7 @@
         hidden_sel[0], cache_keys[0], cache_values[0], w4, w_out, w_gate_up, w_down, gains,
         picked, order, lengths, offsets,
     )
-    return (out[None], fresh[None])
+    return (both[:1], both[1:])
 
 
 def solution(mesh):

time: 132 us -> 125 us (0.947)
  Pallas kernels: 126 us -> 122 us
  local copies, waits for them, and re-layouts: 4.94 us -> 1.53 us
    pallas_call x1, Pallas kernels: 126 us -> 122 us  [layer(): pl.pallas_call(kernel, out_shape=jax.ShapeDtypeStruct((2, OWN, D), BF16),...]
    unnamed x6 -> x0, local copies, waits for them, and re-layouts: 3.41 us -> none
where the time goes in v7:
time: 125 us; the launch traced here: 124 us
  Pallas kernels  122 us (98%)
  local copies, waits for them, and re-layouts  1.53 us (1%)
    pallas_call x1, Pallas kernels, layer(): pl.pallas_call(kernel, out_shape=jax.ShapeDtypeStruct((2, OWN, D), BF16),...  122 us

profile of v7, /device:TPU:6, one launch (start us, length us, event | category | flops | bytes accessed | tf_op | source)
XLA Modules:
  0.0 124.2 jit_solution(10377683390400399429)
XLA Ops:
  0.6 122.1 %shard_map.131 = bf16[2,16,2048]{2,1,0:T(8,128)(2,1)} custom-call(bf16[16,2048]{1,0:T(8,128)(2,1)} %bitcast.7, bf16[384,2048]{1,0:T(8,128)(2,1)} %bitcast.4, bf16[384,2048]{1,0:T(8,128)(2,1)} %bitcast.5, bf16[3,64,256]{2,1,0:T(8,128)(2,1)} %bitcast.6, bf16[64,256]{1,0:T(8,128)(2,1)} %wo.1, bf16[2,256,256]{2,1,0:T(8,128)(2,1)} %wgu.1, bf16[256,256]{1,0:T(8,128)(2,1)} %wd.1, ...), custom_call_target="tpu_custom_call" | custom-call | tf_op jit(solution)/shard_map/pallas_call | solution.py:809
  122.7 1.5 %fusion = (bf16[1,16,2048]{2,1,0:T(8,128)(2,1)}, bf16[1,16,2048]{2,1,0:T(8,128)(2,1)}) fusion(bf16[2,16,2048]{2,1,0:T(8,128)(2,1)} %shard_map.131), kind=kLoop, calls=%fused_computation | loop fusion | bytes 262144 | tf_op jit(solution)/shard_map/slice | solution.py:878

commit v8 on v7

--- a/solution.py
+++ b/solution.py
@@ -768,6 +768,14 @@
     for p in range(NX):
         both_out[1, :, p * PART : (p + 1) * PART] = frecv[p]
 
+    each(0, NX, lambda j: each(1, NZ, lambda k: qz(j, k).wait_send()))
+    for copy in (hz, cz, oex, nz):
+        each(1, NZ, lambda k, copy=copy: copy(k).wait_send())
+    for copy in (kx, vx, px, stx, fx, yx):
+        each(1, NX, lambda k, copy=copy: copy(k).wait_send())
+    for weights in (qkv_w, out_w, ffn_w):
+        weights.finish()
+
     each(0, 2, lambda half: each(1, NZ, lambda k: dz_in(half, k).wait_recv()))
     halves = []
     for half in range(2):
@@ -778,15 +786,7 @@
     t = jnp.concatenate(halves, axis=1)
     t = t * lax.rsqrt(jnp.mean(t * t, axis=1, keepdims=True) + EPSILON) * gains[3:4, :]
     both_out[0] = (hn[...].astype(F32) + t).astype(BF16)
-
-    each(0, NX, lambda j: each(1, NZ, lambda k: qz(j, k).wait_send()))
-    for copy in (hz, cz, oex, nz):
-        each(1, NZ, lambda k, copy=copy: copy(k).wait_send())
-    for copy in (kx, vx, px, stx, fx, yx):
-        each(1, NX, lambda k, copy=copy: copy(k).wait_send())
     each(0, 2, lambda half: each(1, NZ, lambda k: dz(half, k).wait_send()))
-    for weights in (qkv_w, out_w, ffn_w):
-        weights.finish()
 
 
 def layer(

time: 125 us -> 124 us (level)
  no operation moved by 1% of the time
where the time goes in v8:
time: 124 us; the launch traced here: 123 us
  Pallas kernels  121 us (98%)
  local copies, waits for them, and re-layouts  1.53 us (1%)
    pallas_call x1, Pallas kernels, layer(): pl.pallas_call(kernel, out_shape=jax.ShapeDtypeStruct((2, OWN, D), BF16),...  121 us

profile of v8, /device:TPU:6, one launch (start us, length us, event | category | flops | bytes accessed | tf_op | source)
XLA Modules:
  0.0 123.3 jit_solution(3355716897824754586)
XLA Ops:
  0.6 121.1 %shard_map.131 = bf16[2,16,2048]{2,1,0:T(8,128)(2,1)} custom-call(bf16[16,2048]{1,0:T(8,128)(2,1)} %bitcast.7, bf16[384,2048]{1,0:T(8,128)(2,1)} %bitcast.4, bf16[384,2048]{1,0:T(8,128)(2,1)} %bitcast.5, bf16[3,64,256]{2,1,0:T(8,128)(2,1)} %bitcast.6, bf16[64,256]{1,0:T(8,128)(2,1)} %wo.1, bf16[2,256,256]{2,1,0:T(8,128)(2,1)} %wgu.1, bf16[256,256]{1,0:T(8,128)(2,1)} %wd.1, ...), custom_call_target="tpu_custom_call" | custom-call | tf_op jit(solution)/shard_map/pallas_call | solution.py:809
  121.8 1.5 %fusion = (bf16[1,16,2048]{2,1,0:T(8,128)(2,1)}, bf16[1,16,2048]{2,1,0:T(8,128)(2,1)}) fusion(bf16[2,16,2048]{2,1,0:T(8,128)(2,1)} %shard_map.131), kind=kLoop, calls=%fused_computation | loop fusion | bytes 262144 | tf_op jit(solution)/shard_map/slice | solution.py:878

commit v9 on v8

--- a/solution.py
+++ b/solution.py
@@ -672,8 +672,12 @@
         offset = lax.rem(2 * part + NZ - z, NZ)
         oex(offset).start()
         oex(lax.rem(offset + 1, NZ)).start()
-        ffn_w.step_near(i + lax.div(i, 2))
-
+
+        @pl.when(i > 0)
+        def _():
+            ffn_w.step_near(2 * i - 1)
+
+    ffn_w.step_near(0)
     each(0, 3, attend_far)
     attend(lax.div(z, 2))
     beside = lax.rem(NZ + 1 - 2 * lax.rem(z, 2), NZ)

time: 124 us -> 124 us (level); the launches traced: 123 us -> 122 us
    pallas_call x1, Pallas kernels: 121 us -> 120 us  [layer(): pl.pallas_call(kernel, out_shape=jax.ShapeDtypeStruct((2, OWN, D), BF16),...]
where the time goes in v9:
time: 124 us; the launch traced here: 122 us
  Pallas kernels  120 us (97%)
  local copies, waits for them, and re-layouts  1.53 us (1%)
    pallas_call x1, Pallas kernels, layer(): pl.pallas_call(kernel, out_shape=jax.ShapeDtypeStruct((2, OWN, D), BF16),...  120 us

profile of v9, /device:TPU:6, one launch (start us, length us, event | category | flops | bytes accessed | tf_op | source)
XLA Modules:
  0.0 121.8 jit_solution(14610018804053827922)
XLA Ops:
  0.6 119.6 %shard_map.131 = bf16[2,16,2048]{2,1,0:T(8,128)(2,1)} custom-call(bf16[16,2048]{1,0:T(8,128)(2,1)} %bitcast.7, bf16[384,2048]{1,0:T(8,128)(2,1)} %bitcast.4, bf16[384,2048]{1,0:T(8,128)(2,1)} %bitcast.5, bf16[3,64,256]{2,1,0:T(8,128)(2,1)} %bitcast.6, bf16[64,256]{1,0:T(8,128)(2,1)} %wo.1, bf16[2,256,256]{2,1,0:T(8,128)(2,1)} %wgu.1, bf16[256,256]{1,0:T(8,128)(2,1)} %wd.1, ...), custom_call_target="tpu_custom_call" | custom-call | tf_op jit(solution)/shard_map/pallas_call | solution.py:813
  120.3 1.5 %fusion = (bf16[1,16,2048]{2,1,0:T(8,128)(2,1)}, bf16[1,16,2048]{2,1,0:T(8,128)(2,1)}) fusion(bf16[2,16,2048]{2,1,0:T(8,128)(2,1)} %shard_map.131), kind=kLoop, calls=%fused_computation | loop fusion | bytes 262144 | tf_op jit(solution)/shard_map/slice | solution.py:882
